TPU v7x, 32 devices: a whole 2x2x4 slice. The times are simulated.
32 devices in a mesh: dp: 8 (over y, x, core), ctx: 4 (over z).
Axes of the slice: x: 2, y: 2, z: 4, core: 2. Of those that a mesh axis runs over, the one named last changes fastest.
Arguments:
- enc_in: bfloat16 [16, 1024, 768], P('dp', 'ctx'), may hold values from -6 to 6
- segments: int32 [16, 1024], P('dp'), may hold values from 0 to 3, never falling along the last dimension, each value on 1 to 682 neighbouring positions
- dec_in: bfloat16 [16, 1024, 768], P('dp', 'ctx'), may hold values from -6 to 6
- retrieved: int32 [16, 8, 512], P('dp'), may hold values from 0 to 1023, as said below
- enc_cot: bfloat16 [16, 1024, 768], P('dp', 'ctx'), may hold values from -6 to 6
- dec_cot: bfloat16 [16, 1024, 768], P('dp', 'ctx'), may hold values from -6 to 6
- enc_qkv: bfloat16 [768, 2304], P(('dp', 'ctx')), may hold values from -0.3125 to 0.3125
- enc_out: bfloat16 [768, 768], P(('dp', 'ctx')), may hold values from -1.75 to 1.75
- enc_up: bfloat16 [768, 3072], P(('dp', 'ctx')), may hold values from -0.21875 to 0.21875
- enc_down: bfloat16 [3072, 768], P(('dp', 'ctx')), may hold values from -0.109375 to 0.109375
- enc_bias: bfloat16 [768, 6], P(('dp', 'ctx')), may hold values from -1.25 to 1.25
- enc_up_bias: bfloat16 [3072], P(('dp', 'ctx')), may hold values from -1.25 to 1.25
- enc_gain: bfloat16 [768, 2], P(('dp', 'ctx')), may hold values from 0.5 to 1.5
- decoder_self_projections: bfloat16 [768, 2304], P(('dp', 'ctx')), may hold values from -0.3125 to 0.3125
- dec_out: bfloat16 [768, 768], P(('dp', 'ctx')), may hold values from -1.75 to 1.75
- cross_q: bfloat16 [768, 768], P(('dp', 'ctx')), may hold values from -0.3125 to 0.3125
- cross_kv: bfloat16 [768, 1536], P(('dp', 'ctx')), may hold values from -0.3125 to 0.3125
- cross_out: bfloat16 [768, 768], P(('dp', 'ctx')), may hold values from -1.75 to 1.75
- dec_up: bfloat16 [768, 3072], P(('dp', 'ctx')), may hold values from -0.21875 to 0.21875
- dec_down: bfloat16 [3072, 768], P(('dp', 'ctx')), may hold values from -0.109375 to 0.109375
- dec_bias: bfloat16 [768, 10], P(('dp', 'ctx')), may hold values from -1.25 to 1.25
- dec_up_bias: bfloat16 [3072], P(('dp', 'ctx')), may hold values from -1.25 to 1.25
- dec_gain: bfloat16 [768, 3], P(('dp', 'ctx')), may hold values from 0.5 to 1.5
Outputs:
- enc_hidden: bfloat16 [16, 1024, 768], P('dp', 'ctx')
- dec_hidden: bfloat16 [16, 1024, 768], P('dp', 'ctx')
- enc_in_grad: float32 [16, 1024, 768], P('dp', 'ctx')
- dec_in_grad: float32 [16, 1024, 768], P('dp', 'ctx')
- enc_qkv_grad: float32 [768, 2304], P(('dp', 'ctx'))
- enc_out_grad: float32 [768, 768], P(('dp', 'ctx'))
- enc_up_grad: float32 [768, 3072], P(('dp', 'ctx'))
- enc_down_grad: float32 [3072, 768], P(('dp', 'ctx'))
- enc_bias_grad: float32 [768, 6], P(('dp', 'ctx'))
- enc_up_bias_grad: float32 [3072], P(('dp', 'ctx'))
- enc_gain_grad: float32 [768, 2], P(('dp', 'ctx'))
- dec_qkv_grad: float32 [768, 2304], P(('dp', 'ctx'))
- dec_out_grad: float32 [768, 768], P(('dp', 'ctx'))
- cross_q_grad: float32 [768, 768], P(('dp', 'ctx'))
- mixed_pair_slope: float32 [768, 1536], P(('dp', 'ctx'))
- cross_out_grad: float32 [768, 768], P(('dp', 'ctx'))
- dec_up_grad: float32 [768, 3072], P(('dp', 'ctx'))
- dec_down_grad: float32 [3072, 768], P(('dp', 'ctx'))
- dec_bias_grad: float32 [768, 10], P(('dp', 'ctx'))
- dec_up_bias_grad: float32 [3072], P(('dp', 'ctx'))
- dec_gain_grad: float32 [768, 3], P(('dp', 'ctx'))
Inputs may be any that keep to these rules, and one draw needn't show every extreme that they name: `segments`: segment numbers never fall along a sequence; a document holds at most 682 tokens. `retrieved`: the 512 positions of one decoder block are distinct encoder positions of its own sequence.
All inputs are finite; a program needn't handle non-finite values.
Results may differ from a plain program's by a relative error of at most 0.03.
Values may be sent and summed in bfloat16 or wider, within the bound.
A program may use at most 384 MiB of HBM per device.

v0:
```python
import jax
import jax.numpy as jnp
from jax import lax
from jax.sharding import PartitionSpec as P

D = 768
HEADS = 12
HEAD_DIM = 64
BLOCK = 128


EPS = 1e-05
NEG = -1e30
FLOAT = jnp.float32
BRAIN = jnp.bfloat16


def matmul(left_side, right_side):
    return jnp.dot(left_side, right_side, preferred_element_type=FLOAT)


def matmul_left(left_side, right_side):
    return lax.dot_general(
        left_side, right_side, (((0,), (0,)), ((), ())), preferred_element_type=FLOAT
    )


def matmul_right(left_side, right_side):
    return lax.dot_general(
        left_side, right_side, (((1,), (1,)), ((), ())), preferred_element_type=FLOAT
    )


def column_sum(values):
    return jnp.sum(values, axis=0, dtype=FLOAT)


def layer_norm(hidden, gain_row, shift_row):
    center = hidden - jnp.mean(hidden, axis=-1, keepdims=True)
    spread = jnp.mean(center * center, axis=-1, keepdims=True)
    return center * lax.rsqrt(spread + EPS) * gain_row + shift_row


def gelu_exact(values):
    return jax.nn.gelu(values, approximate=False)


def split_pairs(pairs):
    pair_shape = pairs.shape
    both_parts = pairs.reshape(pair_shape[0], pair_shape[1], 2, HEADS, HEAD_DIM)
    return (both_parts[:, :, 0], both_parts[:, :, 1])


def head_scores(query_heads, key_heads, allowed):
    scores = jnp.einsum(
        "brhd,bkhd->bhrk", query_heads, key_heads, preferred_element_type=FLOAT
    ) * HEAD_DIM ** (-0.5)
    if allowed is not None:
        scores = jnp.where(allowed[:, None], scores, NEG)
    return scores


def attend_forward(queries, pairs, allowed):
    query_heads = queries.reshape(queries.shape[:2] + (HEADS, HEAD_DIM))
    key_heads, value_heads = split_pairs(pairs)
    scores = head_scores(query_heads, key_heads, allowed)
    row_max = jnp.max(scores, axis=-1, keepdims=True)
    log_total = row_max + jnp.log(jnp.sum(jnp.exp(scores - row_max), axis=-1, keepdims=True))
    attn_probs = jnp.exp(scores - log_total).astype(BRAIN)
    output = jnp.einsum("bhrk,bkhd->brhd", attn_probs, value_heads, preferred_element_type=FLOAT)
    return (output.reshape(queries.shape).astype(BRAIN), log_total)


def attend_backward(queries, pairs, allowed, log_total, grad_output):
    query_heads = queries.reshape(queries.shape[:2] + (HEADS, HEAD_DIM))
    key_heads, value_heads = split_pairs(pairs)
    grad_heads = grad_output.reshape(query_heads.shape)
    attn_probs = jnp.exp(head_scores(query_heads, key_heads, allowed) - log_total)
    grad_probs = jnp.einsum(
        "brhd,bkhd->bhrk", grad_heads, value_heads, preferred_element_type=FLOAT
    )
    inner_sum = jnp.sum(attn_probs * grad_probs, axis=-1, keepdims=True)
    grad_scores = (attn_probs * (grad_probs - inner_sum)).astype(BRAIN)
    score_scale = HEAD_DIM ** (-0.5)
    grad_queries = (
        jnp.einsum("bhrk,bkhd->brhd", grad_scores, key_heads, preferred_element_type=FLOAT)
        * score_scale
    )
    grad_keys = (
        jnp.einsum("bhrk,brhd->bkhd", grad_scores, query_heads, preferred_element_type=FLOAT)
        * score_scale
    )
    grad_values = jnp.einsum(
        "bhrk,brhd->bkhd", attn_probs.astype(BRAIN), grad_heads, preferred_element_type=FLOAT
    )
    batch_count, key_count = (pairs.shape[0], pairs.shape[1])
    grad_pairs = jnp.concatenate(
        [
            grad_keys.reshape(batch_count, key_count, D),
            grad_values.reshape(batch_count, key_count, D),
        ],
        axis=-1,
    )
    return (grad_queries.reshape(queries.shape), grad_pairs)


def project_forward(attended, residual, out_w, out_bias, gain_row, shift_row):
    summed = residual + matmul(attended, out_w) + out_bias
    return (layer_norm(summed, gain_row, shift_row), summed)


def project_backward(grad_norm, attended, summed, out_w, gain_row, shift_row):
    normed, pull_back = jax.vjp(layer_norm, summed, gain_row, shift_row)
    grad_summed, grad_gain, grad_shift = pull_back(grad_norm)
    grad_branch = grad_summed.astype(BRAIN)
    grad_out_w = matmul_left(attended, grad_branch)
    grad_out_bias = column_sum(grad_branch)
    grad_attended = matmul_right(grad_branch, out_w).astype(BRAIN)
    return (grad_summed, grad_attended, (grad_out_w, grad_out_bias, grad_gain, grad_shift))


def ffn_forward(first_norm, up_w, up_bias, down_w, down_bias, gain_row, shift_row):
    first_bf = first_norm.astype(BRAIN)
    lifted = matmul(first_bf, up_w) + up_bias
    activated = gelu_exact(lifted).astype(BRAIN)
    summed = first_norm + matmul(activated, down_w) + down_bias
    return (layer_norm(summed, gain_row, shift_row), (first_bf, lifted, activated, summed))


def ffn_backward(grad_norm, retained_context, up_w, down_w, gain_row, shift_row):
    first_bf, lifted, activated, summed = retained_context
    normed, pull_back = jax.vjp(layer_norm, summed, gain_row, shift_row)
    grad_summed, grad_gain, grad_shift = pull_back(grad_norm)
    grad_branch = grad_summed.astype(BRAIN)
    grad_down_w = matmul_left(activated, grad_branch)
    grad_down_bias = column_sum(grad_branch)
    grad_act = matmul_right(grad_branch, down_w)
    lifted_out, pull_gelu = jax.vjp(gelu_exact, lifted)
    grad_lifted = pull_gelu(grad_act)[0].astype(BRAIN)
    grad_up_w = matmul_left(first_bf, grad_lifted)
    up_bias_gradient = column_sum(grad_lifted)
    grad_first = grad_summed + matmul_right(grad_lifted, up_w)
    return (
        grad_first,
        (grad_up_w, up_bias_gradient, grad_down_w, grad_down_bias, grad_gain, grad_shift),
    )


def encoder_forward(weights, tokens, seg_rows, ctx_rank):
    qkv_w, out_w, up_w, down_w, bias_cols, up_bias, gain_cols = weights
    bias_vals = bias_cols.astype(FLOAT).T
    gain_vals = gain_cols.astype(FLOAT).T
    batch_count, row_count = (tokens.shape[0], tokens.shape[1])
    flat_tokens = tokens.reshape(batch_count * row_count, D)
    zero_row = jnp.zeros((D,), FLOAT)
    projected = (
        matmul(flat_tokens, qkv_w) + jnp.concatenate([bias_vals[0], zero_row, bias_vals[1]])
    ).astype(BRAIN)
    projected = projected.reshape(batch_count, row_count, 3 * D)
    all_pairs = lax.all_gather(projected[:, :, D:], "ctx", axis=1, tiled=True)
    own_segs = lax.dynamic_slice_in_dim(seg_rows, ctx_rank * row_count, row_count, axis=1)
    allowed = own_segs[:, :, None] == seg_rows[:, None, :]
    attended, log_total = attend_forward(projected[:, :, :D], all_pairs, allowed)
    attended = attended.reshape(batch_count * row_count, D)
    first_norm, first_sum = project_forward(
        attended, flat_tokens.astype(FLOAT), out_w, bias_vals[2], gain_vals[0], bias_vals[4]
    )
    final_norm, ffn_state = ffn_forward(
        first_norm, up_w, up_bias.astype(FLOAT), down_w, bias_vals[3], gain_vals[1], bias_vals[5]
    )
    return (
        final_norm,
        (flat_tokens, projected, all_pairs, allowed, log_total, attended, first_sum, ffn_state),
    )


def encoder_backward(weights, retained_context, grad_final):
    qkv_w, out_w, up_w, down_w, bias_cols, up_bias, gain_cols = weights
    bias_vals = bias_cols.astype(FLOAT).T
    gain_vals = gain_cols.astype(FLOAT).T
    flat_tokens, projected, all_pairs, allowed, log_total, attended, first_sum, ffn_state = (
        retained_context
    )
    batch_count, row_count = (projected.shape[0], projected.shape[1])
    grad_first, ffn_grads = ffn_backward(
        grad_final, ffn_state, up_w, down_w, gain_vals[1], bias_vals[5]
    )
    grad_tokens, grad_attended, proj_grads = project_backward(
        grad_first, attended, first_sum, out_w, gain_vals[0], bias_vals[4]
    )
    grad_queries, grad_pairs = attend_backward(
        projected[:, :, :D],
        all_pairs,
        allowed,
        log_total,
        grad_attended.reshape(batch_count, row_count, D),
    )
    own_pairs = lax.psum_scatter(
        grad_pairs.astype(jnp.bfloat16), "ctx", scatter_dimension=1, tiled=True
    ).astype(jnp.float32)
    mapped_slope = (
        jnp.concatenate([grad_queries, own_pairs], axis=-1)
        .astype(BRAIN)
        .reshape(batch_count * row_count, 3 * D)
    )
    grad_tokens = grad_tokens + matmul_right(mapped_slope, qkv_w)
    grad_qkv_w = matmul_left(flat_tokens, mapped_slope)
    proj_bias = column_sum(mapped_slope)
    up_grad_w, up_grad_bias, down_grad_w, down_grad_bias, gain_two, shift_two = ffn_grads
    out_grad_w, out_grad_bias, gain_one, shift_one = proj_grads
    bias_grads = jnp.stack(
        [proj_bias[:D], proj_bias[2 * D :], out_grad_bias, down_grad_bias, shift_one, shift_two],
        axis=1,
    )
    gain_grads = jnp.stack([gain_one, gain_two], axis=1)
    return (
        grad_tokens,
        (grad_qkv_w, out_grad_w, up_grad_w, down_grad_w, bias_grads, up_grad_bias, gain_grads),
    )


def decoder_forward(weights, tokens, memory_bf, pick_table, ctx_rank):
    (
        self_w,
        self_out_w,
        query_w,
        pair_w,
        cross_out_w,
        up_w,
        down_w,
        bias_cols,
        up_bias,
        gain_cols,
    ) = weights
    bias_vals = bias_cols.astype(FLOAT).T
    gain_vals = gain_cols.astype(FLOAT).T
    batch_count, row_count = (tokens.shape[0], tokens.shape[1])
    flat_tokens = tokens.reshape(batch_count * row_count, D)
    ctx_count = lax.axis_size("ctx")
    zero_row = jnp.zeros((D,), FLOAT)
    projected = (
        matmul(flat_tokens, self_w) + jnp.concatenate([bias_vals[0], zero_row, bias_vals[1]])
    ).astype(BRAIN)
    projected = projected.reshape(batch_count, row_count, 3 * D)
    all_pairs = lax.all_gather(projected[:, :, D:], "ctx", axis=1, tiled=True)
    query_pos = ctx_rank * row_count + jnp.arange(row_count, dtype=jnp.int32)
    key_pos = jnp.arange(row_count * ctx_count, dtype=jnp.int32)
    causal = (query_pos[:, None] >= key_pos[None, :])[None]
    attended, self_total = attend_forward(projected[:, :, :D], all_pairs, causal)
    attended = attended.reshape(batch_count * row_count, D)
    first_norm, first_sum = project_forward(
        attended, flat_tokens.astype(FLOAT), self_out_w, bias_vals[2], gain_vals[0], bias_vals[7]
    )
    first_bf = first_norm.astype(BRAIN)
    cross_queries = (matmul(first_bf, query_w) + bias_vals[3]).astype(BRAIN)
    memory_pairs = (matmul(memory_bf, pair_w) + jnp.concatenate([zero_row, bias_vals[4]])).astype(
        BRAIN
    )
    memory_rows = memory_pairs.shape[0] // batch_count
    memory_all = lax.all_gather(
        memory_pairs.reshape(batch_count, memory_rows, 2 * D), "ctx", axis=1, tiled=True
    )
    source_count = memory_all.shape[1]
    group_rows = min(row_count, BLOCK)
    group_count = row_count // group_rows
    group_start = ctx_rank * row_count + jnp.arange(group_count, dtype=jnp.int32) * group_rows
    pick_rows = jnp.take(pick_table, group_start // BLOCK, axis=1)
    pick_flat = (
        pick_rows + jnp.arange(batch_count, dtype=jnp.int32)[:, None, None] * source_count
    ).reshape(-1)
    picked = jnp.take(
        memory_all.reshape(batch_count * source_count, 2 * D), pick_flat, axis=0
    ).reshape(batch_count * group_count, pick_rows.shape[2], 2 * D)
    grouped = cross_queries.reshape(batch_count * group_count, group_rows, D)
    crossed, cross_total = attend_forward(grouped, picked, None)
    crossed = crossed.reshape(batch_count * row_count, D)
    second, second_sum = project_forward(
        crossed, first_norm, cross_out_w, bias_vals[5], gain_vals[1], bias_vals[8]
    )
    final_norm, ffn_state = ffn_forward(
        second, up_w, up_bias.astype(FLOAT), down_w, bias_vals[6], gain_vals[2], bias_vals[9]
    )
    retained_context = (
        flat_tokens,
        projected,
        all_pairs,
        causal,
        self_total,
        attended,
        first_sum,
        first_bf,
        grouped,
        pick_flat,
        picked,
        cross_total,
        crossed,
        second_sum,
        ffn_state,
        source_count,
    )
    return (final_norm, retained_context)


def decoder_backward(weights, memory_bf, retained_context, grad_final):
    (
        self_w,
        self_out_w,
        query_w,
        pair_w,
        cross_out_w,
        up_w,
        down_w,
        bias_cols,
        up_bias,
        gain_cols,
    ) = weights
    bias_vals = bias_cols.astype(FLOAT).T
    gain_vals = gain_cols.astype(FLOAT).T
    (
        flat_tokens,
        projected,
        all_pairs,
        causal,
        self_total,
        attended,
        first_sum,
        first_bf,
        grouped,
        pick_flat,
        picked,
        cross_total,
        crossed,
        second_sum,
        ffn_state,
        source_count,
    ) = retained_context
    batch_count, row_count = (projected.shape[0], projected.shape[1])
    grad_second, ffn_grads = ffn_backward(
        grad_final, ffn_state, up_w, down_w, gain_vals[2], bias_vals[9]
    )
    grad_first, grad_crossed, cross_grads = project_backward(
        grad_second, crossed, second_sum, cross_out_w, gain_vals[1], bias_vals[8]
    )
    grad_grouped, grad_picked = attend_backward(
        grouped, picked, None, cross_total, grad_crossed.reshape(grouped.shape)
    )
    grad_memory = (
        jnp.zeros((batch_count * source_count, 2 * D), FLOAT)
        .at[pick_flat]
        .add(grad_picked.reshape(-1, 2 * D))
    )
    own_memory = (
        lax.psum_scatter(
            grad_memory.reshape(batch_count, source_count, 2 * D).astype(jnp.bfloat16),
            "ctx",
            scatter_dimension=1,
            tiled=True,
        )
        .astype(jnp.float32)
        .astype(BRAIN)
    )
    own_memory = own_memory.reshape(-1, 2 * D)
    grad_memory_in = matmul_right(own_memory, pair_w)
    grad_pair_w = matmul_left(memory_bf, own_memory)
    pair_bias = column_sum(own_memory[:, D:])
    grad_cross_q = grad_grouped.reshape(batch_count * row_count, D).astype(BRAIN)
    grad_query_w = matmul_left(first_bf, grad_cross_q)
    query_bias = column_sum(grad_cross_q)
    grad_first = grad_first + matmul_right(grad_cross_q, query_w)
    grad_tokens, grad_attended, self_grads = project_backward(
        grad_first, attended, first_sum, self_out_w, gain_vals[0], bias_vals[7]
    )
    grad_queries, grad_pairs = attend_backward(
        projected[:, :, :D],
        all_pairs,
        causal,
        self_total,
        grad_attended.reshape(batch_count, row_count, D),
    )
    own_pairs = lax.psum_scatter(
        grad_pairs.astype(jnp.bfloat16), "ctx", scatter_dimension=1, tiled=True
    ).astype(jnp.float32)
    mapped_slope = (
        jnp.concatenate([grad_queries, own_pairs], axis=-1)
        .astype(BRAIN)
        .reshape(batch_count * row_count, 3 * D)
    )
    grad_tokens = grad_tokens + matmul_right(mapped_slope, self_w)
    grad_self_w = matmul_left(flat_tokens, mapped_slope)
    self_bias = column_sum(mapped_slope)
    up_grad_w, up_grad_bias, down_grad_w, down_grad_bias, gain_three, shift_three = ffn_grads
    cross_out_grad_w, cross_out_bias, gain_two, shift_two = cross_grads
    self_out_grad_w, self_out_bias, gain_one, shift_one = self_grads
    bias_grads = jnp.stack(
        [
            self_bias[:D],
            self_bias[2 * D :],
            self_out_bias,
            query_bias,
            pair_bias,
            cross_out_bias,
            down_grad_bias,
            shift_one,
            shift_two,
            shift_three,
        ],
        axis=1,
    )
    gain_grads = jnp.stack([gain_one, gain_two, gain_three], axis=1)
    weight_grads = (
        grad_self_w,
        self_out_grad_w,
        grad_query_w,
        grad_pair_w,
        cross_out_grad_w,
        up_grad_w,
        down_grad_w,
        bias_grads,
        up_grad_bias,
        gain_grads,
    )
    return (grad_tokens, grad_memory_in, weight_grads)


def fetch_weights(shards):
    return (
        lax.all_gather(shards[0], ("dp", "ctx"), axis=0, tiled=True),
        lax.all_gather(shards[1], ("dp", "ctx"), axis=0, tiled=True),
        lax.all_gather(shards[2], ("dp", "ctx"), axis=0, tiled=True),
        lax.all_gather(shards[3], ("dp", "ctx"), axis=0, tiled=True),
        lax.all_gather(shards[4], ("dp", "ctx"), axis=0, tiled=True),
        lax.all_gather(shards[5], ("dp", "ctx"), axis=0, tiled=True),
        lax.all_gather(shards[6], ("dp", "ctx"), axis=0, tiled=True),
        lax.all_gather(shards[7], ("dp", "ctx"), axis=0, tiled=True),
        lax.all_gather(shards[8], ("dp", "ctx"), axis=0, tiled=True),
        lax.all_gather(shards[9], ("dp", "ctx"), axis=0, tiled=True),
        lax.all_gather(shards[10], ("dp", "ctx"), axis=0, tiled=True),
        lax.all_gather(shards[11], ("dp", "ctx"), axis=0, tiled=True),
        lax.all_gather(shards[12], ("dp", "ctx"), axis=0, tiled=True),
        lax.all_gather(shards[13], ("dp", "ctx"), axis=0, tiled=True),
        lax.all_gather(shards[14], ("dp", "ctx"), axis=0, tiled=True),
        lax.all_gather(shards[15], ("dp", "ctx"), axis=0, tiled=True),
        lax.all_gather(shards[16], ("dp", "ctx"), axis=0, tiled=True),
    )


def body(
    enc_in,
    segments,
    dec_in,
    retrieved,
    enc_cot,
    dec_cot,
    enc_qkv,
    enc_out,
    enc_up,
    enc_down,
    enc_bias,
    enc_up_bias,
    enc_gain,
    decoder_self_projections,
    dec_out,
    cross_q,
    cross_kv,
    cross_out,
    dec_up,
    dec_down,
    dec_bias,
    dec_up_bias,
    dec_gain,
):
    shards = (
        enc_qkv,
        enc_out,
        enc_up,
        enc_down,
        enc_bias,
        enc_up_bias,
        enc_gain,
        decoder_self_projections,
        dec_out,
        cross_q,
        cross_kv,
        cross_out,
        dec_up,
        dec_down,
        dec_bias,
        dec_up_bias,
        dec_gain,
    )
    ctx_rank = lax.axis_index("ctx")
    batch_count, enc_rows, dec_rows = (enc_in.shape[0], enc_in.shape[1], dec_in.shape[1])
    kept_weights = fetch_weights(shards)
    enc_final, enc_state = encoder_forward(kept_weights[:7], enc_in, segments, ctx_rank)
    memory_bf = enc_final.astype(BRAIN)
    dec_final, dec_state = decoder_forward(kept_weights[7:], dec_in, memory_bf, retrieved, ctx_rank)
    dec_grad_in, memory_grad, dec_weight_grads = decoder_backward(
        kept_weights[7:], memory_bf, dec_state, dec_cot.reshape(-1, D).astype(FLOAT)
    )
    enc_grad_in, enc_weight_grads = encoder_backward(
        kept_weights[:7], enc_state, enc_cot.reshape(-1, D).astype(FLOAT) + memory_grad
    )
    totals = enc_weight_grads + dec_weight_grads
    reduced = (
        lax.psum_scatter(totals[0], ("dp", "ctx"), scatter_dimension=0, tiled=True),
        lax.psum_scatter(totals[1], ("dp", "ctx"), scatter_dimension=0, tiled=True),
        lax.psum_scatter(totals[2], ("dp", "ctx"), scatter_dimension=0, tiled=True),
        lax.psum_scatter(totals[3], ("dp", "ctx"), scatter_dimension=0, tiled=True),
        lax.psum_scatter(totals[4], ("dp", "ctx"), scatter_dimension=0, tiled=True),
        lax.psum_scatter(totals[5], ("dp", "ctx"), scatter_dimension=0, tiled=True),
        lax.psum_scatter(totals[6], ("dp", "ctx"), scatter_dimension=0, tiled=True),
        lax.psum_scatter(totals[7], ("dp", "ctx"), scatter_dimension=0, tiled=True),
        lax.psum_scatter(totals[8], ("dp", "ctx"), scatter_dimension=0, tiled=True),
        lax.psum_scatter(totals[9], ("dp", "ctx"), scatter_dimension=0, tiled=True),
        lax.psum_scatter(totals[10], ("dp", "ctx"), scatter_dimension=0, tiled=True),
        lax.psum_scatter(totals[11], ("dp", "ctx"), scatter_dimension=0, tiled=True),
        lax.psum_scatter(totals[12], ("dp", "ctx"), scatter_dimension=0, tiled=True),
        lax.psum_scatter(totals[13], ("dp", "ctx"), scatter_dimension=0, tiled=True),
        lax.psum_scatter(totals[14], ("dp", "ctx"), scatter_dimension=0, tiled=True),
        lax.psum_scatter(totals[15], ("dp", "ctx"), scatter_dimension=0, tiled=True),
        lax.psum_scatter(totals[16], ("dp", "ctx"), scatter_dimension=0, tiled=True),
    )
    return (
        memory_bf.reshape(batch_count, enc_rows, D),
        dec_final.astype(BRAIN).reshape(batch_count, dec_rows, D),
        enc_grad_in.reshape(batch_count, enc_rows, D),
        dec_grad_in.reshape(batch_count, dec_rows, D),
        reduced[0],
        reduced[1],
        reduced[2],
        reduced[3],
        reduced[4],
        reduced[5],
        reduced[6],
        reduced[7],
        reduced[8],
        reduced[9],
        reduced[10],
        reduced[11],
        reduced[12],
        reduced[13],
        reduced[14],
        reduced[15],
        reduced[16],
    )


def solution(mesh):
    in_specs = (
        P("dp", "ctx", None),
        P("dp", None),
        P("dp", "ctx", None),
        P("dp", None, None),
        P("dp", "ctx", None),
        P("dp", "ctx", None),
        P(("dp", "ctx"), None),
        P(("dp", "ctx"), None),
        P(("dp", "ctx"), None),
        P(("dp", "ctx"), None),
        P(("dp", "ctx"), None),
        P(("dp", "ctx")),
        P(("dp", "ctx"), None),
        P(("dp", "ctx"), None),
        P(("dp", "ctx"), None),
        P(("dp", "ctx"), None),
        P(("dp", "ctx"), None),
        P(("dp", "ctx"), None),
        P(("dp", "ctx"), None),
        P(("dp", "ctx"), None),
        P(("dp", "ctx"), None),
        P(("dp", "ctx")),
        P(("dp", "ctx"), None),
    )
    out_specs = (
        P("dp", "ctx", None),
        P("dp", "ctx", None),
        P("dp", "ctx", None),
        P("dp", "ctx", None),
        P(("dp", "ctx"), None),
        P(("dp", "ctx"), None),
        P(("dp", "ctx"), None),
        P(("dp", "ctx"), None),
        P(("dp", "ctx"), None),
        P(("dp", "ctx")),
        P(("dp", "ctx"), None),
        P(("dp", "ctx"), None),
        P(("dp", "ctx"), None),
        P(("dp", "ctx"), None),
        P(("dp", "ctx"), None),
        P(("dp", "ctx"), None),
        P(("dp", "ctx"), None),
        P(("dp", "ctx"), None),
        P(("dp", "ctx"), None),
        P(("dp", "ctx")),
        P(("dp", "ctx"), None),
    )
    return jax.shard_map(body, mesh=mesh, in_specs=in_specs, out_specs=out_specs, check_vma=False)
```

profile of v0, /device:TPU:0, one launch (start us, length us, event | category | flops | bytes accessed | tf_op | source)
XLA Modules:
  0.0 3071.5 jit_solution(9131268328243848427)
XLA Ops:
  8.7 70.1 %all-gather.3 = bf16[32,24,3]{1,2,0:T(4,128)(2,1)S(1)} all-gather(bf16[1,24,3]{1,2,0:T(4,128)(2,1)} %bitcast.358), channel_id=1, replica_groups=mesh['dp'=8,'ctx'=4] {'dp','ctx'}, dimensions={0}, use_global_device_ids=true | all-gather | bytes 4752 | tf_op jit(solution)/shard_map/all_gather | solution.py:443
  79.1 64.5 %all-gather = bf16[32,24,6]{1,2,0:T(8,128)(2,1)S(1)} all-gather(bf16[1,24,6]{1,2,0:T(8,128)(2,1)} %bitcast.357), channel_id=1, replica_groups=mesh['dp'=8,'ctx'=4] {'dp','ctx'}, dimensions={0}, use_global_device_ids=true | all-gather | bytes 9504 | tf_op jit(solution)/shard_map/all_gather | solution.py:431
  143.9 66.8 %all-gather.2 = bf16[32,24,10]{1,2,0:T(8,128)(2,1)S(1)} all-gather(bf16[1,24,10]{1,2,0:T(8,128)(2,1)} %bitcast.356), channel_id=1, replica_groups=mesh['dp'=8,'ctx'=4] {'dp','ctx'}, dimensions={0}, use_global_device_ids=true | all-gather | bytes 15840 | tf_op jit(solution)/shard_map/all_gather | solution.py:441
  231.4 60.7 %all-reduce.10 = (bf16[3072]{0:T(1024)(128)(2,1)S(1)}, bf16[3072]{0:T(1024)(128)(2,1)S(1)}) all-reduce(bf16[3072]{0:T(1024)(128)(2,1)S(1)} %dynamic-update-slice, bf16[3072]{0:T(1024)(128)(2,1)S(1)} %dynamic-update-slice.1), channel_id=1, replica_groups=mesh['dp'=8,'ctx'=4] {'dp','ctx'}, use_global_device_ids=true, to_apply=%add.1 | all-reduce | flops 6144 | bytes 24576
  292.1 80.8 %all-gather.1 = bf16[32,24,2]{1,2,0:T(2,128)(2,1)S(1)} all-gather(bf16[1,24,2]{1,2,0:T(2,128)(2,1)S(1)} %bitcast.359), channel_id=1, replica_groups=mesh['dp'=8,'ctx'=4] {'dp','ctx'}, dimensions={0}, use_global_device_ids=true | all-gather | bytes 3168 | tf_op jit(solution)/shard_map/all_gather | solution.py:433
  417.2 34.8 %all-gather.25.cloned.1.call-done = bf16[768,3072]{1,0:T(8,128)(2,1)} async-done(((bf16[24,3072]{1,0:T(8,128)(2,1)}), bf16[768,3072]{1,0:T(8,128)(2,1)}) %all-gather.25.cloned.1.call-update) | async-done | bytes 4718608 | tf_op jit(solution)/shard_map/all_gather | solution.py:429
  452.0 19.8 multiply_convert_fusion.6
  471.9 45.2 %all-gather.27.cloned.1.call-done = bf16[3072,768]{1,0:T(8,128)(2,1)} async-done(((bf16[96,768]{1,0:T(8,128)(2,1)}), bf16[3072,768]{1,0:T(8,128)(2,1)}) %all-gather.27.cloned.1.call-update) | async-done | bytes 4718608 | tf_op jit(solution)/shard_map/all_gather | solution.py:430
  524.6 51.4 %all-gather.35.cloned.1.call-done = bf16[768,1536]{1,0:T(8,128)(2,1)} async-done(((bf16[24,1536]{1,0:T(8,128)(2,1)}), bf16[768,1536]{1,0:T(8,128)(2,1)}) %all-gather.35.cloned.1.call-update) | async-done | bytes 2359312 | tf_op jit(solution)/shard_map/all_gather | solution.py:437
  585.3 106.7 %all-gather.31.cloned.1.call-done = bf16[2,1024,1536]{1,2,0:T(8,128)(2,1)} async-done(((bf16[2,256,1536]{1,2,0:T(8,128)(2,1)}), bf16[2,1024,1536]{1,2,0:T(8,128)(2,1)}) %all-gather.31.cloned.1.call-update) | async-done | bytes 6291472 | tf_op jit(solution)/shard_map/all_gather | solution.py:245
  749.7 53.2 %all-gather.39.cloned.1.call-done = bf16[768,768]{1,0:T(8,128)(2,1)} async-done(((bf16[24,768]{1,0:T(8,128)(2,1)}), bf16[768,768]{1,0:T(8,128)(2,1)}) %all-gather.39.cloned.1.call-update) | async-done | bytes 1179664 | tf_op jit(solution)/shard_map/all_gather | solution.py:436
  807.5 111.8 %all-gather.37.cloned.1.call-done = bf16[2,1024,1536]{2,1,0:T(8,128)(2,1)} async-done(((bf16[2,256,1536]{2,1,0:T(8,128)(2,1)}), bf16[2,1024,1536]{2,1,0:T(8,128)(2,1)}) %all-gather.37.cloned.1.call-update) | async-done | bytes 6291472 | tf_op jit(solution)/shard_map/all_gather | solution.py:260
  981.8 57.9 %all-gather.43.cloned.1.call-done = bf16[768,3072]{1,0:T(8,128)(2,1)} async-done(((bf16[24,3072]{1,0:T(8,128)(2,1)}), bf16[768,3072]{1,0:T(8,128)(2,1)}) %all-gather.43.cloned.1.call-update) | async-done | bytes 4718608 | tf_op jit(solution)/shard_map/all_gather | solution.py:439
  1039.6 21.1 multiply_convert_fusion.5
  1060.7 44.0 %all-gather.45.cloned.1.call-done = bf16[3072,768]{1,0:T(8,128)(2,1)} async-done(((bf16[96,768]{1,0:T(8,128)(2,1)}), bf16[3072,768]{1,0:T(8,128)(2,1)}) %all-gather.45.cloned.1.call-update) | async-done | bytes 4718608 | tf_op jit(solution)/shard_map/all_gather | solution.py:440
  1215.3 26.9 scatter_custom_fusion
  1262.8 19.7 multiply_reduce_fusion
  1321.0 38.8 %reduce-scatter.23.cloned.1.call-done = bf16[2,256,1536]{2,1,0:T(8,128)(2,1)} async-done(((bf16[2,1024,1536]{2,1,0:T(8,128)(2,1)}), bf16[2,256,1536]{2,1,0:T(8,128)(2,1)}) %reduce-scatter.23.cloned.1.call-update) | async-done | bytes 1572880 | tf_op jit(solution)/shard_map/reduce_scatter | solution.py:353
  1381.9 19.2 multiply_reduce_fusion.1
  1477.4 109.4 %reduce-scatter.25.cloned.1.call-done = bf16[2,256,1536]{1,2,0:T(8,128)(2,1)} async-done(((bf16[2,1024,1536]{1,2,0:T(8,128)(2,1)}), bf16[2,256,1536]{1,2,0:T(8,128)(2,1)}) %reduce-scatter.25.cloned.1.call-update) | async-done | bytes 1572880 | tf_op jit(solution)/shard_map/reduce_scatter | solution.py:198
  1686.6 32.0 %all-reduce.13.cloned.1.call-done = (f32[768,6]{0,1:T(8,128)}, f32[3072]{0:T(1024)}, f32[768,2]{0,1:T(2,128)}, f32[768,10]{0,1:T(8,128)}, f32[3072]{0:T(1024)}, /*index=5*/f32[768,3]{0,1:T(4,128)}) async-done(((f32[768,6]{0,1:T(8,128)}, f32[3072]{0:T(1024)}, f32[768,2]{0,1:T(2,128)}, f32[768,10]{0,1:T(8,128)}, f32[3072]{0:T(1024)}, /*index=5*/f32[768,3]{0,1:T(4,128)}), (f32[768,6]{0,1:T(8,128)}, ...) | async-done | bytes 89104
  1726.4 96.9 %reduce-scatter.41.cloned.1.call-done = f32[24,768]{1,0:T(8,128)} async-done(((f32[768,768]{1,0:T(8,128)}), f32[24,768]{1,0:T(8,128)}) %reduce-scatter.41.cloned.1.call-update) | async-done | bytes 73744 | tf_op jit(solution)/shard_map/reduce_scatter | solution.py:516
  1823.3 104.6 %reduce-scatter.37.cloned.1.call-done = f32[24,768]{1,0:T(8,128)} async-done(((f32[768,768]{1,0:T(8,128)}), f32[24,768]{1,0:T(8,128)}) %reduce-scatter.37.cloned.1.call-update) | async-done | bytes 73744 | tf_op jit(solution)/shard_map/reduce_scatter | solution.py:514
  1927.9 103.9 %reduce-scatter.35.cloned.1.call-done = f32[24,768]{1,0:T(8,128)} async-done(((f32[768,768]{1,0:T(8,128)}), f32[24,768]{1,0:T(8,128)}) %reduce-scatter.35.cloned.1.call-update) | async-done | bytes 73744 | tf_op jit(solution)/shard_map/reduce_scatter | solution.py:513
  2031.8 142.2 %reduce-scatter.43.cloned.1.call-done = f32[24,3072]{1,0:T(8,128)} async-done(((f32[768,3072]{1,0:T(8,128)}), f32[24,3072]{1,0:T(8,128)}) %reduce-scatter.43.cloned.1.call-update) | async-done | bytes 294928 | tf_op jit(solution)/shard_map/reduce_scatter | solution.py:517
  2174.0 141.1 %reduce-scatter.45.cloned.1.call-done = f32[96,768]{1,0:T(8,128)} async-done(((f32[3072,768]{1,0:T(8,128)}), f32[96,768]{1,0:T(8,128)}) %reduce-scatter.45.cloned.1.call-update) | async-done | bytes 294928 | tf_op jit(solution)/shard_map/reduce_scatter | solution.py:518
  2315.0 104.5 %reduce-scatter.29.cloned.1.call-done = f32[24,768]{1,0:T(8,128)} async-done(((f32[768,768]{1,0:T(8,128)}), f32[24,768]{1,0:T(8,128)}) %reduce-scatter.29.cloned.1.call-update) | async-done | bytes 73744 | tf_op jit(solution)/shard_map/reduce_scatter | solution.py:506
  2419.6 112.1 %reduce-scatter.39.cloned.1.call-done = f32[24,1536]{1,0:T(8,128)} async-done(((f32[768,1536]{1,0:T(8,128)}), f32[24,1536]{1,0:T(8,128)}) %reduce-scatter.39.cloned.1.call-update) | async-done | bytes 147472 | tf_op jit(solution)/shard_map/reduce_scatter | solution.py:515
  2531.6 125.4 %reduce-scatter.49.cloned.1.call-done = f32[24,2304]{1,0:T(8,128)} async-done(((f32[768,2304]{1,0:T(8,128)}), f32[24,2304]{1,0:T(8,128)}) %reduce-scatter.49.cloned.1.call-update) | async-done | bytes 221200
  2657.0 141.1 %reduce-scatter.31.cloned.1.call-done = f32[24,3072]{1,0:T(8,128)} async-done(((f32[768,3072]{1,0:T(8,128)}), f32[24,3072]{1,0:T(8,128)}) %reduce-scatter.31.cloned.1.call-update) | async-done | bytes 294928 | tf_op jit(solution)/shard_map/reduce_scatter | solution.py:507
  2798.1 142.2 %reduce-scatter.33.cloned.1.call-done = f32[96,768]{1,0:T(8,128)} async-done(((f32[3072,768]{1,0:T(8,128)}), f32[96,768]{1,0:T(8,128)}) %reduce-scatter.33.cloned.1.call-update) | async-done | bytes 294928 | tf_op jit(solution)/shard_map/reduce_scatter | solution.py:508
  2940.3 124.4 %reduce-scatter.47.cloned.1.call-done = f32[24,2304]{1,0:T(8,128)} async-done(((f32[768,2304]{1,0:T(8,128)}), f32[24,2304]{1,0:T(8,128)}) %reduce-scatter.47.cloned.1.call-update) | async-done | bytes 221200
  (544 shorter events, 581.9 us)
Async XLA Ops:
  7.2 204.8 %all-gather.19.cloned.1.call-start = ((), (), s32[]{:S(2)}) async-start(), calls=%async_computation.14 | async-start | bytes 3649536 | tf_op jit(solution)/shard_map/all_gather | solution.py:427
  7.9 214.0 %all-gather.29.cloned.1.call-start = ((), (), s32[]{:S(2)}) async-start(), calls=%async_computation.19 | async-start | bytes 3649536 | tf_op jit(solution)/shard_map/all_gather | solution.py:434
  8.7 366.7 %all-gather.21.cloned.1.call-start = ((), (), s32[]{:S(2)}) async-start(), calls=%async_computation.15 | async-start | bytes 7864320 | tf_op jit(solution)/shard_map/all_gather | solution.py:160
  211.9 765.8 %copy-start.95 = (f32[768]{0:T(1024)}, f32[768]{0:T(1024)S(1)}, u32[]{:S(2)}) copy-start(f32[768]{0:T(1024)S(1)} %get-tuple-element.146) | copy-start | bytes 9220
  211.9 1046.7 %copy-start.78 = (f32[768]{0:T(1024)}, f32[768]{0:T(1024)S(1)}, u32[]{:S(2)}) copy-start(f32[768]{0:T(1024)S(1)} %get-tuple-element.234) | copy-start | bytes 9220
  219.4 194.1 %all-gather.23.cloned.1.call-start = ((), (), s32[]{:S(2)}) async-start(), calls=%async_computation.16 | async-start | bytes 1216512 | tf_op jit(solution)/shard_map/all_gather | solution.py:428
  219.9 232.1 %all-gather.25.cloned.1.call-start = ((), (), s32[]{:S(2)}) async-start(), calls=%async_computation.17 | async-start | bytes 4866048 | tf_op jit(solution)/shard_map/all_gather | solution.py:429
  220.5 296.6 %all-gather.27.cloned.1.call-start = ((), (), s32[]{:S(2)}) async-start(), calls=%async_computation.18 | async-start | bytes 4866048 | tf_op jit(solution)/shard_map/all_gather | solution.py:430
  221.1 355.0 %all-gather.35.cloned.1.call-start = ((), (), s32[]{:S(2)}) async-start(), calls=%async_computation.22 | async-start | bytes 2433024 | tf_op jit(solution)/shard_map/all_gather | solution.py:437
  221.8 470.2 %all-gather.31.cloned.1.call-start = ((), (), s32[]{:S(2)}) async-start(), calls=%async_computation.20 | async-start | bytes 7864320 | tf_op jit(solution)/shard_map/all_gather | solution.py:245
  229.5 517.6 %all-gather.33.cloned.1.call-start = ((), (), s32[]{:S(2)}) async-start(), calls=%async_computation.21 | async-start | bytes 1216512 | tf_op jit(solution)/shard_map/all_gather | solution.py:435
  230.2 572.6 %all-gather.39.cloned.1.call-start = ((), (), s32[]{:S(2)}) async-start(), calls=%async_computation.24 | async-start | bytes 1216512 | tf_op jit(solution)/shard_map/all_gather | solution.py:436
  230.8 688.5 %all-gather.37.cloned.1.call-start = ((), (), s32[]{:S(2)}) async-start(), calls=%async_computation.23 | async-start | bytes 7864320 | tf_op jit(solution)/shard_map/all_gather | solution.py:260
  580.3 397.4 %all-gather.41.cloned.1.call-start = ((), (), s32[]{:S(2)}) async-start(), calls=%async_computation.25 | async-start | bytes 1216512 | tf_op jit(solution)/shard_map/all_gather | solution.py:438
  580.9 458.7 %all-gather.43.cloned.1.call-start = ((), (), s32[]{:S(2)}) async-start(), calls=%async_computation.26 | async-start | bytes 4866048 | tf_op jit(solution)/shard_map/all_gather | solution.py:439
  581.6 523.0 %all-gather.45.cloned.1.call-start = ((), (), s32[]{:S(2)}) async-start(), calls=%async_computation.27 | async-start | bytes 4866048 | tf_op jit(solution)/shard_map/all_gather | solution.py:440
  582.2 777.6 %reduce-scatter.23.cloned.1.call-start = ((), (), s32[]{:S(2)}) async-start(), calls=%async_computation.28 | async-start | bytes 7864320 | tf_op jit(solution)/shard_map/reduce_scatter | solution.py:353
  1250.2 223.2 %reduce-scatter.27.cloned.1.call-start = ((), (), s32[]{:S(2)}) async-start(), calls=%async_computation.30 | async-start | bytes 7864320 | tf_op jit(solution)/shard_map/reduce_scatter | solution.py:380
  1321.0 265.8 %reduce-scatter.25.cloned.1.call-start = ((), (), s32[]{:S(2)}) async-start(), calls=%async_computation.29 | async-start | bytes 7864320 | tf_op jit(solution)/shard_map/reduce_scatter | solution.py:198
  1440.1 278.4 %all-reduce.13.cloned.1.call-start = ((), (), s32[]{:S(2)}) async-start(), calls=%async_computation.42 | async-start | bytes 233472
  1590.8 232.5 %reduce-scatter.41.cloned.1.call-start = ((), (), s32[]{:S(2)}) async-start(), calls=%async_computation.37 | async-start | bytes 2433024 | tf_op jit(solution)/shard_map/reduce_scatter | solution.py:516
  1594.4 333.4 %reduce-scatter.37.cloned.1.call-start = ((), (), s32[]{:S(2)}) async-start(), calls=%async_computation.35 | async-start | bytes 2433024 | tf_op jit(solution)/shard_map/reduce_scatter | solution.py:514
  1598.8 433.0 %reduce-scatter.35.cloned.1.call-start = ((), (), s32[]{:S(2)}) async-start(), calls=%async_computation.34 | async-start | bytes 2433024 | tf_op jit(solution)/shard_map/reduce_scatter | solution.py:513
  1602.5 571.5 %reduce-scatter.43.cloned.1.call-start = ((), (), s32[]{:S(2)}) async-start(), calls=%async_computation.38 | async-start | bytes 9732096 | tf_op jit(solution)/shard_map/reduce_scatter | solution.py:517
  1611.5 703.6 %reduce-scatter.45.cloned.1.call-start = ((), (), s32[]{:S(2)}) async-start(), calls=%async_computation.39 | async-start | bytes 9732096 | tf_op jit(solution)/shard_map/reduce_scatter | solution.py:518
  1619.9 799.6 %reduce-scatter.29.cloned.1.call-start = ((), (), s32[]{:S(2)}) async-start(), calls=%async_computation.31 | async-start | bytes 2433024 | tf_op jit(solution)/shard_map/reduce_scatter | solution.py:506
  1623.6 908.0 %reduce-scatter.39.cloned.1.call-start = ((), (), s32[]{:S(2)}) async-start(), calls=%async_computation.36 | async-start | bytes 4866048 | tf_op jit(solution)/shard_map/reduce_scatter | solution.py:515
  1628.9 1028.1 %reduce-scatter.49.cloned.1.call-start = ((), (), s32[]{:S(2)}) async-start(), calls=%async_computation.41 | async-start | bytes 7299072
  1643.8 1154.3 %reduce-scatter.31.cloned.1.call-start = ((), (), s32[]{:S(2)}) async-start(), calls=%async_computation.32 | async-start | bytes 9732096 | tf_op jit(solution)/shard_map/reduce_scatter | solution.py:507
  1653.4 1286.9 %reduce-scatter.33.cloned.1.call-start = ((), (), s32[]{:S(2)}) async-start(), calls=%async_computation.33 | async-start | bytes 9732096 | tf_op jit(solution)/shard_map/reduce_scatter | solution.py:508
  1661.9 1402.8 %reduce-scatter.47.cloned.1.call-start = ((), (), s32[]{:S(2)}) async-start(), calls=%async_computation.40 | async-start | bytes 7299072
  1683.4 1381.4 %copy-start.1 = (s32[2,8,512]{2,1,0:T(8,128)S(1)}, s32[2,8,512]{2,1,0:T(8,128)}, u32[]{:S(2)}) copy-start(s32[2,8,512]{2,1,0:T(8,128)} %param.26) | copy-start | bytes 98308
  (125 other events, 5553.3 us)
Sparse Core Ops, SparseCore 0:
  10.8 62.9 all-gather.18
  76.6 59.0 all-gather.28
  219.5 112.3 all-gather.20
  334.5 52.3 all-gather.22
  389.5 62.4 all-gather.24
  454.7 62.3 all-gather.26
  519.9 56.1 all-gather.34
  578.2 113.7 all-gather.30
  694.8 52.2 all-gather.32
  749.8 53.0 all-gather.38
  805.0 114.2 all-gather.36
  922.0 52.2 all-gather.40
  977.1 62.4 all-gather.42
  1042.3 62.3 all-gather.44
  1250.3 109.5 reduce-scatter.22
  1362.0 111.2 reduce-scatter.26
  1475.5 111.2 reduce-scatter.24
  1593.6 124.8 all-reduce.12
  1724.4 98.8 reduce-scatter.40
  1829.9 97.9 reduce-scatter.36
  1933.7 98.0 reduce-scatter.34
  2039.3 134.6 reduce-scatter.42
  2180.4 134.5 reduce-scatter.44
  2321.6 97.9 reduce-scatter.28
  2425.6 105.9 reduce-scatter.38
  2538.7 118.2 reduce-scatter.48
  2663.3 134.6 reduce-scatter.30
  2805.5 134.7 reduce-scatter.32
  2946.6 118.1 reduce-scatter.46
where the time goes:
time: 3080 us; the launch traced here: 3070 us
  waiting for transfers between devices  2050 us (67%)
  matrix products  358 us (12%)
  blocking collectives  343 us (11%)
  local copies, waits for them, and re-layouts  156 us (5%)
  other arithmetic  142 us (5%)
    unnamed x32, waiting for transfers between devices  289 us
    reduce_scatter x1, waiting for transfers between devices, body(): lax.psum_scatter(totals[3], ('dp', 'ctx'), scatter_dimension=0, tiled=True)  142 us
    reduce_scatter x1, waiting for transfers between devices, body(): lax.psum_scatter(totals[12], ('dp', 'ctx'), scatter_dimension=0, tiled=True)  142 us
    reduce_scatter x1, waiting for transfers between devices, body(): lax.psum_scatter(totals[13], ('dp', 'ctx'), scatter_dimension=0, tiled=True)  141 us
    reduce_scatter x1, waiting for transfers between devices, body(): lax.psum_scatter(totals[2], ('dp', 'ctx'), scatter_dimension=0, tiled=True)  141 us
    reduce_scatter x1, waiting for transfers between devices, body(): lax.psum_scatter(totals[10], ('dp', 'ctx'), scatter_dimension=0, tiled=True)  112 us
    all_gather x1, waiting for transfers between devices, decoder_forward(): lax.all_gather(memory_pairs.reshape(batch_count, memory_rows, 2 * D), 'ct...  112 us
    reduce_scatter x1, waiting for transfers between devices, encoder_backward(): lax.psum_scatter(grad_pairs.astype(jnp.bfloat16), 'ctx', scatter_dimensio...  109 us
  transfers between devices with their start and end apart: 29, of which 24 were waited for; matrix products, arithmetic and copies ran while one was open for 16% of the time, Pallas kernels for 0%

commit v1 on v0

--- a/solution.py
+++ b/solution.py
@@ -1,6 +1,10 @@
+import functools
+
 import jax
 import jax.numpy as jnp
 from jax import lax
+from jax.experimental import pallas as pl
+from jax.experimental.pallas import tpu as pltpu
 from jax.sharding import PartitionSpec as P
 
 D = 768
@@ -545,6 +549,468 @@
     )
 
 
+MESH_ID = pl.DeviceIdType.MESH
+LOG2E = 1.4426950408889634
+PAIR = 128
+ANY = pl.BlockSpec(memory_space=pl.ANY)
+DMA_SEM = pltpu.SemaphoreType.DMA
+
+
+def place():
+    dp = lax.axis_index("dp")
+    return dp, lax.axis_index("ctx"), lax.rem(dp, 2)
+
+
+def spread_kernel(token_count, zs, *refs):
+    tokens, ints = refs[:token_count], refs[token_count : token_count + 2]
+    outs, int_outs = refs[token_count + 2 : 2 * token_count + 2], refs[2 * token_count + 2 : 2 * token_count + 4]
+    send, recv, local, int_send, int_recv = refs[2 * token_count + 4 :]
+    dp, z, core = place()
+    pair = dp - core
+    barrier = pltpu.get_barrier_semaphore()
+    for step in range(zs):
+        for other in range(2):
+            if step or other:
+                pl.semaphore_signal(
+                    barrier, 1, device_id=(pair + lax.rem(core + other, 2), lax.rem(z + step, zs)), device_id_type=MESH_ID
+                )
+    pl.semaphore_wait(barrier, 2 * zs - 1)
+    sibling = (pair + 1 - core, z)
+    int_copies = []
+    for i in range(2):
+        copy = pltpu.make_async_remote_copy(
+            ints[i], int_outs[i], int_send.at[i], int_recv.at[i], device_id=sibling, device_id_type=MESH_ID
+        )
+        copy.start()
+        int_copies.append(copy)
+
+    def each(what):
+        for t in range(token_count):
+            for i in range(2):
+                for h in range(2):
+                    z_to, core_to = 2 * core + i, lax.rem(h + z, 2)
+                    source, target = tokens[t].at[i, pl.ds(h * BLOCK, BLOCK)], outs[t].at[z]
+                    stays = jnp.logical_and(z_to == z, core_to == core)
+
+                    @pl.when(stays)
+                    def _(source=source, target=target, t=t):
+                        what(pltpu.make_async_copy(source, target, local.at[t]), False)
+
+                    @pl.when(jnp.logical_not(stays))
+                    def _(source=source, target=target, t=t, i=i, h=h, z_to=z_to, core_to=core_to):
+                        what(
+                            pltpu.make_async_remote_copy(
+                                source,
+                                target,
+                                send.at[t, 2 * i + h],
+                                recv.at[t, z],
+                                device_id=(pair + core_to, z_to),
+                                device_id_type=MESH_ID,
+                            ),
+                            True,
+                        )
+
+    each(lambda copy, remote: copy.start())
+    each(lambda copy, remote: copy.wait_send() if remote else copy.wait())
+    for t in range(token_count):
+        for s in range(zs):
+            @pl.when(jnp.logical_not(jnp.logical_and(s == z, z // 2 == core)))
+            def _(t=t, s=s):
+                pltpu.make_async_remote_copy(
+                    outs[t].at[s], outs[t].at[s], send.at[t, 0], recv.at[t, s], device_id=sibling, device_id_type=MESH_ID
+                ).wait_recv()
+    for copy in int_copies:
+        copy.wait()
+
+
+def spread(tokens, ints, collective_id):
+    zs, count = lax.axis_size("ctx"), len(tokens)
+    shapes = [jax.ShapeDtypeStruct((zs, BLOCK, D), t.dtype) for t in tokens]
+    shapes += [jax.ShapeDtypeStruct(i.shape, i.dtype) for i in ints]
+    got = pl.pallas_call(
+        functools.partial(spread_kernel, count, zs),
+        out_shape=shapes,
+        in_specs=[ANY] * (count + 2),
+        out_specs=[ANY] * (count + 2),
+        scratch_shapes=[DMA_SEM((count, 4)), DMA_SEM((count, zs)), DMA_SEM((count,)), DMA_SEM((2,)), DMA_SEM((2,))],
+        compiler_params=pltpu.CompilerParams(collective_id=collective_id, has_side_effects=True),
+        name="spread_tokens",
+    )(*tokens, *ints)
+    return got[:count], got[count:]
+
+
+def collect_kernel(count, zs, *refs):
+    blocks, outs = refs[:count], refs[count : 2 * count]
+    send, recv, local = refs[2 * count :]
+    dp, z, core = place()
+    pair = dp - core
+    barrier = pltpu.get_barrier_semaphore()
+    for step in range(zs):
+        for other in range(2):
+            if step or other:
+                pl.semaphore_signal(
+                    barrier, 1, device_id=(pair + lax.rem(core + other, 2), lax.rem(z + step, zs)), device_id_type=MESH_ID
+                )
+    pl.semaphore_wait(barrier, 2 * zs - 1)
+    owner, place_in = z // 2, lax.rem(z, 2)
+
+    def each(what):
+        for t in range(count):
+            for s in range(zs):
+                half = lax.rem(core + s, 2)
+                source = blocks[t].at[s]
+                target = outs[t].at[place_in, pl.ds(half * BLOCK, BLOCK)]
+                stays = jnp.logical_and(s == z, owner == core)
+
+                @pl.when(stays)
+                def _(source=source, target=target, t=t):
+                    what(pltpu.make_async_copy(source, target, local.at[t]), False)
+
+                @pl.when(jnp.logical_not(stays))
+                def _(source=source, target=target, t=t, s=s, half=half):
+                    what(
+                        pltpu.make_async_remote_copy(
+                            source,
+                            target,
+                            send.at[t, s],
+                            recv.at[t, 2 * place_in + half],
+                            device_id=(pair + owner, s),
+                            device_id_type=MESH_ID,
+                        ),
+                        True,
+                    )
+
+    each(lambda copy, remote: copy.start())
+    each(lambda copy, remote: copy.wait_send() if remote else copy.wait())
+    for t in range(count):
+        for i in range(2):
+            for h in range(2):
+                z_from, core_from = 2 * core + i, lax.rem(h + z, 2)
+
+                @pl.when(jnp.logical_not(jnp.logical_and(z_from == z, core_from == core)))
+                def _(t=t, i=i, h=h):
+                    target = outs[t].at[i, pl.ds(h * BLOCK, BLOCK)]
+                    pltpu.make_async_remote_copy(
+                        target, target, send.at[t, 0], recv.at[t, 2 * i + h], device_id=(pair + 1 - core, z), device_id_type=MESH_ID
+                    ).wait_recv()
+
+
+def collect(blocks, collective_id):
+    zs, count = lax.axis_size("ctx"), len(blocks)
+    return pl.pallas_call(
+        functools.partial(collect_kernel, count, zs),
+        out_shape=[jax.ShapeDtypeStruct((2, 2 * BLOCK, D), b.dtype) for b in blocks],
+        in_specs=[ANY] * count,
+        out_specs=[ANY] * count,
+        scratch_shapes=[DMA_SEM((count, zs)), DMA_SEM((count, 4)), DMA_SEM((count,))],
+        compiler_params=pltpu.CompilerParams(collective_id=collective_id, has_side_effects=True),
+        name="collect_tokens",
+    )(*blocks)
+
+
+def key_chunks(rows, causal):
+    if causal:
+        return [(half, r, BLOCK, r) for r in range(0, rows, BLOCK) for half in range(2)]
+    return [(half, r, 2 * BLOCK, 0) for half in range(2) for r in range(0, rows, 2 * BLOCK)]
+
+
+def nt_dot(a, b):
+    return lax.dot_general(a, b, (((1,), (1,)), ((), ())), preferred_element_type=FLOAT)
+
+
+def head_lanes(values, head):
+    lanes = lax.broadcasted_iota(jnp.int32, values.shape, 1)
+    return jnp.where(lanes // HEAD_DIM == head, values, jnp.zeros_like(values))
+
+
+def fold_rows(values, how):
+    grouped = values.reshape(values.shape[0] // 8, 8, values.shape[1])
+    return how(how(grouped, axis=0), axis=0, keepdims=True)
+
+
+def attend_fwd_kernel(causal, has_bias, q_ref, k0_ref, v0_ref, k1_ref, v1_ref, bias_ref, o_ref, lse_ref, s_ref, p_ref):
+    rows = q_ref.shape[0]
+    k_refs = (k0_ref, k1_ref)
+    v_all = jnp.concatenate([v0_ref[...], v1_ref[...]], axis=0)
+    v_t = v_all.T
+    factor = HEAD_DIM ** (-0.5) * LOG2E
+    out_t = []
+    for head in range(2):
+        q = head_lanes(q_ref[...], head)
+        top = jnp.full((1, rows), -3e38, FLOAT)
+        for half, r, n, c in key_chunks(rows, causal):
+            s = nt_dot(k_refs[half][pl.ds(r, n), :], q[c:])
+            s = s * factor + bias_ref[pl.ds(half * rows + r, n), c:].astype(FLOAT)
+            s_ref[pl.ds(half * rows + r, n), c:] = s
+            peak = fold_rows(s, jnp.max)
+            peak = jnp.maximum(top[:, c:], peak)
+            top = jnp.concatenate([top[:, :c], peak], axis=1) if c else peak
+        total = jnp.zeros((1, rows), FLOAT)
+        for half, r, n, c in key_chunks(rows, causal):
+            p = jnp.exp2(s_ref[pl.ds(half * rows + r, n), c:] - top[:, c:])
+            part = total[:, c:] + fold_rows(p, jnp.sum)
+            total = jnp.concatenate([total[:, :c], part], axis=1) if c else part
+            p_ref[pl.ds(half * rows + r, n), c:] = p.astype(BRAIN)
+            if c:
+                p_ref[pl.ds(half * rows + r, n), :c] = jnp.zeros((n, c), BRAIN)
+        o_t = jnp.dot(v_t[head * HEAD_DIM : (head + 1) * HEAD_DIM], p_ref[...], preferred_element_type=FLOAT)
+        out_t.append(o_t / total)
+        lse_ref[0, pl.ds(head, 1), :] = top + jnp.log(total) * LOG2E
+    o_ref[...] = jnp.concatenate(out_t, axis=0).T.astype(o_ref.dtype)
+
+
+def attention_forward(queries, q_col, pairs, kv_col, pairs_other, bias, causal):
+    rows = queries.shape[0]
+    pair_count = D // PAIR
+    q_spec = pl.BlockSpec((rows, PAIR), lambda p: (0, q_col + p))
+    k_spec = pl.BlockSpec((rows, PAIR), lambda p: (0, kv_col + p))
+    v_spec = pl.BlockSpec((rows, PAIR), lambda p: (0, kv_col + pair_count + p))
+    k1_spec = pl.BlockSpec((rows, PAIR), lambda p: (0, p))
+    v1_spec = pl.BlockSpec((rows, PAIR), lambda p: (0, pair_count + p))
+    bias_spec = pl.BlockSpec((2 * rows, rows), lambda p: (0, 0))
+    return pl.pallas_call(
+        functools.partial(attend_fwd_kernel, causal, True),
+        grid=(pair_count,),
+        out_shape=[jax.ShapeDtypeStruct((rows, D), BRAIN), jax.ShapeDtypeStruct((pair_count, 8, rows), FLOAT)],
+        in_specs=[q_spec, k_spec, v_spec, k1_spec, v1_spec, bias_spec],
+        out_specs=[pl.BlockSpec((rows, PAIR), lambda p: (0, p)), pl.BlockSpec((1, 8, rows), lambda p: (p, 0, 0))],
+        scratch_shapes=[pltpu.VMEM((2 * rows, rows), FLOAT), pltpu.VMEM((2 * rows, rows), BRAIN)],
+        compiler_params=pltpu.CompilerParams(vmem_limit_bytes=48 << 20),
+        cost_estimate=pl.CostEstimate(flops=16 * rows * rows * D, bytes_accessed=10 * rows * D * 2, transcendentals=24 * rows * rows),
+        name="attend_fwd",
+    )(queries, pairs, pairs, pairs_other, pairs_other, bias)
+
+
+def attend_bwd_kernel(
+    causal, q_ref, k0_ref, v0_ref, k1_ref, v1_ref, bias_ref, o_ref, do_ref, lse_ref,
+    dq_ref, dk0_ref, dv0_ref, dk1_ref, dv1_ref, ds_ref,
+):
+    rows = q_ref.shape[0]
+    k_refs, v_refs = (k0_ref, k1_ref), (v0_ref, v1_ref)
+    dk_refs, dv_refs = (dk0_ref, dk1_ref), (dv0_ref, dv1_ref)
+    k_t = jnp.concatenate([k0_ref[...], k1_ref[...]], axis=0).T
+    scale = HEAD_DIM ** (-0.5)
+    factor = scale * LOG2E
+    prod_t = (o_ref[...].astype(FLOAT) * do_ref[...].astype(FLOAT)).T
+    dq_t = []
+    q_heads = [head_lanes(q_ref[...], head) for head in range(2)]
+    do_heads = [head_lanes(do_ref[...], head) for head in range(2)]
+    lses = [lse_ref[0, pl.ds(head, 1), :] for head in range(2)]
+    deltas = [fold_rows(prod_t[head * HEAD_DIM : (head + 1) * HEAD_DIM], jnp.sum) for head in range(2)]
+    for half, r, n, c in key_chunks(rows, causal):
+        k, v = k_refs[half][pl.ds(r, n), :], v_refs[half][pl.ds(r, n), :]
+        bias = bias_ref[pl.ds(half * rows + r, n), c:].astype(FLOAT)
+        dk = dv = None
+        for head in range(2):
+            q, do = q_heads[head][c:], do_heads[head][c:]
+            p = jnp.exp2(nt_dot(k, q) * factor + bias - lses[head][:, c:])
+            dv_part = jnp.dot(p.astype(BRAIN), do, preferred_element_type=FLOAT)
+            ds = (p * (nt_dot(v, do) - deltas[head][:, c:])).astype(BRAIN)
+            ds_ref[head, pl.ds(half * rows + r, n), c:] = ds
+            if c:
+                ds_ref[head, pl.ds(half * rows + r, n), :c] = jnp.zeros((n, c), BRAIN)
+            dk_part = jnp.dot(ds, q, preferred_element_type=FLOAT)
+            dk = dk_part if dk is None else dk + dk_part
+            dv = dv_part if dv is None else dv + dv_part
+        dk_refs[half][pl.ds(r, n), :] = (dk * scale).astype(dk_refs[half].dtype)
+        dv_refs[half][pl.ds(r, n), :] = dv.astype(dv_refs[half].dtype)
+    for head in range(2):
+        dq_t.append(jnp.dot(k_t[head * HEAD_DIM : (head + 1) * HEAD_DIM], ds_ref[head], preferred_element_type=FLOAT))
+    dq_ref[...] = (jnp.concatenate(dq_t, axis=0) * scale).T.astype(dq_ref.dtype)
+
+
+def attention_backward(queries, q_col, pairs, kv_col, pairs_other, bias, causal, attended, grad_attended, lse):
+    rows = queries.shape[0]
+    pair_count = D // PAIR
+    own = lambda p: (0, p)
+    block = (rows, PAIR)
+    q_spec = pl.BlockSpec(block, lambda p: (0, q_col + p))
+    k_spec = pl.BlockSpec(block, lambda p: (0, kv_col + p))
+    v_spec = pl.BlockSpec(block, lambda p: (0, kv_col + pair_count + p))
+    k1_spec = pl.BlockSpec(block, own)
+    v1_spec = pl.BlockSpec(block, lambda p: (0, pair_count + p))
+    bias_spec = pl.BlockSpec((2 * rows, rows), lambda p: (0, 0))
+    part = pl.BlockSpec(block, own)
+    return pl.pallas_call(
+        functools.partial(attend_bwd_kernel, causal),
+        grid=(pair_count,),
+        out_shape=[jax.ShapeDtypeStruct((rows, D), t) for t in (BRAIN, FLOAT, FLOAT, BRAIN, BRAIN)],
+        in_specs=[q_spec, k_spec, v_spec, k1_spec, v1_spec, bias_spec, part, part, pl.BlockSpec((1, 8, rows), lambda p: (p, 0, 0))],
+        out_specs=[part] * 5,
+        scratch_shapes=[pltpu.VMEM((2, 2 * rows, rows), BRAIN)],
+        compiler_params=pltpu.CompilerParams(vmem_limit_bytes=48 << 20),
+        cost_estimate=pl.CostEstimate(flops=40 * rows * rows * D, bytes_accessed=18 * rows * D * 2, transcendentals=24 * rows * rows),
+        name="attend_bwd",
+    )(queries, pairs, pairs, pairs_other, pairs_other, bias, attended, grad_attended, lse)
+
+
+def to_sibling(values):
+    count = lax.axis_size("dp")
+    return lax.ppermute(values, "dp", [(i, i ^ 1) for i in range(count)])
+
+
+def own_blocks(per_block, core):
+    zs = per_block.shape[0] // 2
+    both = per_block.reshape((zs, 2) + per_block.shape[1:])
+    flip = lax.rem(jnp.arange(zs, dtype=jnp.int32) + core, 2).reshape((zs,) + (1,) * (per_block.ndim - 1))
+    own = jnp.where(flip == 0, both[:, 0], both[:, 1])
+    return own, jnp.where(flip == 0, both[:, 1], both[:, 0])
+
+
+def ordered_keys(per_token, core):
+    own, other = own_blocks(per_token.reshape(-1, BLOCK), core)
+    return own.reshape(-1), jnp.concatenate([own.reshape(-1), other.reshape(-1)])
+
+
+def pack_small(enc_bias, dec_bias, enc_gain, dec_gain, enc_up_bias, dec_up_bias):
+    rows = enc_bias.shape[0]
+    parts = [enc_bias, dec_bias, enc_gain, dec_gain, enc_up_bias.reshape(rows, -1), dec_up_bias.reshape(rows, -1)]
+    width = sum(p.shape[1] for p in parts)
+    parts.append(jnp.zeros((rows, PAIR - width), parts[0].dtype))
+    return jnp.concatenate(parts, axis=1)
+
+
+def unpack_small(packed):
+    cuts, at = [], 0
+    for width in (6, 10, 2, 3, 4, 4):
+        cuts.append(packed[:, at : at + width])
+        at += width
+    return cuts[0], cuts[1], cuts[2], cuts[3], cuts[4].reshape(-1), cuts[5].reshape(-1)
+
+
+def columns(packed, widths):
+    cuts, at = [], 0
+    for width in widths:
+        cuts.append(packed[:, at : at + width])
+        at += width
+    return cuts
+
+
+def with_sibling(own_keys, own_values, other_keys, other_values):
+    got = to_sibling(jnp.concatenate([other_keys, other_values], axis=1)).astype(FLOAT)
+    return (jnp.concatenate([own_keys, own_values], axis=1) + got).astype(BRAIN)
+
+
+def self_attention_block(tokens, qkv_w, bias_vals, score_bias, causal):
+    zero_row = jnp.zeros((D,), FLOAT)
+    projected = (matmul(tokens, qkv_w) + jnp.concatenate([bias_vals[0], zero_row, bias_vals[1]])).astype(BRAIN)
+    other = to_sibling(projected[:, D:])
+    attended, lse = attention_forward(projected, 0, projected, D // PAIR, other, score_bias, causal)
+    return attended, (projected, other, lse)
+
+
+def self_attention_grad(state, attended, grad_attended, score_bias, causal):
+    projected, other, lse = state
+    dq, dk, dv, dk_other, dv_other = attention_backward(
+        projected, 0, projected, D // PAIR, other, score_bias, causal, attended, grad_attended, lse
+    )
+    return jnp.concatenate([dq, with_sibling(dk, dv, dk_other, dv_other)], axis=1)
+
+
+def fast_body(
+    enc_in, segments, dec_in, retrieved, enc_cot, dec_cot,
+    enc_qkv, enc_out, enc_up, enc_down, enc_bias, enc_up_bias, enc_gain,
+    dec_qkv, dec_out, cross_q, cross_kv, cross_out, dec_up, dec_down, dec_bias, dec_up_bias, dec_gain,
+):
+    dp, z, core = place()
+    axes = ("dp", "ctx")
+    small = pack_small(enc_bias, dec_bias, enc_gain, dec_gain, enc_up_bias, dec_up_bias)
+    first_pack = jnp.concatenate([enc_qkv, enc_out, enc_up, small], axis=1)
+    down_pack = jnp.concatenate([enc_down, dec_down], axis=1)
+    last_pack = jnp.concatenate([dec_qkv, dec_out, cross_q, cross_kv, cross_out, dec_up], axis=1)
+    first_widths = [w.shape[1] for w in (enc_qkv, enc_out, enc_up, small)]
+    last_widths = [w.shape[1] for w in (dec_qkv, dec_out, cross_q, cross_kv, cross_out, dec_up)]
+    first_all = lax.all_gather(first_pack, axes, axis=0, tiled=True)
+    down_all = lax.all_gather(down_pack, axes, axis=0, tiled=True)
+    last_all = lax.all_gather(last_pack, axes, axis=0, tiled=True)
+
+    (enc_t, dec_t, enc_c, dec_c), (seg_other, ret_other) = spread([enc_in, dec_in, enc_cot, dec_cot], [segments, retrieved], 0)
+    zs = enc_t.shape[0]
+    rows = zs * BLOCK
+    enc_t, dec_t, enc_c, dec_c = (t.reshape(rows, D) for t in (enc_t, dec_t, enc_c, dec_c))
+    here = z // 2 == core
+    seg = lax.dynamic_index_in_dim(jnp.where(here, segments, seg_other), lax.rem(z, 2), 0, keepdims=False)
+    ret = lax.dynamic_index_in_dim(jnp.where(here, retrieved, ret_other), lax.rem(z, 2), 0, keepdims=False)
+    seg_q, seg_k = ordered_keys(seg, core)
+    pos_q, pos_k = ordered_keys(jnp.arange(2 * rows, dtype=jnp.int32), core)
+    enc_mask = jnp.where(seg_k[:, None] == seg_q[None, :], 0.0, NEG).astype(FLOAT)
+    dec_mask = jnp.where(pos_k[:, None] <= pos_q[None, :], 0.0, NEG).astype(FLOAT)
+    ret_own, _ = own_blocks(ret, core)
+    member = jnp.any(pos_k[:, None, None] == ret_own[None], axis=-1)
+    cross_mask = jnp.broadcast_to(jnp.where(member, 0.0, NEG).astype(FLOAT)[:, :, None], (2 * rows, zs, BLOCK)).reshape(2 * rows, rows)
+
+    w_enc_qkv, w_enc_out, w_enc_up, smalls = columns(first_all, first_widths)
+    b_enc, b_dec, g_enc, g_dec, enc_ub, dec_ub = unpack_small(smalls)
+    eb, db, eg, dg = (v.astype(FLOAT).T for v in (b_enc, b_dec, g_enc, g_dec))
+    enc_ub, dec_ub = enc_ub.astype(FLOAT), dec_ub.astype(FLOAT)
+    w_enc_down, w_dec_down = down_all[:, :D], down_all[:, D:]
+    w_dec_qkv, w_dec_out, w_cross_q, w_cross_kv, w_cross_out, w_dec_up = columns(last_all, last_widths)
+
+    e_att, e_state = self_attention_block(enc_t, w_enc_qkv, eb, enc_mask, False)
+    e_first, e_sum = project_forward(e_att, enc_t.astype(FLOAT), w_enc_out, eb[2], eg[0], eb[4])
+    enc_final, e_ffn = ffn_forward(e_first, w_enc_up, enc_ub, w_enc_down, eb[3], eg[1], eb[5])
+    memory = enc_final.astype(BRAIN)
+    zero_row = jnp.zeros((D,), FLOAT)
+    d_att, d_state = self_attention_block(dec_t, w_dec_qkv, db, dec_mask, True)
+    d_first, d_sum = project_forward(d_att, dec_t.astype(FLOAT), w_dec_out, db[2], dg[0], db[7])
+    first_bf = d_first.astype(BRAIN)
+    cross_queries = (matmul(first_bf, w_cross_q) + db[3]).astype(BRAIN)
+    mem_pairs = (matmul(memory, w_cross_kv) + jnp.concatenate([zero_row, db[4]])).astype(BRAIN)
+    mem_other = to_sibling(mem_pairs)
+    crossed, cross_lse = attention_forward(cross_queries, 0, mem_pairs, 0, mem_other, cross_mask, False)
+    second, second_sum = project_forward(crossed, d_first, w_cross_out, db[5], dg[1], db[8])
+    dec_final, d_ffn = ffn_forward(second, w_dec_up, dec_ub, w_dec_down, db[6], dg[2], db[9])
+    grad_second, (g_dec_up, g_dec_ub, g_dec_down, g_db6, g_dg2, g_db9) = ffn_backward(
+        dec_c.astype(FLOAT), d_ffn, w_dec_up, w_dec_down, dg[2], db[9]
+    )
+    grad_first, grad_crossed, (g_cross_out, g_db5, g_dg1, g_db8) = project_backward(
+        grad_second, crossed, second_sum, w_cross_out, dg[1], db[8]
+    )
+    g_cq, dk, dv, dk_o, dv_o = attention_backward(
+        cross_queries, 0, mem_pairs, 0, mem_other, cross_mask, False, crossed, grad_crossed, cross_lse
+    )
+    own_memory = with_sibling(dk, dv, dk_o, dv_o)
+    g_cross_q, g_db3 = matmul_left(first_bf, g_cq), column_sum(g_cq)
+    grad_first = grad_first + matmul_right(g_cq, w_cross_q)
+    memory_grad = matmul_right(own_memory, w_cross_kv)
+    g_cross_kv, g_db4 = matmul_left(memory, own_memory), column_sum(own_memory[:, D:])
+    grad_dec, grad_d_att, (g_dec_out, g_db2, g_dg0, g_db7) = project_backward(grad_first, d_att, d_sum, w_dec_out, dg[0], db[7])
+    d_slope = self_attention_grad(d_state, d_att, grad_d_att, dec_mask, True)
+    grad_dec = grad_dec + matmul_right(d_slope, w_dec_qkv)
+    g_dec_qkv, d_slope_sum = matmul_left(dec_t, d_slope), column_sum(d_slope)
+    grad_e_first, (g_enc_up, g_enc_ub, g_enc_down, g_eb3, g_eg1, g_eb5) = ffn_backward(
+        enc_c.astype(FLOAT) + memory_grad, e_ffn, w_enc_up, w_enc_down, eg[1], eb[5]
+    )
+    grad_enc, grad_e_att, (g_enc_out, g_eb2, g_eg0, g_eb4) = project_backward(grad_e_first, e_att, e_sum, w_enc_out, eg[0], eb[4])
+    e_slope = self_attention_grad(e_state, e_att, grad_e_att, enc_mask, False)
+    grad_enc = grad_enc + matmul_right(e_slope, w_enc_qkv)
+    g_enc_qkv, e_slope_sum = matmul_left(enc_t, e_slope), column_sum(e_slope)
+
+    g_eb = jnp.stack([e_slope_sum[:D], e_slope_sum[2 * D :], g_eb2, g_eb3, g_eb4, g_eb5], axis=1)
+    g_db = jnp.stack(
+        [d_slope_sum[:D], d_slope_sum[2 * D :], g_db2, g_db3, g_db4, g_db5, g_db6, g_db7, g_db8, g_db9], axis=1
+    )
+    g_eg, g_dg = jnp.stack([g_eg0, g_eg1], axis=1), jnp.stack([g_dg0, g_dg1, g_dg2], axis=1)
+    g_small = pack_small(g_eb, g_db, g_eg, g_dg, g_enc_ub, g_dec_ub)
+    join = lambda parts: jnp.concatenate([p.astype(BRAIN) for p in parts], axis=1)
+    scatter = lambda packed: lax.psum_scatter(packed, axes, scatter_dimension=0, tiled=True).astype(FLOAT)
+    last_sum = scatter(join([g_dec_qkv, g_dec_out, g_cross_q, g_cross_kv, g_cross_out, g_dec_up]))
+    down_sum = scatter(join([g_enc_down, g_dec_down]))
+    first_sum = scatter(join([g_enc_qkv, g_enc_out, g_enc_up, g_small]))
+    r_dec_qkv, r_dec_out, r_cross_q, r_cross_kv, r_cross_out, r_dec_up = columns(last_sum, last_widths)
+    r_enc_down, r_dec_down = columns(down_sum, [D, D])
+    r_enc_qkv, r_enc_out, r_enc_up, r_small = columns(first_sum, first_widths)
+    r_eb, r_db, r_eg, r_dg, r_enc_ub, r_dec_ub = unpack_small(r_small)
+    home = collect(
+        [v.astype(BRAIN).reshape(zs, BLOCK, D) for v in (memory, dec_final, grad_enc, grad_dec)], 1
+    )
+    return (
+        home[0], home[1], home[2].astype(FLOAT), home[3].astype(FLOAT),
+        r_enc_qkv, r_enc_out, r_enc_up, r_enc_down, r_eb, r_enc_ub, r_eg,
+        r_dec_qkv, r_dec_out, r_cross_q, r_cross_kv, r_cross_out, r_dec_up, r_dec_down, r_db, r_dec_ub, r_dg,
+    )
+
+
 def solution(mesh):
     in_specs = (
         P("dp", "ctx", None),
@@ -594,4 +1060,18 @@
         P(("dp", "ctx")),
         P(("dp", "ctx"), None),
     )
-    return jax.shard_map(body, mesh=mesh, in_specs=in_specs, out_specs=out_specs, check_vma=False)
+
+    def run(*args):
+        sequences, tokens = args[0].shape[:2]
+        fits = (
+            mesh.shape["dp"] % 2 == 0
+            and sequences == 2 * mesh.shape["dp"]
+            and mesh.shape["ctx"] == 4
+            and tokens == 2 * BLOCK * mesh.shape["ctx"]
+            and args[2].shape == args[0].shape
+            and D % (mesh.shape["dp"] * mesh.shape["ctx"] * 8) == 0
+        )
+        chosen = fast_body if fits else body
+        return jax.shard_map(chosen, mesh=mesh, in_specs=in_specs, out_specs=out_specs, check_vma=False)(*args)
+
+    return run

time: 3080 us -> 983 us (0.32)
  waiting for transfers between devices: 2050 us -> 316 us
  blocking collectives: 343 us -> 0 us
  Pallas kernels: 0 us -> 307 us
  matrix products: 358 us -> 167 us
  other arithmetic: 142 us -> 39.2 us
    reduce_scatter x12 -> x1, waiting for transfers between devices: 1240 us -> 156 us  [fast_body(): lax.psum_scatter(packed, axes, scatter_dimension=0, tiled=True)]
    all_gather x14 -> x3, waiting for transfers between devices: 522 us -> 116 us  [the longest x1 76.7 us: fast_body(): down_all = lax.all_gather(down_pack, axes, axis=0, tiled=True)]
    pallas_call x0 -> x8, Pallas kernels: none -> 307 us  [the longest x1 114 us: spread(): pl.pallas_call(functools.partial(spread_kernel, count, zs), out_shape=sha...]
    all_gather x4 -> x0, blocking collectives: 282 us -> none  [the longest x1 80.8 us: fetch_weights(): lax.all_gather(shards[6], ('dp', 'ctx'), axis=0, tiled=True)]
    unnamed x32 -> x8, waiting for transfers between devices: 289 us -> 43.8 us
    dot_general x18 -> x0, matrix products: 171 us -> none  [the longest x3 51.4 us: attend_backward(): jnp.einsum('brhd,bkhd->bhrk', grad_heads, value_heads, preferred_element_...]
    unnamed x1 -> x0, blocking collectives: 60.7 us -> none
    convert_element_type x7, other arithmetic: 49.4 us -> 9.29 us  [the longest x3 4.02 us: with_sibling(): return (jnp.concatenate([own_keys, own_values], axis=1) + got).astype(BRAIN)]
  transfers between devices with their start and end apart: 29 -> 12, of which waited for: 24 -> 4; matrix products, arithmetic and copies ran while one was open for 16% -> 24% of each run, Pallas kernels for 0% -> 27%
where the time goes in v1:
time: 983 us; the launch traced here: 975 us
  waiting for transfers between devices  316 us (32%)
  Pallas kernels  307 us (31%)
  matrix products  167 us (17%)
  local copies, waits for them, and re-layouts  126 us (13%)
  other arithmetic  39.2 us (4%)
  between operations  16.3 us (2%)
    reduce_scatter x1, waiting for transfers between devices, fast_body(): lax.psum_scatter(packed, axes, scatter_dimension=0, tiled=True)  156 us
    pallas_call x1, Pallas kernels, spread(): pl.pallas_call(functools.partial(spread_kernel, count, zs), out_shape=sha...  114 us
    pallas_call x1, Pallas kernels, collect(): pl.pallas_call(functools.partial(collect_kernel, count, zs), out_shape=[j...  77.7 us
    all_gather x1, waiting for transfers between devices, fast_body(): down_all = lax.all_gather(down_pack, axes, axis=0, tiled=True)  76.7 us
    pallas_call x3, Pallas kernels, attention_backward(): pl.pallas_call(functools.partial(attend_bwd_kernel, causal), grid=(pair_c...  74.9 us
    dot_general x11, matrix products, matmul(): return jnp.dot(left_side, right_side, preferred_element_type=FLOAT)  71.3 us
    dot_general x11, matrix products, matmul_right(): lax.dot_general(left_side, right_side, (((1,), (1,)), ((), ())), preferre...  52.4 us
    unnamed x273, local copies, waits for them, and re-layouts  44.7 us
  transfers between devices with their start and end apart: 12, of which 4 were waited for; matrix products, arithmetic and copies ran while one was open for 24% of the time, Pallas kernels for 27%

profile of v1, /device:TPU:0, one launch (start us, length us, event | category | flops | bytes accessed | tf_op | source)
XLA Modules:
  0.0 974.8 jit_solution(13775179951996619366)
XLA Ops:
  20.5 114.2 %spread_tokens.1 = (bf16[4,128,768]{2,1,0:T(8,128)(2,1)}, bf16[4,128,768]{2,1,0:T(8,128)(2,1)}, bf16[4,128,768]{2,1,0:T(8,128)(2,1)}, bf16[4,128,768]{2,1,0:T(8,...) custom-call(bf16[2,256,768]{2,1,0:T(8,128)(2,1)} %refs_0_.1, bf16[2,256,768]{2,1,0:T(8,128)(2,1)} %refs_1_.1, ...), custom_call_target="tpu_custom_call" | custom-call | tf_op jit(solution)/shard_map/spread_tokens/pallas_call | solution.py:630
  142.9 4.2 fusion.14.q_ref.k0_ref.v0_ref
  161.8 13.6 %attend_fwd.3 = (bf16[512,768]{1,0:T(8,128)(2,1)S(1)}, f32[6,8,512]{2,1,0:T(8,128)S(1)}) custom-call(bf16[512,2304]{1,0:T(8,128)(2,1)} %copy-done.18, bf16[512,2304]{1,0:T(8,128)(2,1)} %copy-done.18, bf16[512,2304]{1,0:T(8,128)(2,1)} %copy-done.18, bf16[512,1536]{1,0:T(8,128)(2,1)} %collective-permute-done.k1_ref.v1_ref, ...), custom_call_target="tpu_custom_call" | custom-call | flops 3221225472 | bytes 7864320 | tf_op jit(solution)/shard_map/attend_fwd/pallas_call | solution.py:771
  179.1 20.2 %multiply_convert_fusion.1 = (bf16[512,3072]{1,0:T(8,128)(2,1)}, f32[512,3072]{1,0:T(8,128)}, f32[512,3072]{1,0:T(8,128)}) fusion(f32[3072]{0:T(1024)S(1)} %reshape.375, bf16[768,6272]{1,0:T(8,128)(2,1)} %all-gather.4.cloned.1.call-done, f32[512,768]{1,0:T(8,128)S(1)} %get-tuple-element.255, f32[768]{0:T(1024)S(1)} %get-tuple-element.198, ...), kind=kOutput, calls=%fused_computation.21 | convolution fusion | flops 2521694208 | bytes 22042624 | tf_op jit(solution)/shard_map/dot_general | solution.py:23
  199.3 39.7 %all-gather.8.cloned.1.call-done = bf16[768,9216]{1,0:T(8,128)(2,1)} async-done(((bf16[24,9216]{1,0:T(8,128)(2,1)}), bf16[768,9216]{1,0:T(8,128)(2,1)}) %all-gather.8.cloned.1.call-update) | async-done | bytes 14155792 | tf_op jit(solution)/shard_map/all_gather | solution.py:925
  239.1 4.0 fusion.15.q_ref.k0_ref.v0_ref
  246.0 76.7 %all-gather.6.cloned.1.call-done = bf16[3072,1536]{1,0:T(8,128)(2,1)} async-done(((bf16[96,1536]{1,0:T(8,128)(2,1)}), bf16[3072,1536]{1,0:T(8,128)(2,1)}) %all-gather.6.cloned.1.call-update) | async-done | bytes 9437200 | tf_op jit(solution)/shard_map/all_gather | solution.py:924
  322.7 6.5 fusion.122
  333.5 11.5 %attend_fwd.4 = (bf16[512,768]{1,0:T(8,128)(2,1)S(1)}, f32[6,8,512]{2,1,0:T(8,128)S(1)}) custom-call(bf16[512,2304]{1,0:T(8,128)(2,1)} %copy-done.19, bf16[512,2304]{1,0:T(8,128)(2,1)} %copy-done.19, bf16[512,2304]{1,0:T(8,128)(2,1)} %copy-done.19, bf16[512,1536]{1,0:T(8,128)(2,1)} %collective-permute-done.1.k1_ref.v1_ref, ...), custom_call_target="tpu_custom_call" | custom-call | flops 3221225472 | bytes 7864320 | tf_op jit(solution)/shard_map/attend_fwd/pallas_call | solution.py:771
  350.3 14.8 %attend_fwd.5 = (bf16[512,768]{1,0:T(8,128)(2,1)S(1)}, f32[6,8,512]{2,1,0:T(8,128)S(1)}) custom-call(bf16[512,768]{1,0:T(8,128)(2,1)S(1)} %add_convert_fusion.5.q_ref, bf16[512,1536]{1,0:T(8,128)(2,1)S(1)} %fusion.42.k0_ref.v0_ref, bf16[512,1536]{1,0:T(8,128)(2,1)S(1)} %fusion.42.k0_ref.v0_ref, bf16[512,1536]{1,0:T(8,128)(2,1)S(1)} %collective-permute-done.2.k1_ref.v1_ref, ...), custom_call_target="tpu_custom_call" | custom-call | flops 3221225472 | bytes 7864320 | tf_op jit(solution)/shard_map/attend_fwd/pallas_call | solution.py:771
  368.0 20.5 %multiply_convert_fusion = (bf16[512,3072]{1,0:T(8,128)(2,1)S(1)}, f32[512,3072]{1,0:T(8,128)}, f32[512,3072]{1,0:T(8,128)}) fusion(f32[3072]{0:T(1024)S(1)} %reshape.376, bf16[768,9216]{1,0:T(8,128)(2,1)} %all-gather.8.cloned.1.call-done, f32[512,768]{1,0:T(8,128)S(1)} %get-tuple-element.262, f32[768]{0:T(1024)S(1)} %get-tuple-element.186, ...), kind=kOutput, calls=%fused_computation.8 | convolution fusion | flops 2521694208 | bytes 22042624 | tf_op jit(solution)/shard_map/dot_general | solution.py:23
  395.4 8.5 fusion.127
  403.8 7.1 multiply_reduce_fusion
  414.8 24.4 %attend_bwd.3 = (bf16[512,768]{1,0:T(8,128)(2,1)S(1)}, f32[512,768]{1,0:T(8,128)}, f32[512,768]{1,0:T(8,128)}, bf16[512,768]{1,0:T(8,128)(2,1)S(1)}, bf16[512,768]{1,0:T(8,128)(2,1)S(1)}) custom-call(bf16[512,768]{1,0:T(8,128)(2,1)S(1)} %add_convert_fusion.5.q_ref, bf16[512,1536]{1,0:T(8,128)(2,1)} %copy-done.9, bf16[512,1536]{1,0:T(8,128)(2,1)} %copy-done.9, ...), custom_call_target="tpu_custom_call" | custom-call | flops 8053063680 | bytes 14155776 | tf_op jit(solution)/shard_map/attend_bwd/pallas_call | solution.py:834
  440.5 5.2 convolution_convert_fusion.2
  447.0 4.0 multiply_reduce_fusion.2
  456.6 4.2 pad_maximum_fusion
  460.9 12.7 %copy.168 = bf16[3072,1536]{1,0:T(8,128)(2,1)} copy(bf16[3072,1536]{0,1:T(8,128)(2,1)} %pad_maximum_fusion) | data formatting | bytes 18874368
  491.3 9.9 %fusion.126 = (bf16[3072]{0:T(1024)(128)(2,1)}, bf16[512,3072]{1,0:T(8,128)(2,1)S(1)}) fusion(f32[512,3072]{1,0:T(8,128)} %get-tuple-element.225, bf16[512,768]{1,0:T(8,128)(2,1)S(1)} %copy-done.61, bf16[3072,1536]{1,0:T(8,128)(2,1)} %all-gather.6.cloned.1.call-done, f32[512,3072]{1,0:T(8,128)} %get-tuple-element.256, f32[3072]{0:T(1024)S(1)} %copy-done.80), kind=kOutput, calls=%fused_computation.267 | convolution fusion | flops 2441081856 | bytes 21252096 | tf_op jit(solution)/shard_map/dot_general | solution.py:33
  501.3 3.6 multiply_reduce_fusion.3
  508.6 24.5 %attend_bwd.4 = (bf16[512,768]{1,0:T(8,128)(2,1)S(1)}, f32[512,768]{1,0:T(8,128)S(1)}, f32[512,768]{1,0:T(8,128)}, bf16[512,768]{1,0:T(8,128)(2,1)S(1)}, bf16[512,768]{1,0:T(8,128)(2,1)S(1)}) custom-call(bf16[512,2304]{1,0:T(8,128)(2,1)} %copy-done.18, bf16[512,2304]{1,0:T(8,128)(2,1)} %copy-done.18, bf16[512,2304]{1,0:T(8,128)(2,1)} %copy-done.18, ...), custom_call_target="tpu_custom_call" | custom-call | flops 8053063680 | bytes 14155776 | tf_op jit(solution)/shard_map/attend_bwd/pallas_call | solution.py:834
  537.4 26.1 %attend_bwd.5 = (bf16[512,768]{1,0:T(8,128)(2,1)S(1)}, f32[512,768]{1,0:T(8,128)S(1)}, f32[512,768]{1,0:T(8,128)}, bf16[512,768]{1,0:T(8,128)(2,1)S(1)}, bf16[512,768]{1,0:T(8,128)(2,1)S(1)}) custom-call(bf16[512,2304]{1,0:T(8,128)(2,1)} %copy-done.19, bf16[512,2304]{1,0:T(8,128)(2,1)} %copy-done.19, bf16[512,2304]{1,0:T(8,128)(2,1)} %copy-done.19, ...), custom_call_target="tpu_custom_call" | custom-call | flops 8053063680 | bytes 14155776 | tf_op jit(solution)/shard_map/attend_bwd/pallas_call | solution.py:834
  577.9 7.5 convolution_convert_fusion.4
  593.6 3.9 convolution_convert_fusion.5
  598.2 18.8 %concatenate.76 = bf16[768,6272]{1,0:T(8,128)(2,1)} concatenate(bf16[768,2304]{1,0:T(8,128)(2,1)} %convolution_convert_fusion.5, bf16[768,768]{1,0:T(8,128)(2,1)S(1)} %copy-done.37, bf16[768,3072]{1,0:T(8,128)(2,1)} %convolution_convert_fusion.4, bf16[768,1]{1,0:T(8,128)(2,1)} %stack.105, bf16[768,1]{1,0:T(8,128)(2,1)} %stack.106, bf16[768,1]{1,0:T(8,128)(2,1)} %stack.107, ...), dimensions={1} | concatenate | bytes 19267584 | tf_op jit(solution)/shard_map/concatenate | solution.py:995
  632.6 5.0 fusion.13
  645.4 4.8 fusion.12
  652.0 5.7 add_convert_fusion.3
  657.7 4.9 add_convert_fusion.2
  662.6 77.7 %collect_tokens.1 = (bf16[2,256,768]{2,1,0:T(8,128)(2,1)}, bf16[2,256,768]{2,1,0:T(8,128)(2,1)}, bf16[2,256,768]{2,1,0:T(8,128)(2,1)}, bf16[2,256,768]{2,1,0:T(8,128)(2,1)}) custom-call(bf16[4,128,768]{2,1,0:T(8,128)(2,1)} %bitcast.79, bf16[4,128,768]{2,1,0:T(8,128)(2,1)} %bitcast.78, bf16[4,128,768]{2,1,0:T(8,128)(2,1)} %bitcast.82, ...), custom_call_target="tpu_custom_call" | custom-call | tf_op jit(solution)/shard_map/collect_tokens/pallas_call | solution.py:700
  747.1 43.7 %reduce-scatter.12.cloned.1.call-done = bf16[24,6272]{1,0:T(8,128)(2,1)} async-done(((bf16[768,6272]{1,0:T(8,128)(2,1)}), bf16[24,6272]{1,0:T(8,128)(2,1)}) %reduce-scatter.12.cloned.1.call-update) | async-done | bytes 301072
  803.3 156.2 %reduce-scatter.8.cloned.1.call-done = bf16[24,9216]{1,0:T(8,128)(2,1)} async-done(((bf16[768,9216]{1,0:T(8,128)(2,1)}), bf16[24,9216]{1,0:T(8,128)(2,1)}) %reduce-scatter.8.cloned.1.call-update) | async-done | bytes 442384 | tf_op jit(solution)/shard_map/reduce_scatter | solution.py:996
  (450 shorter events, 174.0 us)
Async XLA Ops:
  7.2 130.3 %all-gather.4.cloned.1.call-start = ((), (), s32[]{:S(2)}) async-start(), calls=%async_computation.3 | async-start | bytes 9934848 | tf_op jit(solution)/shard_map/all_gather | solution.py:923
  13.7 225.3 %all-gather.8.cloned.1.call-start = ((), (), s32[]{:S(2)}) async-start(), calls=%async_computation.5 | async-start | bytes 14598144 | tf_op jit(solution)/shard_map/all_gather | solution.py:925
  18.8 115.8 %copy-start.68 = (s32[2,8,512]{2,1,0:T(8,128)S(1)}, s32[2,8,512]{2,1,0:T(8,128)}, u32[]{:S(2)}) copy-start(s32[2,8,512]{2,1,0:T(8,128)} %refs_5_.1) | copy-start | bytes 98308
  18.9 116.6 %copy-start.69 = (s32[2,1024]{1,0:T(2,128)S(1)}, s32[2,1024]{1,0:T(2,128)}, u32[]{:S(2)}) copy-start(s32[2,1024]{1,0:T(2,128)} %refs_4_.1) | copy-start | bytes 24580
  19.6 303.1 %all-gather.6.cloned.1.call-start = ((), (), s32[]{:S(2)}) async-start(), calls=%async_computation.4 | async-start | bytes 9732096 | tf_op jit(solution)/shard_map/all_gather | solution.py:924
  20.4 723.7 %reduce-scatter.10.cloned.1.call-start = ((), (), s32[]{:S(2)}) async-start(), calls=%async_computation.7 | async-start | bytes 9732096
  139.7 183.0 %copy-start.100 = (f32[768]{0:T(1024)}, f32[768]{0:T(1024)S(1)}, u32[]{:S(2)}) copy-start(f32[768]{0:T(1024)S(1)} %get-tuple-element.198) | copy-start | bytes 9220
  142.8 222.3 %copy-start.104 = (f32[768]{0:T(1024)}, f32[768]{0:T(1024)S(1)}, u32[]{:S(2)}) copy-start(f32[768]{0:T(1024)S(1)} %get-tuple-element.190) | copy-start | bytes 9220
  142.8 245.7 %copy-start.102 = (f32[768]{0:T(1024)}, f32[768]{0:T(1024)S(1)}, u32[]{:S(2)}) copy-start(f32[768]{0:T(1024)S(1)} %get-tuple-element.186) | copy-start | bytes 9220
  149.9 12.0 %collective-permute-start = (bf16[512,1536]{1,0:T(8,128)(2,1)}, bf16[512,1536]{1,0:T(8,128)(2,1)}, u32[]{:S(2)}, u32[]{:S(2)}) collective-permute-start(bf16[512,1536]{1,0:T(8,128)(2,1)} %slice.307), channel_id=1, source_target_pairs={{0,4},{4,0},{8,12},{12,8},{16,20},{20,16},{24,28},{28,24},{1,5},{5... | collective-permute-start | bytes 4718600 | tf_op jit(solution)/shard_map/ppermute | solution.py:849
  155.1 178.4 %copy-start = (f32[1024,512]{1,0:T(8,128)}, f32[1024,512]{1,0:T(8,128)S(1)}, u32[]{:S(2)}) copy-start(f32[1024,512]{1,0:T(8,128)S(1)} %compare_select_fusion.bias_ref) | copy-start | bytes 6291460
  160.1 162.6 %copy-start.74 = (f32[768]{0:T(1024)}, f32[768]{0:T(1024)S(1)}, u32[]{:S(2)}) copy-start(f32[768]{0:T(1024)S(1)} %get-tuple-element.195) | copy-start | bytes 9220
  161.8 203.4 %copy-start.72 = (f32[768]{0:T(1024)}, f32[768]{0:T(1024)S(1)}, u32[]{:S(2)}) copy-start(f32[768]{0:T(1024)S(1)} %get-tuple-element.183) | copy-start | bytes 9220
  161.8 249.1 %copy-start.77 = (f32[768]{0:T(1024)}, f32[768]{0:T(1024)S(1)}, u32[]{:S(2)}) copy-start(f32[768]{0:T(1024)S(1)} %get-tuple-element.182) | copy-start | bytes 9220
  178.2 21.1 %copy-start.70 = (f32[512]{0:T(512)}, f32[512]{0:T(512)S(1)}, u32[]{:S(2)}) copy-start(f32[512]{0:T(512)S(1)} %multiply_reduce_fusion.12) | copy-start | bytes 6148
  178.3 144.4 %copy-start.96 = (f32[512]{0:T(512)}, f32[512]{0:T(512)S(1)}, u32[]{:S(2)}) copy-start(f32[512]{0:T(512)S(1)} %fusion.84) | copy-start | bytes 6148
  179.1 60.0 %copy-start.109 = (bf16[4,128,768]{2,1,0:T(8,128)(2,1)S(1)}, bf16[4,128,768]{2,1,0:T(8,128)(2,1)}, u32[]{:S(2)}) copy-start(bf16[4,128,768]{2,1,0:T(8,128)(2,1)} %get-tuple-element.55) | copy-start | bytes 2359300
  245.7 87.8 %collective-permute-start.1 = (bf16[512,1536]{1,0:T(8,128)(2,1)}, bf16[512,1536]{1,0:T(8,128)(2,1)}, u32[]{:S(2)}, u32[]{:S(2)}) collective-permute-start(bf16[512,1536]{1,0:T(8,128)(2,1)} %slice.325), channel_id=1, source_target_pairs={{0,4},{4,0},{8,12},{12,8},{16,20},{20,16},{24,28},{28,24},{1,5},{5... | collective-permute-start | bytes 4718600 | tf_op jit(solution)/shard_map/ppermute | solution.py:849
  333.2 17.1 %collective-permute-start.2 = (bf16[512,1536]{1,0:T(8,128)(2,1)S(1)}, bf16[512,1536]{1,0:T(8,128)(2,1)S(1)}, u32[]{:S(2)}, u32[]{:S(2)}) collective-permute-start(bf16[512,1536]{1,0:T(8,128)(2,1)S(1)} %fusion.42.k0_ref.v0_ref), channel_id=1, source_target_pairs={{0,4},{4,0},{8,12},{12,8},{16,20},{20,16},{24,28},{28,24},{1,5},{5... | collective-permute-start | bytes 4718600 | tf_op jit(solution)/shard_map/ppermute | solution.py:849
  365.1 49.6 %copy-start.16 = (bf16[512,768]{1,0:T(8,128)(2,1)}, bf16[512,768]{1,0:T(8,128)(2,1)S(1)}, u32[]{:S(2)}) copy-start(bf16[512,768]{1,0:T(8,128)(2,1)S(1)} %get-tuple-element.58.o_ref) | copy-start | bytes 2359300
  365.2 23.4 %slice-start.3 = ((s8[9437184]{0:T(1024)(128)(4,1)}), s8[4194304]{0:T(1024)(128)(4,1)S(1)}, s32[]{:S(2)}) async-start(s8[9437184]{0:T(1024)(128)(4,1)} %bitcast.91), calls=%async_computation.12 | async-start | bytes 8388608
  367.7 43.3 %copy-start.21 = (f32[512,768]{1,0:T(8,128)}, f32[512,768]{1,0:T(8,128)S(1)}, u32[]{:S(2)}) copy-start(f32[512,768]{1,0:T(8,128)S(1)} %get-tuple-element.262) | copy-start | bytes 4718596
  368.0 42.9 %copy-start.84 = (f32[512]{0:T(512)}, f32[512]{0:T(512)S(1)}, u32[]{:S(2)}) copy-start(f32[512]{0:T(512)S(1)} %fusion.87) | copy-start | bytes 6148
  439.1 46.3 %copy-start.2 = (bf16[512,768]{1,0:T(8,128)(2,1)}, bf16[512,768]{1,0:T(8,128)(2,1)S(1)}, u32[]{:S(2)}) copy-start(bf16[512,768]{1,0:T(8,128)(2,1)S(1)} %get-tuple-element.72) | copy-start | bytes 2359300
  439.3 6.5 collective-permute-start.3
  473.6 317.3 %reduce-scatter.12.cloned.1.call-start = ((), (), s32[]{:S(2)}) async-start(), calls=%async_computation.8 | async-start | bytes 9934848
  506.2 28.5 %copy-start.34 = (f32[512,768]{1,0:T(8,128)}, f32[512,768]{1,0:T(8,128)S(1)}, u32[]{:S(2)}) copy-start(f32[512,768]{1,0:T(8,128)S(1)} %get-tuple-element.213) | copy-start | bytes 4718596
  534.5 51.0 %collective-permute-start.4 = (bf16[512,1536]{1,0:T(8,128)(2,1)}, bf16[512,1536]{1,0:T(8,128)(2,1)}, u32[]{:S(2)}, u32[]{:S(2)}) collective-permute-start(bf16[512,1536]{1,0:T(8,128)(2,1)} %pad_maximum_fusion.4), channel_id=1, source_target_pairs={{0,4},{4,0},{8,12},{12,8},{16,20},{20,16},{24,28},{28,24},{1,5},{5... | collective-permute-start | bytes 4718600 | tf_op jit(solution)/shard_map/ppermute | solution.py:849
  565.0 24.5 %collective-permute-start.5 = (bf16[512,1536]{1,0:T(8,128)(2,1)}, bf16[512,1536]{1,0:T(8,128)(2,1)}, u32[]{:S(2)}, u32[]{:S(2)}) collective-permute-start(bf16[512,1536]{1,0:T(8,128)(2,1)} %pad_maximum_fusion.5), channel_id=1, source_target_pairs={{0,4},{4,0},{8,12},{12,8},{16,20},{20,16},{24,28},{28,24},{1,5},{5... | collective-permute-start | bytes 4718600 | tf_op jit(solution)/shard_map/ppermute | solution.py:849
  617.1 342.3 %reduce-scatter.8.cloned.1.call-start = ((), (), s32[]{:S(2)}) async-start(), calls=%async_computation.6 | async-start | bytes 14598144 | tf_op jit(solution)/shard_map/reduce_scatter | solution.py:996
  745.4 220.3 %copy-start.57 = (bf16[2,256,768]{2,1,0:T(8,128)(2,1)S(1)}, bf16[2,256,768]{2,1,0:T(8,128)(2,1)}, u32[]{:S(2)}) copy-start(bf16[2,256,768]{2,1,0:T(8,128)(2,1)} %get-tuple-element.297) | copy-start | bytes 2359300
  792.3 174.3 %copy-start.56 = (bf16[2,256,768]{2,1,0:T(8,128)(2,1)S(1)}, bf16[2,256,768]{2,1,0:T(8,128)(2,1)}, u32[]{:S(2)}) copy-start(bf16[2,256,768]{2,1,0:T(8,128)(2,1)} %get-tuple-element.298) | copy-start | bytes 2359300
  (105 other events, 593.8 us)
Sparse Core Ops, SparseCore 0:
  13.9 117.7 all-gather.3
  135.1 103.9 all-gather.7
  242.4 80.2 all-gather.5
  473.7 134.0 reduce-scatter.9
  617.2 173.5 reduce-scatter.11
  797.7 161.6 reduce-scatter.7

commit v2 on v1

--- a/solution.py
+++ b/solution.py
@@ -550,10 +550,9 @@
 
 
 MESH_ID = pl.DeviceIdType.MESH
-LOG2E = 1.4426950408889634
-PAIR = 128
 ANY = pl.BlockSpec(memory_space=pl.ANY)
 DMA_SEM = pltpu.SemaphoreType.DMA
+PAIR = 128
 
 
 def place():
@@ -561,151 +560,413 @@
     return dp, lax.axis_index("ctx"), lax.rem(dp, 2)
 
 
-def spread_kernel(token_count, zs, *refs):
-    tokens, ints = refs[:token_count], refs[token_count : token_count + 2]
-    outs, int_outs = refs[token_count + 2 : 2 * token_count + 2], refs[2 * token_count + 2 : 2 * token_count + 4]
-    send, recv, local, int_send, int_recv = refs[2 * token_count + 4 :]
+def spot():
     dp, z, core = place()
-    pair = dp - core
+    return dp, z, core, lax.rem(dp // 2, 2), dp // 4
+
+
+def dp_of(y, x, core):
+    return (y * 2 + x) * 2 + core
+
+
+def greet():
+    dp, z, core, x, y = spot()
+    zs = lax.axis_size("ctx")
     barrier = pltpu.get_barrier_semaphore()
+
+    def hello(dp_to, z_to):
+        pl.semaphore_signal(barrier, 1, device_id=(dp_to, z_to), device_id_type=MESH_ID)
+
     for step in range(zs):
-        for other in range(2):
-            if step or other:
-                pl.semaphore_signal(
-                    barrier, 1, device_id=(pair + lax.rem(core + other, 2), lax.rem(z + step, zs)), device_id_type=MESH_ID
-                )
-    pl.semaphore_wait(barrier, 2 * zs - 1)
-    sibling = (pair + 1 - core, z)
-    int_copies = []
-    for i in range(2):
-        copy = pltpu.make_async_remote_copy(
-            ints[i], int_outs[i], int_send.at[i], int_recv.at[i], device_id=sibling, device_id_type=MESH_ID
-        )
-        copy.start()
-        int_copies.append(copy)
-
-    def each(what):
-        for t in range(token_count):
+        if step:
+            hello(dp, lax.rem(z + step, zs))
+        hello(dp_of(y, x, 1 - core), lax.rem(z + step, zs))
+    hello(dp_of(y, 1 - x, core), z)
+    hello(dp_of(1 - y, x, core), z)
+    pl.semaphore_wait(barrier, 2 * zs + 1)
+
+
+def remote(source, target, send, recv, dp_to, z_to):
+    return pltpu.make_async_remote_copy(source, target, send, recv, device_id=(dp_to, z_to), device_id_type=MESH_ID)
+
+
+def staged(count, stages):
+    steps = []
+    for turn in range(count + max(lag for lag, _ in stages)):
+        for lag, fn in stages:
+            if 0 <= turn - lag < count:
+                steps.append(functools.partial(fn, turn - lag))
+    return steps
+
+
+def halves(shapes):
+    chunks = []
+    for i, (rows, n) in enumerate(shapes):
+        cut = (n // 2) // PAIR * PAIR
+        for order, (at, width) in enumerate(((0, cut), (cut, n - cut))):
+            if width:
+                chunks.append((i, at, width, order))
+    return chunks
+
+
+def gather_job(shards):
+    zs = lax.axis_size("ctx")
+    everyone = lax.axis_size("dp") * zs
+    chunks = halves([s.shape for s in shards])
+    count = len(chunks)
+
+    def steps(ins, outs, scratch):
+        send, recv, local = scratch
+        dp, z, core, x, y = spot()
+
+        def own_part(t):
+            i, at, width, _ = chunks[t]
+            return ins[i].at[:, pl.ds(at, width)]
+
+        def rows_of(t, dp_at, z_at=None):
+            i, at, width, _ = chunks[t]
+            where = pl.ds(dp_at * zs, zs) if z_at is None else dp_at * zs + z_at
+            return outs[i].at[where, :, pl.ds(at, width)]
+
+        def keep(t):
+            return pltpu.make_async_copy(own_part(t), rows_of(t, dp, z), local.at[t])
+
+        def along_z(t, k):
+            return remote(own_part(t), rows_of(t, dp, z), send.at[t, k - 1], recv.at[t, k - 1], dp, lax.rem(z + k, zs))
+
+        def hop(t, kind):
+            order = chunks[t][3]
+            near = (y, 1 - x) if order == 0 else (1 - y, x)
+            far = (1 - y, x) if order == 0 else (y, 1 - x)
+            block, to = {
+                3: ((y, x), near), 4: ((y, x), far), 5: (near, far),
+                6: ((y, x), None), 7: (near, None), 8: (far, None), 9: ((1 - y, 1 - x), None),
+            }[kind]
+            dp_to = dp_of(y, x, 1 - core) if to is None else dp_of(to[0], to[1], core)
+            part = rows_of(t, dp_of(block[0], block[1], core))
+            return remote(part, part, send.at[t, kind], recv.at[t, kind], dp_to, z)
+
+        def begin(t):
+            keep(t).start()
+            for k in range(1, zs):
+                along_z(t, k).start()
+
+        def first(t):
+            keep(t).wait()
+            for k in range(1, zs):
+                along_z(t, k).wait_recv()
+            for kind in (3, 4, 6):
+                hop(t, kind).start()
+
+        def second(t):
+            hop(t, 3).wait_recv()
+            for kind in (5, 7):
+                hop(t, kind).start()
+
+        def third(t):
+            hop(t, 4).wait_recv()
+            hop(t, 8).start()
+            hop(t, 5).wait_recv()
+            hop(t, 9).start()
+
+        def finish(t):
+            for kind in range(6, 10):
+                hop(t, kind).wait_recv()
+            for k in range(1, zs):
+                along_z(t, k).wait_send()
+            for kind in range(3, 10):
+                hop(t, kind).wait_send()
+
+        return staged(count, [(0, begin), (2, first), (3, second), (4, third), (5, finish)])
+
+    shapes = [jax.ShapeDtypeStruct((everyone,) + s.shape, s.dtype) for s in shards]
+    scratch = [DMA_SEM((count, 10)), DMA_SEM((count, 10)), DMA_SEM((count,))]
+    return shards, [ANY] * len(shards), shapes, [ANY] * len(shards), scratch, steps
+
+
+def scatter_job(grads):
+    zs, dps = lax.axis_size("ctx"), lax.axis_size("dp")
+    rows = [g.shape[0] // (zs * dps) for g in grads]
+    chunks = halves([(r, g.shape[1]) for r, g in zip(rows, grads)])
+    count = len(chunks)
+    inputs = [g.reshape(dps, zs * r, g.shape[1]) for r, g in zip(rows, grads)]
+    scratch = [DMA_SEM((count, 10)), DMA_SEM((count, 10)), DMA_SEM((count, 4))]
+    for i, _, width, _ in chunks:
+        scratch += [
+            pltpu.VMEM((4, zs * rows[i], width), BRAIN),
+            pltpu.VMEM((4, zs * rows[i], width), BRAIN),
+            pltpu.VMEM((2, zs * rows[i], width), BRAIN),
+            pltpu.VMEM((zs * rows[i], width), BRAIN),
+            pltpu.VMEM((zs, rows[i], width), BRAIN),
+            pltpu.VMEM((zs - 1, rows[i], width), BRAIN),
+        ]
+
+    def steps(ins, outs, scratch):
+        send, recv, local = scratch[:3]
+        dp, z, core, x, y = spot()
+        buffers = [scratch[3 + 6 * t : 9 + 6 * t] for t in range(count)]
+
+        def source(t, dp_at):
+            i, at, width, _ = chunks[t]
+            return ins[i].at[dp_at, :, pl.ds(at, width)]
+
+        def load(t, b):
+            return pltpu.make_async_copy(source(t, dp_of(b // 2, b % 2, core)), buffers[t][0].at[b], local.at[t, b])
+
+        def to_core(t, b):
+            return remote(
+                source(t, dp_of(b // 2, b % 2, 1 - core)), buffers[t][1].at[b], send.at[t, b], recv.at[t, b], dp_of(y, x, 1 - core), z
+            )
+
+        def wide(t, j):
+            if chunks[t][3] == 0:
+                block, to = (1 - y) * 2 + j, (1 - y, x)
+            else:
+                block, to = j * 2 + 1 - x, (y, 1 - x)
+            return remote(
+                buffers[t][0].at[block], buffers[t][2].at[j], send.at[t, 4 + j], recv.at[t, 4 + j], dp_of(to[0], to[1], core), z
+            )
+
+        def narrow(t):
+            block, to = (y * 2 + 1 - x, (y, 1 - x)) if chunks[t][3] == 0 else ((1 - y) * 2 + x, (1 - y, x))
+            return remote(
+                buffers[t][0].at[block], buffers[t][3], send.at[t, 6], recv.at[t, 6], dp_of(to[0], to[1], core), z
+            )
+
+        def along_z(t, k):
+            z_to = lax.rem(z + k, zs)
+            return remote(buffers[t][4].at[z_to], buffers[t][5].at[k - 1], send.at[t, 6 + k], recv.at[t, 6 + k], dp, z_to)
+
+        def add_into(target, other):
+            total, width = target.shape
+
+            def some(r, _):
+                at = pl.ds(pl.multiple_of(r * 32, 32), 32)
+                target[at, :] = (target[at, :].astype(FLOAT) + other[at, :].astype(FLOAT)).astype(BRAIN)
+                return 0
+
+            lax.fori_loop(0, total // 32, some, 0)
+
+        def begin(t):
+            for b in range(4):
+                to_core(t, b).start()
+                load(t, b).start()
+
+        def first(t):
+            for b in range(4):
+                load(t, b).wait()
+                to_core(t, b).wait_recv()
+                add_into(buffers[t][0].at[b], buffers[t][1].at[b])
+            for j in range(2):
+                wide(t, j).start()
+
+        def second(t):
+            for j in range(2):
+                wide(t, j).wait_recv()
+                block = y * 2 + j if chunks[t][3] == 0 else j * 2 + x
+                add_into(buffers[t][0].at[block], buffers[t][2].at[j])
+            narrow(t).start()
+
+        def third(t):
+            narrow(t).wait_recv()
+            r = rows[chunks[t][0]]
+            for s in range(zs):
+                at = pl.ds(s * r, r)
+                mine = buffers[t][0][y * 2 + x, at, :].astype(FLOAT)
+                buffers[t][4][s] = (mine + buffers[t][3][at, :].astype(FLOAT)).astype(BRAIN)
+            for k in range(1, zs):
+                along_z(t, k).start()
+
+        def finish(t):
+            i, at, width, _ = chunks[t]
+            total = buffers[t][4][z].astype(FLOAT)
+            for k in range(1, zs):
+                along_z(t, k).wait_recv()
+                total = total + buffers[t][5][k - 1].astype(FLOAT)
+            outs[i][:, pl.ds(at, width)] = total
+            for b in range(4):
+                to_core(t, b).wait_send()
+            for j in range(2):
+                wide(t, j).wait_send()
+            narrow(t).wait_send()
+            for k in range(1, zs):
+                along_z(t, k).wait_send()
+
+        return staged(count, [(0, begin), (1, first), (2, second), (3, third), (4, finish)])
+
+    shapes = [jax.ShapeDtypeStruct((r, g.shape[1]), FLOAT) for r, g in zip(rows, grads)]
+    out_specs = [pl.BlockSpec(s.shape, lambda *_: (0, 0)) for s in shapes]
+    return inputs, [ANY] * len(grads), shapes, out_specs, scratch, steps
+
+
+def spread_job(tokens, ints=()):
+    zs, count, int_count = lax.axis_size("ctx"), len(tokens), len(ints)
+
+    def steps(ins, outs, scratch):
+        send, recv, local, int_send, int_recv = scratch
+        dp, z, core = place()
+        pair = dp - core
+
+        def swap(i):
+            return remote(ins[count + i], outs[count + i], int_send.at[i], int_recv.at[i], pair + 1 - core, z)
+
+        def each(t, what):
             for i in range(2):
                 for h in range(2):
                     z_to, core_to = 2 * core + i, lax.rem(h + z, 2)
-                    source, target = tokens[t].at[i, pl.ds(h * BLOCK, BLOCK)], outs[t].at[z]
+                    source, target = ins[t].at[i, pl.ds(h * BLOCK, BLOCK)], outs[t].at[z]
                     stays = jnp.logical_and(z_to == z, core_to == core)
 
                     @pl.when(stays)
-                    def _(source=source, target=target, t=t):
+                    def _():
                         what(pltpu.make_async_copy(source, target, local.at[t]), False)
 
                     @pl.when(jnp.logical_not(stays))
-                    def _(source=source, target=target, t=t, i=i, h=h, z_to=z_to, core_to=core_to):
-                        what(
-                            pltpu.make_async_remote_copy(
-                                source,
-                                target,
-                                send.at[t, 2 * i + h],
-                                recv.at[t, z],
-                                device_id=(pair + core_to, z_to),
-                                device_id_type=MESH_ID,
-                            ),
-                            True,
-                        )
-
-    each(lambda copy, remote: copy.start())
-    each(lambda copy, remote: copy.wait_send() if remote else copy.wait())
-    for t in range(token_count):
-        for s in range(zs):
-            @pl.when(jnp.logical_not(jnp.logical_and(s == z, z // 2 == core)))
-            def _(t=t, s=s):
-                pltpu.make_async_remote_copy(
-                    outs[t].at[s], outs[t].at[s], send.at[t, 0], recv.at[t, s], device_id=sibling, device_id_type=MESH_ID
-                ).wait_recv()
-    for copy in int_copies:
-        copy.wait()
-
-
-def spread(tokens, ints, collective_id):
-    zs, count = lax.axis_size("ctx"), len(tokens)
+                    def _():
+                        what(remote(source, target, send.at[t, 2 * i + h], recv.at[t, z], pair + core_to, z_to), True)
+
+        def begin(t):
+            if t == 0:
+                for i in range(int_count):
+                    swap(i).start()
+            each(t, lambda copy, far: copy.start())
+
+        def finish(t):
+            each(t, lambda copy, far: copy.wait_send() if far else copy.wait())
+            for s in range(zs):
+
+                @pl.when(jnp.logical_not(jnp.logical_and(s == z, z // 2 == core)))
+                def _():
+                    remote(outs[t].at[s], outs[t].at[s], send.at[t, 0], recv.at[t, s], pair + 1 - core, z).wait_recv()
+
+            if t == 0:
+                for i in range(int_count):
+                    swap(i).wait()
+
+        return [functools.partial(begin, t) for t in range(count)] + [functools.partial(finish, t) for t in range(count)]
+
     shapes = [jax.ShapeDtypeStruct((zs, BLOCK, D), t.dtype) for t in tokens]
     shapes += [jax.ShapeDtypeStruct(i.shape, i.dtype) for i in ints]
-    got = pl.pallas_call(
-        functools.partial(spread_kernel, count, zs),
-        out_shape=shapes,
-        in_specs=[ANY] * (count + 2),
-        out_specs=[ANY] * (count + 2),
-        scratch_shapes=[DMA_SEM((count, 4)), DMA_SEM((count, zs)), DMA_SEM((count,)), DMA_SEM((2,)), DMA_SEM((2,))],
-        compiler_params=pltpu.CompilerParams(collective_id=collective_id, has_side_effects=True),
-        name="spread_tokens",
-    )(*tokens, *ints)
-    return got[:count], got[count:]
-
-
-def collect_kernel(count, zs, *refs):
-    blocks, outs = refs[:count], refs[count : 2 * count]
-    send, recv, local = refs[2 * count :]
-    dp, z, core = place()
-    pair = dp - core
-    barrier = pltpu.get_barrier_semaphore()
-    for step in range(zs):
-        for other in range(2):
-            if step or other:
-                pl.semaphore_signal(
-                    barrier, 1, device_id=(pair + lax.rem(core + other, 2), lax.rem(z + step, zs)), device_id_type=MESH_ID
-                )
-    pl.semaphore_wait(barrier, 2 * zs - 1)
-    owner, place_in = z // 2, lax.rem(z, 2)
-
-    def each(what):
-        for t in range(count):
+    n = count + int_count
+    scratch = [DMA_SEM((count, 4)), DMA_SEM((count, zs)), DMA_SEM((count,)), DMA_SEM((2,)), DMA_SEM((2,))]
+    return list(tokens) + list(ints), [ANY] * n, shapes, [ANY] * n, scratch, steps
+
+
+def collect_job(blocks):
+    zs, count = lax.axis_size("ctx"), len(blocks)
+
+    def steps(ins, outs, scratch):
+        send, recv, local = scratch
+        dp, z, core = place()
+        pair = dp - core
+        owner, inside = z // 2, lax.rem(z, 2)
+
+        def each(t, what):
             for s in range(zs):
                 half = lax.rem(core + s, 2)
-                source = blocks[t].at[s]
-                target = outs[t].at[place_in, pl.ds(half * BLOCK, BLOCK)]
+                source = ins[t].at[s]
+                target = outs[t].at[inside, pl.ds(half * BLOCK, BLOCK)]
                 stays = jnp.logical_and(s == z, owner == core)
 
                 @pl.when(stays)
-                def _(source=source, target=target, t=t):
+                def _():
                     what(pltpu.make_async_copy(source, target, local.at[t]), False)
 
                 @pl.when(jnp.logical_not(stays))
-                def _(source=source, target=target, t=t, s=s, half=half):
-                    what(
-                        pltpu.make_async_remote_copy(
-                            source,
-                            target,
-                            send.at[t, s],
-                            recv.at[t, 2 * place_in + half],
-                            device_id=(pair + owner, s),
-                            device_id_type=MESH_ID,
-                        ),
-                        True,
-                    )
-
-    each(lambda copy, remote: copy.start())
-    each(lambda copy, remote: copy.wait_send() if remote else copy.wait())
-    for t in range(count):
-        for i in range(2):
-            for h in range(2):
-                z_from, core_from = 2 * core + i, lax.rem(h + z, 2)
-
-                @pl.when(jnp.logical_not(jnp.logical_and(z_from == z, core_from == core)))
-                def _(t=t, i=i, h=h):
-                    target = outs[t].at[i, pl.ds(h * BLOCK, BLOCK)]
-                    pltpu.make_async_remote_copy(
-                        target, target, send.at[t, 0], recv.at[t, 2 * i + h], device_id=(pair + 1 - core, z), device_id_type=MESH_ID
-                    ).wait_recv()
-
-
-def collect(blocks, collective_id):
-    zs, count = lax.axis_size("ctx"), len(blocks)
-    return pl.pallas_call(
-        functools.partial(collect_kernel, count, zs),
-        out_shape=[jax.ShapeDtypeStruct((2, 2 * BLOCK, D), b.dtype) for b in blocks],
-        in_specs=[ANY] * count,
-        out_specs=[ANY] * count,
-        scratch_shapes=[DMA_SEM((count, zs)), DMA_SEM((count, 4)), DMA_SEM((count,))],
-        compiler_params=pltpu.CompilerParams(collective_id=collective_id, has_side_effects=True),
-        name="collect_tokens",
-    )(*blocks)
+                def _():
+                    what(remote(source, target, send.at[t, s], recv.at[t, 2 * inside + half], pair + owner, s), True)
+
+        def begin(t):
+            each(t, lambda copy, far: copy.start())
+
+        def finish(t):
+            each(t, lambda copy, far: copy.wait_send() if far else copy.wait())
+            for i in range(2):
+                for h in range(2):
+                    z_from, core_from = 2 * core + i, lax.rem(h + z, 2)
+
+                    @pl.when(jnp.logical_not(jnp.logical_and(z_from == z, core_from == core)))
+                    def _():
+                        target = outs[t].at[i, pl.ds(h * BLOCK, BLOCK)]
+                        remote(target, target, send.at[t, 0], recv.at[t, 2 * i + h], pair + 1 - core, z).wait_recv()
+
+        return [functools.partial(begin, t) for t in range(count)] + [functools.partial(finish, t) for t in range(count)]
+
+    inputs = [b.reshape(zs, BLOCK, D) for b in blocks]
+    shapes = [jax.ShapeDtypeStruct((2, 2 * BLOCK, D), b.dtype) for b in blocks]
+    scratch = [DMA_SEM((count, zs)), DMA_SEM((count, 4)), DMA_SEM((count,))]
+    return inputs, [ANY] * count, shapes, [ANY] * count, scratch, steps
+
+
+def merge(lists):
+    tagged = []
+    for order, steps in enumerate(lists):
+        tagged += [((k + 0.5) / len(steps), order, k, step) for k, step in enumerate(steps)]
+    return [t[3] for t in sorted(tagged, key=lambda t: t[:3])]
+
+
+def carry(jobs, collective_id, name, kernel=None, grid=1, args=(), in_specs=(), out_shape=(), out_specs=(), scratch=(), cost=None):
+    sizes = [(len(j[0]), len(j[2]), len(j[4])) for j in jobs]
+
+    def body(*refs):
+        def take(n):
+            nonlocal refs
+            got, refs = refs[:n], refs[n:]
+            return list(got)
+
+        mine_in = take(len(args))
+        job_in = [take(s[0]) for s in sizes]
+        mine_out = take(len(out_shape))
+        job_out = [take(s[1]) for s in sizes]
+        mine_scratch = take(len(scratch))
+        job_scratch = [take(s[2]) for s in sizes]
+        steps = merge([j[5](i, o, s) for j, i, o, s in zip(jobs, job_in, job_out, job_scratch)])
+        if kernel is None:
+            greet()
+            for step in steps:
+                step()
+            return
+        turn = pl.program_id(0)
+        for g in range(grid if jobs else 0):
+
+            @pl.when(turn == g)
+            def _():
+                if g == 0:
+                    greet()
+                for step in steps[g * len(steps) // (grid + 1) : (g + 1) * len(steps) // (grid + 1)]:
+                    step()
+
+        kernel(*mine_in, *mine_out, *mine_scratch)
+        if not jobs:
+            return
+
+        @pl.when(turn == grid - 1)
+        def _():
+            for step in steps[grid * len(steps) // (grid + 1) :]:
+                step()
+
+    flat = lambda k: [v for j in jobs for v in j[k]]
+    got = pl.pallas_call(
+        body,
+        grid=(grid,),
+        out_shape=list(out_shape) + flat(2),
+        in_specs=list(in_specs) + flat(1),
+        out_specs=list(out_specs) + flat(3),
+        scratch_shapes=list(scratch) + flat(4),
+        compiler_params=pltpu.CompilerParams(
+            collective_id=collective_id if jobs else None, has_side_effects=bool(jobs), vmem_limit_bytes=60 << 20
+        ),
+        cost_estimate=cost,
+        name=name,
+    )(*args, *flat(0))
+    own, rest, parts = got[: len(out_shape)], got[len(out_shape) :], []
+    for s in sizes:
+        parts.append(rest[: s[1]])
+        rest = rest[s[1] :]
+    return own, parts
+
+
+LOG2E = 1.4426950408889634
 
 
 def key_chunks(rows, causal):
@@ -728,7 +989,7 @@
     return how(how(grouped, axis=0), axis=0, keepdims=True)
 
 
-def attend_fwd_kernel(causal, has_bias, q_ref, k0_ref, v0_ref, k1_ref, v1_ref, bias_ref, o_ref, lse_ref, s_ref, p_ref):
+def attend_fwd_kernel(causal, q_ref, k0_ref, v0_ref, k1_ref, v1_ref, bias_ref, o_ref, lse_ref, s_ref, p_ref):
     rows = q_ref.shape[0]
     k_refs = (k0_ref, k1_ref)
     v_all = jnp.concatenate([v0_ref[...], v1_ref[...]], axis=0)
@@ -759,26 +1020,28 @@
     o_ref[...] = jnp.concatenate(out_t, axis=0).T.astype(o_ref.dtype)
 
 
-def attention_forward(queries, q_col, pairs, kv_col, pairs_other, bias, causal):
+def attention_forward(queries, q_col, pairs, kv_col, pairs_other, bias, causal, jobs=(), collective_id=None):
     rows = queries.shape[0]
     pair_count = D // PAIR
-    q_spec = pl.BlockSpec((rows, PAIR), lambda p: (0, q_col + p))
-    k_spec = pl.BlockSpec((rows, PAIR), lambda p: (0, kv_col + p))
-    v_spec = pl.BlockSpec((rows, PAIR), lambda p: (0, kv_col + pair_count + p))
-    k1_spec = pl.BlockSpec((rows, PAIR), lambda p: (0, p))
-    v1_spec = pl.BlockSpec((rows, PAIR), lambda p: (0, pair_count + p))
-    bias_spec = pl.BlockSpec((2 * rows, rows), lambda p: (0, 0))
-    return pl.pallas_call(
-        functools.partial(attend_fwd_kernel, causal, True),
-        grid=(pair_count,),
+    block = (rows, PAIR)
+    spec = lambda at: pl.BlockSpec(block, lambda p: (0, at + p))
+    own, parts = carry(
+        list(jobs),
+        collective_id,
+        "attend_fwd",
+        kernel=functools.partial(attend_fwd_kernel, causal),
+        grid=pair_count,
+        args=(queries, pairs, pairs, pairs_other, pairs_other, bias),
+        in_specs=[
+            spec(q_col), spec(kv_col), spec(kv_col + pair_count), spec(0), spec(pair_count),
+            pl.BlockSpec((2 * rows, rows), lambda p: (0, 0)),
+        ],
         out_shape=[jax.ShapeDtypeStruct((rows, D), BRAIN), jax.ShapeDtypeStruct((pair_count, 8, rows), FLOAT)],
-        in_specs=[q_spec, k_spec, v_spec, k1_spec, v1_spec, bias_spec],
-        out_specs=[pl.BlockSpec((rows, PAIR), lambda p: (0, p)), pl.BlockSpec((1, 8, rows), lambda p: (p, 0, 0))],
-        scratch_shapes=[pltpu.VMEM((2 * rows, rows), FLOAT), pltpu.VMEM((2 * rows, rows), BRAIN)],
-        compiler_params=pltpu.CompilerParams(vmem_limit_bytes=48 << 20),
-        cost_estimate=pl.CostEstimate(flops=16 * rows * rows * D, bytes_accessed=10 * rows * D * 2, transcendentals=24 * rows * rows),
-        name="attend_fwd",
-    )(queries, pairs, pairs, pairs_other, pairs_other, bias)
+        out_specs=[spec(0), pl.BlockSpec((1, 8, rows), lambda p: (p, 0, 0))],
+        scratch=[pltpu.VMEM((2 * rows, rows), FLOAT), pltpu.VMEM((2 * rows, rows), BRAIN)],
+        cost=pl.CostEstimate(flops=16 * rows * rows * D, bytes_accessed=10 * rows * D * 2, transcendentals=24 * rows * rows),
+    )
+    return own[0], own[1], parts
 
 
 def attend_bwd_kernel(
@@ -819,29 +1082,31 @@
     dq_ref[...] = (jnp.concatenate(dq_t, axis=0) * scale).T.astype(dq_ref.dtype)
 
 
-def attention_backward(queries, q_col, pairs, kv_col, pairs_other, bias, causal, attended, grad_attended, lse):
+def attention_backward(
+    queries, q_col, pairs, kv_col, pairs_other, bias, causal, attended, grad_attended, lse, jobs=(), collective_id=None
+):
     rows = queries.shape[0]
     pair_count = D // PAIR
-    own = lambda p: (0, p)
     block = (rows, PAIR)
-    q_spec = pl.BlockSpec(block, lambda p: (0, q_col + p))
-    k_spec = pl.BlockSpec(block, lambda p: (0, kv_col + p))
-    v_spec = pl.BlockSpec(block, lambda p: (0, kv_col + pair_count + p))
-    k1_spec = pl.BlockSpec(block, own)
-    v1_spec = pl.BlockSpec(block, lambda p: (0, pair_count + p))
-    bias_spec = pl.BlockSpec((2 * rows, rows), lambda p: (0, 0))
-    part = pl.BlockSpec(block, own)
-    return pl.pallas_call(
-        functools.partial(attend_bwd_kernel, causal),
-        grid=(pair_count,),
+    spec = lambda at: pl.BlockSpec(block, lambda p: (0, at + p))
+    own, parts = carry(
+        list(jobs),
+        collective_id,
+        "attend_bwd",
+        kernel=functools.partial(attend_bwd_kernel, causal),
+        grid=pair_count,
+        args=(queries, pairs, pairs, pairs_other, pairs_other, bias, attended, grad_attended, lse),
+        in_specs=[
+            spec(q_col), spec(kv_col), spec(kv_col + pair_count), spec(0), spec(pair_count),
+            pl.BlockSpec((2 * rows, rows), lambda p: (0, 0)), spec(0), spec(0),
+            pl.BlockSpec((1, 8, rows), lambda p: (p, 0, 0)),
+        ],
         out_shape=[jax.ShapeDtypeStruct((rows, D), t) for t in (BRAIN, FLOAT, FLOAT, BRAIN, BRAIN)],
-        in_specs=[q_spec, k_spec, v_spec, k1_spec, v1_spec, bias_spec, part, part, pl.BlockSpec((1, 8, rows), lambda p: (p, 0, 0))],
-        out_specs=[part] * 5,
-        scratch_shapes=[pltpu.VMEM((2, 2 * rows, rows), BRAIN)],
-        compiler_params=pltpu.CompilerParams(vmem_limit_bytes=48 << 20),
-        cost_estimate=pl.CostEstimate(flops=40 * rows * rows * D, bytes_accessed=18 * rows * D * 2, transcendentals=24 * rows * rows),
-        name="attend_bwd",
-    )(queries, pairs, pairs, pairs_other, pairs_other, bias, attended, grad_attended, lse)
+        out_specs=[spec(0)] * 5,
+        scratch=[pltpu.VMEM((2, 2 * rows, rows), BRAIN)],
+        cost=pl.CostEstimate(flops=40 * rows * rows * D, bytes_accessed=18 * rows * D * 2, transcendentals=24 * rows * rows),
+    )
+    return own, parts
 
 
 def to_sibling(values):
@@ -878,33 +1143,13 @@
     return cuts[0], cuts[1], cuts[2], cuts[3], cuts[4].reshape(-1), cuts[5].reshape(-1)
 
 
-def columns(packed, widths):
-    cuts, at = [], 0
-    for width in widths:
-        cuts.append(packed[:, at : at + width])
-        at += width
-    return cuts
-
-
 def with_sibling(own_keys, own_values, other_keys, other_values):
     got = to_sibling(jnp.concatenate([other_keys, other_values], axis=1)).astype(FLOAT)
     return (jnp.concatenate([own_keys, own_values], axis=1) + got).astype(BRAIN)
 
 
-def self_attention_block(tokens, qkv_w, bias_vals, score_bias, causal):
-    zero_row = jnp.zeros((D,), FLOAT)
-    projected = (matmul(tokens, qkv_w) + jnp.concatenate([bias_vals[0], zero_row, bias_vals[1]])).astype(BRAIN)
-    other = to_sibling(projected[:, D:])
-    attended, lse = attention_forward(projected, 0, projected, D // PAIR, other, score_bias, causal)
-    return attended, (projected, other, lse)
-
-
-def self_attention_grad(state, attended, grad_attended, score_bias, causal):
-    projected, other, lse = state
-    dq, dk, dv, dk_other, dv_other = attention_backward(
-        projected, 0, projected, D // PAIR, other, score_bias, causal, attended, grad_attended, lse
-    )
-    return jnp.concatenate([dq, with_sibling(dk, dv, dk_other, dv_other)], axis=1)
+def matrix(gathered):
+    return gathered.reshape(-1, gathered.shape[2])
 
 
 def fast_body(
@@ -913,21 +1158,14 @@
     dec_qkv, dec_out, cross_q, cross_kv, cross_out, dec_up, dec_down, dec_bias, dec_up_bias, dec_gain,
 ):
     dp, z, core = place()
-    axes = ("dp", "ctx")
     small = pack_small(enc_bias, dec_bias, enc_gain, dec_gain, enc_up_bias, dec_up_bias)
-    first_pack = jnp.concatenate([enc_qkv, enc_out, enc_up, small], axis=1)
-    down_pack = jnp.concatenate([enc_down, dec_down], axis=1)
-    last_pack = jnp.concatenate([dec_qkv, dec_out, cross_q, cross_kv, cross_out, dec_up], axis=1)
-    first_widths = [w.shape[1] for w in (enc_qkv, enc_out, enc_up, small)]
-    last_widths = [w.shape[1] for w in (dec_qkv, dec_out, cross_q, cross_kv, cross_out, dec_up)]
-    first_all = lax.all_gather(first_pack, axes, axis=0, tiled=True)
-    down_all = lax.all_gather(down_pack, axes, axis=0, tiled=True)
-    last_all = lax.all_gather(last_pack, axes, axis=0, tiled=True)
-
-    (enc_t, dec_t, enc_c, dec_c), (seg_other, ret_other) = spread([enc_in, dec_in, enc_cot, dec_cot], [segments, retrieved], 0)
+    _, ((enc_t, dec_t, seg_other, ret_other), near) = carry(
+        [spread_job([enc_in, dec_in], [segments, retrieved]), gather_job([enc_qkv, dec_qkv, small, enc_out, dec_out])], 0, "begin"
+    )
+    w_enc_qkv, w_dec_qkv, smalls, w_enc_out, w_dec_out = map(matrix, near)
     zs = enc_t.shape[0]
     rows = zs * BLOCK
-    enc_t, dec_t, enc_c, dec_c = (t.reshape(rows, D) for t in (enc_t, dec_t, enc_c, dec_c))
+    enc_t, dec_t = enc_t.reshape(rows, D), dec_t.reshape(rows, D)
     here = z // 2 == core
     seg = lax.dynamic_index_in_dim(jnp.where(here, segments, seg_other), lax.rem(z, 2), 0, keepdims=False)
     ret = lax.dynamic_index_in_dim(jnp.where(here, retrieved, ret_other), lax.rem(z, 2), 0, keepdims=False)
@@ -939,35 +1177,48 @@
     member = jnp.any(pos_k[:, None, None] == ret_own[None], axis=-1)
     cross_mask = jnp.broadcast_to(jnp.where(member, 0.0, NEG).astype(FLOAT)[:, :, None], (2 * rows, zs, BLOCK)).reshape(2 * rows, rows)
 
-    w_enc_qkv, w_enc_out, w_enc_up, smalls = columns(first_all, first_widths)
     b_enc, b_dec, g_enc, g_dec, enc_ub, dec_ub = unpack_small(smalls)
     eb, db, eg, dg = (v.astype(FLOAT).T for v in (b_enc, b_dec, g_enc, g_dec))
     enc_ub, dec_ub = enc_ub.astype(FLOAT), dec_ub.astype(FLOAT)
-    w_enc_down, w_dec_down = down_all[:, :D], down_all[:, D:]
-    w_dec_qkv, w_dec_out, w_cross_q, w_cross_kv, w_cross_out, w_dec_up = columns(last_all, last_widths)
-
-    e_att, e_state = self_attention_block(enc_t, w_enc_qkv, eb, enc_mask, False)
+    zero_row = jnp.zeros((D,), FLOAT)
+
+    e_proj = (matmul(enc_t, w_enc_qkv) + jnp.concatenate([eb[0], zero_row, eb[1]])).astype(BRAIN)
+    e_other = to_sibling(e_proj[:, D:])
+    d_proj = (matmul(dec_t, w_dec_qkv) + jnp.concatenate([db[0], zero_row, db[1]])).astype(BRAIN)
+    d_other = to_sibling(d_proj[:, D:])
+    e_att, e_lse, (far,) = attention_forward(
+        e_proj, 0, e_proj, D // PAIR, e_other, enc_mask, False, [gather_job([enc_up, enc_down])], 1
+    )
+    w_enc_up, w_enc_down = map(matrix, far)
+    d_att, d_lse, (far,) = attention_forward(
+        d_proj, 0, d_proj, D // PAIR, d_other, dec_mask, True, [gather_job([cross_kv, cross_q, cross_out])], 2
+    )
+    w_cross_kv, w_cross_q, w_cross_out = map(matrix, far)
     e_first, e_sum = project_forward(e_att, enc_t.astype(FLOAT), w_enc_out, eb[2], eg[0], eb[4])
     enc_final, e_ffn = ffn_forward(e_first, w_enc_up, enc_ub, w_enc_down, eb[3], eg[1], eb[5])
     memory = enc_final.astype(BRAIN)
-    zero_row = jnp.zeros((D,), FLOAT)
-    d_att, d_state = self_attention_block(dec_t, w_dec_qkv, db, dec_mask, True)
     d_first, d_sum = project_forward(d_att, dec_t.astype(FLOAT), w_dec_out, db[2], dg[0], db[7])
     first_bf = d_first.astype(BRAIN)
     cross_queries = (matmul(first_bf, w_cross_q) + db[3]).astype(BRAIN)
     mem_pairs = (matmul(memory, w_cross_kv) + jnp.concatenate([zero_row, db[4]])).astype(BRAIN)
     mem_other = to_sibling(mem_pairs)
-    crossed, cross_lse = attention_forward(cross_queries, 0, mem_pairs, 0, mem_other, cross_mask, False)
+    crossed, cross_lse, ((enc_c, dec_c), far) = attention_forward(
+        cross_queries, 0, mem_pairs, 0, mem_other, cross_mask, False, [spread_job([enc_cot, dec_cot]), gather_job([dec_up, dec_down])], 3
+    )
+    enc_c, dec_c = enc_c.reshape(rows, D), dec_c.reshape(rows, D)
+    w_dec_up, w_dec_down = map(matrix, far)
     second, second_sum = project_forward(crossed, d_first, w_cross_out, db[5], dg[1], db[8])
     dec_final, d_ffn = ffn_forward(second, w_dec_up, dec_ub, w_dec_down, db[6], dg[2], db[9])
+    low = lambda *grads: [g.astype(BRAIN) for g in grads]
     grad_second, (g_dec_up, g_dec_ub, g_dec_down, g_db6, g_dg2, g_db9) = ffn_backward(
         dec_c.astype(FLOAT), d_ffn, w_dec_up, w_dec_down, dg[2], db[9]
     )
     grad_first, grad_crossed, (g_cross_out, g_db5, g_dg1, g_db8) = project_backward(
         grad_second, crossed, second_sum, w_cross_out, dg[1], db[8]
     )
-    g_cq, dk, dv, dk_o, dv_o = attention_backward(
-        cross_queries, 0, mem_pairs, 0, mem_other, cross_mask, False, crossed, grad_crossed, cross_lse
+    (g_cq, dk, dv, dk_o, dv_o), ((enc_hidden, dec_hidden), (r_dec_up, r_dec_down)) = attention_backward(
+        cross_queries, 0, mem_pairs, 0, mem_other, cross_mask, False, crossed, grad_crossed, cross_lse,
+        [collect_job([memory, dec_final.astype(BRAIN)]), scatter_job(low(g_dec_up, g_dec_down))], 4,
     )
     own_memory = with_sibling(dk, dv, dk_o, dv_o)
     g_cross_q, g_db3 = matmul_left(first_bf, g_cq), column_sum(g_cq)
@@ -975,14 +1226,22 @@
     memory_grad = matmul_right(own_memory, w_cross_kv)
     g_cross_kv, g_db4 = matmul_left(memory, own_memory), column_sum(own_memory[:, D:])
     grad_dec, grad_d_att, (g_dec_out, g_db2, g_dg0, g_db7) = project_backward(grad_first, d_att, d_sum, w_dec_out, dg[0], db[7])
-    d_slope = self_attention_grad(d_state, d_att, grad_d_att, dec_mask, True)
+    (dq, dk, dv, dk_o, dv_o), ((r_cross_out, r_cross_kv, r_cross_q, r_dec_out),) = attention_backward(
+        d_proj, 0, d_proj, D // PAIR, d_other, dec_mask, True, d_att, grad_d_att, d_lse,
+        [scatter_job(low(g_cross_out, g_cross_kv, g_cross_q, g_dec_out))], 5,
+    )
+    d_slope = jnp.concatenate([dq, with_sibling(dk, dv, dk_o, dv_o)], axis=1)
     grad_dec = grad_dec + matmul_right(d_slope, w_dec_qkv)
     g_dec_qkv, d_slope_sum = matmul_left(dec_t, d_slope), column_sum(d_slope)
     grad_e_first, (g_enc_up, g_enc_ub, g_enc_down, g_eb3, g_eg1, g_eb5) = ffn_backward(
         enc_c.astype(FLOAT) + memory_grad, e_ffn, w_enc_up, w_enc_down, eg[1], eb[5]
     )
     grad_enc, grad_e_att, (g_enc_out, g_eb2, g_eg0, g_eb4) = project_backward(grad_e_first, e_att, e_sum, w_enc_out, eg[0], eb[4])
-    e_slope = self_attention_grad(e_state, e_att, grad_e_att, enc_mask, False)
+    (dq, dk, dv, dk_o, dv_o), ((dec_home,), (r_enc_up, r_enc_down)) = attention_backward(
+        e_proj, 0, e_proj, D // PAIR, e_other, enc_mask, False, e_att, grad_e_att, e_lse,
+        [collect_job(low(grad_dec)), scatter_job(low(g_enc_up, g_enc_down))], 6,
+    )
+    e_slope = jnp.concatenate([dq, with_sibling(dk, dv, dk_o, dv_o)], axis=1)
     grad_enc = grad_enc + matmul_right(e_slope, w_enc_qkv)
     g_enc_qkv, e_slope_sum = matmul_left(enc_t, e_slope), column_sum(e_slope)
 
@@ -992,20 +1251,12 @@
     )
     g_eg, g_dg = jnp.stack([g_eg0, g_eg1], axis=1), jnp.stack([g_dg0, g_dg1, g_dg2], axis=1)
     g_small = pack_small(g_eb, g_db, g_eg, g_dg, g_enc_ub, g_dec_ub)
-    join = lambda parts: jnp.concatenate([p.astype(BRAIN) for p in parts], axis=1)
-    scatter = lambda packed: lax.psum_scatter(packed, axes, scatter_dimension=0, tiled=True).astype(FLOAT)
-    last_sum = scatter(join([g_dec_qkv, g_dec_out, g_cross_q, g_cross_kv, g_cross_out, g_dec_up]))
-    down_sum = scatter(join([g_enc_down, g_dec_down]))
-    first_sum = scatter(join([g_enc_qkv, g_enc_out, g_enc_up, g_small]))
-    r_dec_qkv, r_dec_out, r_cross_q, r_cross_kv, r_cross_out, r_dec_up = columns(last_sum, last_widths)
-    r_enc_down, r_dec_down = columns(down_sum, [D, D])
-    r_enc_qkv, r_enc_out, r_enc_up, r_small = columns(first_sum, first_widths)
+    _, ((enc_home,), (r_dec_qkv, r_enc_out, r_enc_qkv, r_small)) = carry(
+        [collect_job(low(grad_enc)), scatter_job(low(g_dec_qkv, g_enc_out, g_enc_qkv, g_small))], 7, "end"
+    )
     r_eb, r_db, r_eg, r_dg, r_enc_ub, r_dec_ub = unpack_small(r_small)
-    home = collect(
-        [v.astype(BRAIN).reshape(zs, BLOCK, D) for v in (memory, dec_final, grad_enc, grad_dec)], 1
-    )
     return (
-        home[0], home[1], home[2].astype(FLOAT), home[3].astype(FLOAT),
+        enc_hidden, dec_hidden, enc_home.astype(FLOAT), dec_home.astype(FLOAT),
         r_enc_qkv, r_enc_out, r_enc_up, r_enc_down, r_eb, r_enc_ub, r_eg,
         r_dec_qkv, r_dec_out, r_cross_q, r_cross_kv, r_cross_out, r_dec_up, r_dec_down, r_db, r_dec_ub, r_dg,
     )

time: 983 us -> 804 us (0.82)
  waiting for transfers between devices: 316 us -> 0.02 us
  Pallas kernels: 307 us -> 533 us
  local copies, waits for them, and re-layouts: 126 us -> 81.7 us
  matrix products: 167 us -> 146 us
  between operations: 16.3 us -> 2.5 us
    pallas_call x8, Pallas kernels: 307 us -> 533 us  [carry(): pl.pallas_call(body, grid=(grid,), out_shape=list(out_shape) + flat(2), i...]
    reduce_scatter x1 -> x0, waiting for transfers between devices: 156 us -> none  [fast_body(): lax.psum_scatter(packed, axes, scatter_dimension=0, tiled=True)]
    all_gather x3 -> x0, waiting for transfers between devices: 116 us -> none  [the longest x1 76.7 us: fast_body(): down_all = lax.all_gather(down_pack, axes, axis=0, tiled=True)]
    unnamed x8 -> x0, waiting for transfers between devices: 43.8 us -> none
    another operation x22 -> x0, local copies, waits for them, and re-layouts: 21.2 us -> none  [the longest x10 10.5 us: fast_body(): jnp.stack([d_slope_sum[:D], d_slope_sum[2 * D:], g_db2, g_db3, g_db4, g_d...]
    concatenate x3 -> x25, local copies, waits for them, and re-layouts: 21.6 us -> 38.9 us  [pack_small(): return jnp.concatenate(parts, axis=1)]
    unnamed x273 -> x243, local copies, waits for them, and re-layouts: 44.7 us -> 28.1 us
    dot_general x11, matrix products: 71.3 us -> 59.2 us  [matmul(): return jnp.dot(left_side, right_side, preferred_element_type=FLOAT)]
  transfers between devices with their start and end apart: 12 -> 6, of which waited for: 4 -> 0; matrix products, arithmetic and copies ran while one was open for 24% -> 12% of each run, Pallas kernels for 27% -> 7%
where the time goes in v2:
time: 804 us; the launch traced here: 796 us
  Pallas kernels  533 us (66%)
  matrix products  146 us (18%)
  local copies, waits for them, and re-layouts  81.7 us (10%)
  other arithmetic  32.3 us (4%)
    pallas_call x8, Pallas kernels, carry(): pl.pallas_call(body, grid=(grid,), out_shape=list(out_shape) + flat(2), i...  533 us
    dot_general x11, matrix products, matmul(): return jnp.dot(left_side, right_side, preferred_element_type=FLOAT)  59.2 us
    dot_general x11, matrix products, matmul_right(): lax.dot_general(left_side, right_side, (((1,), (1,)), ((), ())), preferre...  48.2 us
    concatenate x25, local copies, waits for them, and re-layouts, pack_small(): return jnp.concatenate(parts, axis=1)  38.9 us
    dot_general x11, matrix products, matmul_left(): lax.dot_general(left_side, right_side, (((0,), (0,)), ((), ())), preferre...  38.2 us
    unnamed x243, local copies, waits for them, and re-layouts  28.1 us
  transfers between devices with their start and end apart: 6, of which 0 were waited for; matrix products, arithmetic and copies ran while one was open for 12% of the time, Pallas kernels for 7%

profile of v2, /device:TPU:0, one launch (start us, length us, event | category | flops | bytes accessed | tf_op | source)
XLA Modules:
  0.0 796.1 jit_solution(1864022497329237540)
XLA Ops:
  5.9 78.0 %begin.1 = (bf16[4,128,768]{2,1,0:T(8,128)(2,1)}, bf16[4,128,768]{2,1,0:T(8,128)(2,1)}, s32[2,1024]{1,0:T(2,128)}, s32[2,8,512]{2,1,0:T(8,128)}, bf16[32,24,2304...) custom-call(bf16[2,256,768]{2,1,0:T(8,128)(2,1)} %refs_0_.1, ...), custom_call_target="tpu_custom_call" | custom-call | tf_op jit(solution)/shard_map/begin/pallas_call | solution.py:949
  87.5 4.2 fusion.13.refs_0_.refs_1_.refs_2_
  106.6 59.1 %attend_fwd.4 = (bf16[512,768]{1,0:T(8,128)(2,1)}, f32[6,8,512]{2,1,0:T(8,128)}, bf16[32,24,3072]{2,1,0:T(8,128)(2,1)}, bf16[32,96,768]{2,1,0:T(8,128)(2,1)}) custom-call(bf16[512,2304]{1,0:T(8,128)(2,1)} %copy-done, bf16[512,2304]{1,0:T(8,128)(2,1)} %copy-done, bf16[512,2304]{1,0:T(8,128)(2,1)} %copy-done, ...), custom_call_target="tpu_custom_call" | custom-call | flops 3221225472 | bytes 7864320 | tf_op jit(solution)/shard_map/attend_fwd/pallas_call | solution.py:949
  168.3 18.3 %multiply_convert_fusion.1 = (bf16[512,3072]{1,0:T(8,128)(2,1)S(1)}, f32[512,3072]{1,0:T(8,128)}, f32[512,3072]{1,0:T(8,128)}) fusion(f32[3072]{0:T(1024)S(1)} %reshape.554, bf16[768,3072]{1,0:T(8,128)(2,1)S(1)} %bitcast.152, f32[512,768]{1,0:T(8,128)S(1)} %get-tuple-element.281, f32[768]{0:T(1024)S(1)} %get-tuple-element.215, ...), kind=kOutput, calls=%fused_computation.20 | convolution fusion | flops 2521694208 | bytes 22042624 | tf_op jit(solution)/shard_map/dot_general | solution.py:23
  186.7 2.8 fusion.71
  190.2 42.1 %attend_fwd.3 = (bf16[512,768]{1,0:T(8,128)(2,1)}, f32[6,8,512]{2,1,0:T(8,128)}, bf16[32,24,1536]{2,1,0:T(8,128)(2,1)}, bf16[32,24,768]{2,1,0:T(8,128)(2,1)}, bf16[32,24,768]{2,1,0:T(8,128)(2,1)}) custom-call(bf16[512,2304]{1,0:T(8,128)(2,1)} %copy-done.1, bf16[512,2304]{1,0:T(8,128)(2,1)} %copy-done.1, bf16[512,2304]{1,0:T(8,128)(2,1)} %copy-done.1, ...), custom_call_target="tpu_custom_call" | custom-call | flops 3221225472 | bytes 7864320 | tf_op jit(solution)/shard_map/attend_fwd/pallas_call | solution.py:949
  232.3 3.2 fusion.17.refs_1_.refs_2_
  240.9 78.7 %attend_fwd.5 = (bf16[512,768]{1,0:T(8,128)(2,1)}, f32[6,8,512]{2,1,0:T(8,128)}, bf16[4,128,768]{2,1,0:T(8,128)(2,1)}, bf16[4,128,768]{2,1,0:T(8,128)(2,1)}, bf1...) custom-call(bf16[512,768]{1,0:T(8,128)(2,1)} %add_convert_fusion.6.refs_0_, bf16[512,1536]{1,0:T(8,128)(2,1)} %copy-done.80, ...), custom_call_target="tpu_custom_call" | custom-call | flops 3221225472 | bytes 7864320 | tf_op jit(solution)/shard_map/attend_fwd/pallas_call | solution.py:949
  319.6 2.6 fusion.73
  322.6 18.5 %multiply_convert_fusion = (bf16[512,3072]{1,0:T(8,128)(2,1)S(1)}, f32[512,3072]{1,0:T(8,128)}, f32[512,3072]{1,0:T(8,128)}) fusion(f32[3072]{0:T(1024)S(1)} %reshape.556, bf16[768,3072]{1,0:T(8,128)(2,1)S(1)} %bitcast.180, f32[512,768]{1,0:T(8,128)S(1)} %get-tuple-element.288, f32[768]{0:T(1024)S(1)} %get-tuple-element.221, ...), kind=kOutput, calls=%fused_computation.7 | convolution fusion | flops 2521694208 | bytes 22042624 | tf_op jit(solution)/shard_map/dot_general | solution.py:23
  341.1 2.8 fusion.74
  348.7 9.6 %fusion.50 = (bf16[3072]{0:T(1024)(128)(2,1)}, bf16[512,3072]{1,0:T(8,128)(2,1)}) fusion(f32[512,3072]{1,0:T(8,128)} %get-tuple-element.254, f32[512,3072]{1,0:T(8,128)} %get-tuple-element.289, f32[3072]{0:T(1024)S(1)} %reshape.556, bf16[512,768]{1,0:T(8,128)(2,1)S(1)} %get-tuple-element.234, bf16[3072,768]{1,0:T(8,128)(2,1)S(1)} %bitcast.185), kind=kOutput, calls=%fused_computation.200 | convolution fusion | flops 2441081856 | bytes 21252096 | tf_op jit(solution)/shard_map/dot_general | solution.py:33
  358.3 5.8 multiply_reduce_fusion
  364.1 4.8 convolution_convert_fusion.5
  368.9 4.4 convolution_convert_fusion.4
  377.3 69.9 %attend_bwd.3 = (bf16[512,768]{1,0:T(8,128)(2,1)}, f32[512,768]{1,0:T(8,128)}, f32[512,768]{1,0:T(8,128)}, bf16[512,768]{1,0:T(8,128)(2,1)}, bf16[512,768]{1,0:T...) custom-call(bf16[512,768]{1,0:T(8,128)(2,1)} %add_convert_fusion.6.r, ...), custom_call_target="tpu_custom_call" | custom-call | flops 8053063680 | bytes 14155776 | tf_op jit(solution)/shard_map/attend_bwd/pallas_call | solution.py:949
  449.3 3.2 multiply_reduce_fusion.1
  457.7 2.8 convolution_convert_fusion.6
  464.3 10.7 %fusion.51 = (bf16[3072]{0:T(1024)(128)(2,1)}, bf16[512,3072]{1,0:T(8,128)(2,1)}) fusion(f32[512,3072]{1,0:T(8,128)} %get-tuple-element.256, f32[512,3072]{1,0:T(8,128)} %get-tuple-element.282, f32[3072]{0:T(1024)S(1)} %reshape.554, bf16[512,768]{1,0:T(8,128)(2,1)S(1)} %get-tuple-element.240, bf16[3072,768]{1,0:T(8,128)(2,1)} %bitcast.156), kind=kOutput, calls=%fused_computation.201 | convolution fusion | flops 2441081856 | bytes 21252096 | tf_op jit(solution)/shard_map/dot_general | solution.py:33
  475.1 5.7 multiply_reduce_fusion.3
  488.1 56.8 %attend_bwd.4 = (bf16[512,768]{1,0:T(8,128)(2,1)}, f32[512,768]{1,0:T(8,128)}, f32[512,768]{1,0:T(8,128)}, bf16[512,768]{1,0:T(8,128)(2,1)}, bf16[512,768]{1,0:T...) custom-call(bf16[512,2304]{1,0:T(8,128)(2,1)} %copy-done.1, ...), custom_call_target="tpu_custom_call" | custom-call | flops 8053063680 | bytes 14155776 | tf_op jit(solution)/shard_map/attend_bwd/pallas_call | solution.py:949
  549.2 4.3 convolution_convert_fusion.2
  553.5 5.0 convolution_convert_fusion.3
  561.2 2.9 add_convert_fusion.3
  564.1 69.3 %attend_bwd.5 = (bf16[512,768]{1,0:T(8,128)(2,1)}, f32[512,768]{1,0:T(8,128)}, f32[512,768]{1,0:T(8,128)}, bf16[512,768]{1,0:T(8,128)(2,1)}, bf16[512,768]{1,0:T...) custom-call(bf16[512,2304]{1,0:T(8,128)(2,1)} %copy-done, ...), custom_call_target="tpu_custom_call" | custom-call | flops 8053063680 | bytes 14155776 | tf_op jit(solution)/shard_map/attend_bwd/pallas_call | solution.py:949
  633.4 2.7 pad_maximum_fusion.4
  665.0 3.2 convolution_convert_fusion.7
  672.1 3.8 convolution_convert_fusion.1
  679.1 2.9 add_convert_fusion.2
  683.3 4.2 convolution_convert_fusion
  690.4 6.9 concatenate.130.refs_4_
  697.3 78.8 %end.1 = (bf16[2,256,768]{2,1,0:T(8,128)(2,1)}, f32[24,2304]{1,0:T(8,128)}, f32[24,768]{1,0:T(8,128)}, f32[24,2304]{1,0:T(8,128)}, f32[24,128]{1,0:T(8,128)}) custom-call(bf16[4,128,768]{2,1,0:T(8,128)(2,1)} %bitcast.144, bf16[8,96,2304]{2,1,0:T(8,128)(2,1)} %bitcast.138, bf16[8,96,768]{2,1,0:T(8,128)(2,1)} %bitcast.142, bf16[8,96,2304]{2,1,0:T(8,128)(2,1)} %bitcast.139, ...), custom_call_target="tpu_custom_call" | custom-call | tf_op jit(solution)/shard_map/end/pallas_call | solution.py:949
  (388 shorter events, 125.7 us)
Async XLA Ops:
  87.5 99.2 %copy-start.72 = (f32[768]{0:T(1024)}, f32[768]{0:T(1024)S(1)}, u32[]{:S(2)}) copy-start(f32[768]{0:T(1024)S(1)} %get-tuple-element.215) | copy-start | bytes 9220
  93.0 13.6 %collective-permute-start.1 = (bf16[512,1536]{1,0:T(8,128)(2,1)}, bf16[512,1536]{1,0:T(8,128)(2,1)}, u32[]{:S(2)}, u32[]{:S(2)}) collective-permute-start(bf16[512,1536]{1,0:T(8,128)(2,1)} %slice.239), channel_id=1, source_target_pairs={{0,4},{4,0},{8,12},{12,8},{16,20},{20,16},{24,28},{28,24},{1,5},{5... | collective-permute-start | bytes 4718600 | tf_op jit(solution)/shard_map/ppermute | solution.py:1114
  97.3 92.8 %collective-permute-start = (bf16[512,1536]{1,0:T(8,128)(2,1)}, bf16[512,1536]{1,0:T(8,128)(2,1)}, u32[]{:S(2)}, u32[]{:S(2)}) collective-permute-start(bf16[512,1536]{1,0:T(8,128)(2,1)} %slice.228), channel_id=1, source_target_pairs={{0,4},{4,0},{8,12},{12,8},{16,20},{20,16},{24,28},{28,24},{1,5},{5... | collective-permute-start | bytes 4718600 | tf_op jit(solution)/shard_map/ppermute | solution.py:1114
  106.6 59.2 %copy-start.82 = (bf16[32,24,768]{2,1,0:T(8,128)(2,1)S(1)}, bf16[32,24,768]{2,1,0:T(8,128)(2,1)}, u32[]{:S(2)}) copy-start(bf16[32,24,768]{2,1,0:T(8,128)(2,1)} %get-tuple-element.86) | copy-start | bytes 3538948
  106.6 59.2 %copy-start.89 = (bf16[4,128,768]{2,1,0:T(8,128)(2,1)S(1)}, bf16[4,128,768]{2,1,0:T(8,128)(2,1)}, u32[]{:S(2)}) copy-start(bf16[4,128,768]{2,1,0:T(8,128)(2,1)} %get-tuple-element.82) | copy-start | bytes 2359300
  165.7 20.9 %slice-start.2 = ((s8[4718592]{0:T(1024)(128)(4,1)}), s8[4194304]{0:T(1024)(128)(4,1)S(1)}, s32[]{:S(2)}) async-start(s8[4718592]{0:T(1024)(128)(4,1)} %bitcast.157), calls=%async_computation.2 | async-start | bytes 8388608
  167.9 18.7 %copy-start.4 = (f32[512,768]{1,0:T(8,128)}, f32[512,768]{1,0:T(8,128)S(1)}, u32[]{:S(2)}) copy-start(f32[512,768]{1,0:T(8,128)S(1)} %get-tuple-element.281) | copy-start | bytes 4718596
  168.2 18.4 %copy-start.64 = (f32[512]{0:T(512)}, f32[512]{0:T(512)S(1)}, u32[]{:S(2)}) copy-start(f32[512]{0:T(512)S(1)} %multiply_reduce_fusion.11) | copy-start | bytes 6148
  168.3 18.4 %slice-start.3 = ((s8[4718592]{0:T(1024)(128)(4,1)}), s8[524288]{0:T(1024)(128)(4,1)S(1)}, s32[]{:S(2)}) async-start(s8[4718592]{0:T(1024)(128)(4,1)} %bitcast.157), calls=%async_computation.3 | async-start | bytes 1048576
  190.1 42.1 %copy-start.40 = (bf16[512,768]{1,0:T(8,128)(2,1)}, bf16[512,768]{1,0:T(8,128)(2,1)S(1)}, u32[]{:S(2)}) copy-start(bf16[512,768]{1,0:T(8,128)(2,1)S(1)} %add_convert_fusion.5) | copy-start | bytes 2359300
  235.5 4.3 collective-permute-start.2
  237.6 82.0 %copy-start.6 = (f32[512,768]{1,0:T(8,128)}, f32[512,768]{1,0:T(8,128)S(1)}, u32[]{:S(2)}) copy-start(f32[512,768]{1,0:T(8,128)S(1)} %get-tuple-element.286) | copy-start | bytes 4718596
  319.6 21.4 %slice-start.4 = ((s8[4718592]{0:T(1024)(128)(4,1)}), s8[4194304]{0:T(1024)(128)(4,1)S(1)}, s32[]{:S(2)}) async-start(s8[4718592]{0:T(1024)(128)(4,1)} %bitcast.182), calls=%async_computation.4 | async-start | bytes 8388608
  322.6 18.5 %slice-start.5 = ((s8[4718592]{0:T(1024)(128)(4,1)}), s8[524288]{0:T(1024)(128)(4,1)S(1)}, s32[]{:S(2)}) async-start(s8[4718592]{0:T(1024)(128)(4,1)} %bitcast.182), calls=%async_computation.5 | async-start | bytes 1048576
  448.9 7.7 collective-permute-start.3
  462.8 12.3 %slice-start = ((s8[4718592]{0:T(1024)(128)(4,1)}), s8[524288]{0:T(1024)(128)(4,1)S(1)}, s32[]{:S(2)}) async-start(s8[4718592]{0:T(1024)(128)(4,1)} %bitcast.153), calls=%async_computation | async-start | bytes 1048576
  464.3 10.7 %copy-start.47 = (bf16[512,768]{1,0:T(8,128)(2,1)}, bf16[512,768]{1,0:T(8,128)(2,1)S(1)}, u32[]{:S(2)}) copy-start(bf16[512,768]{1,0:T(8,128)(2,1)S(1)} %get-tuple-element.240) | copy-start | bytes 2359300
  464.3 10.7 %copy-start.5 = (f32[512,768]{1,0:T(8,128)S(1)}, f32[512,768]{1,0:T(8,128)}, u32[]{:S(2)}) copy-start(f32[512,768]{1,0:T(8,128)} %copy-done.4) | copy-start | bytes 4718596
  464.3 10.7 %slice-start.1 = ((s8[4718592]{0:T(1024)(128)(4,1)}), s8[4194304]{0:T(1024)(128)(4,1)S(1)}, s32[]{:S(2)}) async-start(s8[4718592]{0:T(1024)(128)(4,1)} %bitcast.153), calls=%async_computation.1 | async-start | bytes 8388608
  482.3 64.3 %copy-start.8 = (f32[512,768]{1,0:T(8,128)}, f32[512,768]{1,0:T(8,128)S(1)}, u32[]{:S(2)}) copy-start(f32[512,768]{1,0:T(8,128)S(1)} %get-tuple-element.297) | copy-start | bytes 4718596
  488.1 58.5 %copy-start.69 = (f32[512]{0:T(512)}, f32[512]{0:T(512)S(1)}, u32[]{:S(2)}) copy-start(f32[512]{0:T(512)S(1)} %negate_multiply_fusion.3) | copy-start | bytes 6148
  546.5 11.9 %collective-permute-start.4 = (bf16[512,1536]{1,0:T(8,128)(2,1)S(1)}, bf16[512,1536]{1,0:T(8,128)(2,1)S(1)}, u32[]{:S(2)}, u32[]{:S(2)}) collective-permute-start(bf16[512,1536]{1,0:T(8,128)(2,1)S(1)} %pad_maximum_fusion.3), channel_id=1, source_target_pairs={{0,4},{4,0},{8,12},{12,8},{16,20},{20,16},{24,28},{28,24},{1,5},{5... | collective-permute-start | bytes 4718600 | tf_op jit(solution)/shard_map/ppermute | solution.py:1114
  636.1 39.8 %collective-permute-start.5 = (bf16[512,1536]{1,0:T(8,128)(2,1)}, bf16[512,1536]{1,0:T(8,128)(2,1)}, u32[]{:S(2)}, u32[]{:S(2)}) collective-permute-start(bf16[512,1536]{1,0:T(8,128)(2,1)} %pad_maximum_fusion.4), channel_id=1, source_target_pairs={{0,4},{4,0},{8,12},{12,8},{16,20},{20,16},{24,28},{28,24},{1,5},{5... | collective-permute-start | bytes 4718600 | tf_op jit(solution)/shard_map/ppermute | solution.py:1114
  636.3 15.9 %copy-start.13 = (bf16[512,1536]{1,0:T(8,128)(2,1)S(1)}, bf16[512,1536]{1,0:T(8,128)(2,1)}, u32[]{:S(2)}) copy-start(bf16[512,1536]{1,0:T(8,128)(2,1)} %copy-done.12) | copy-start | bytes 4718596
  637.7 22.6 %copy-start.66 = (bf16[768]{0:T(1024)(128)(2,1)S(1)}, bf16[768]{0:T(1024)(128)(2,1)}, u32[]{:S(2)}) copy-start(bf16[768]{0:T(1024)(128)(2,1)} %get-tuple-element.239) | copy-start | bytes 4612
  637.7 25.3 %copy-start.68 = (bf16[768]{0:T(1024)(128)(2,1)S(1)}, bf16[768]{0:T(1024)(128)(2,1)}, u32[]{:S(2)}) copy-start(bf16[768]{0:T(1024)(128)(2,1)} %get-tuple-element.241) | copy-start | bytes 4612
  638.0 26.0 %copy-start.67 = (bf16[768]{0:T(1024)(128)(2,1)S(1)}, bf16[768]{0:T(1024)(128)(2,1)}, u32[]{:S(2)}) copy-start(bf16[768]{0:T(1024)(128)(2,1)} %get-tuple-element.237) | copy-start | bytes 4612
  660.3 8.0 %copy-start.43 = (bf16[512,768]{1,0:T(8,128)(2,1)S(1)}, bf16[512,768]{1,0:T(8,128)(2,1)}, u32[]{:S(2)}) copy-start(bf16[512,768]{1,0:T(8,128)(2,1)} %get-tuple-element.107) | copy-start | bytes 2359300
  683.2 7.1 copy-start.24
  683.2 7.1 copy-start.25
  776.2 10.3 %copy-start.38 = (bf16[2,256,768]{2,1,0:T(8,128)(2,1)S(1)}, bf16[2,256,768]{2,1,0:T(8,128)(2,1)}, u32[]{:S(2)}) copy-start(bf16[2,256,768]{2,1,0:T(8,128)(2,1)} %get-tuple-element.319) | copy-start | bytes 2359300
  776.2 11.2 %copy-start.37 = (bf16[2,256,768]{2,1,0:T(8,128)(2,1)S(1)}, bf16[2,256,768]{2,1,0:T(8,128)(2,1)}, u32[]{:S(2)}) copy-start(bf16[2,256,768]{2,1,0:T(8,128)(2,1)} %get-tuple-element.320) | copy-start | bytes 2359300
  (84 other events, 314.6 us)

commit v3 on v2

--- a/solution.py
+++ b/solution.py
@@ -599,20 +599,28 @@
     return steps
 
 
-def halves(shapes):
+CHUNK = 24 * 512
+PER_POLL = 4
+LAG = 3
+
+
+def pieces(shapes):
     chunks = []
     for i, (rows, n) in enumerate(shapes):
-        cut = (n // 2) // PAIR * PAIR
-        for order, (at, width) in enumerate(((0, cut), (cut, n - cut))):
-            if width:
-                chunks.append((i, at, width, order))
+        columns = n // PAIR
+        count = max(1, min(columns, -(-rows * n // CHUNK)))
+        at = 0
+        for k in range(count):
+            width = (columns * (k + 1) // count - columns * k // count) * PAIR
+            chunks.append((i, at, width, len(chunks) % 2))
+            at += width
     return chunks
 
 
 def gather_job(shards):
     zs = lax.axis_size("ctx")
     everyone = lax.axis_size("dp") * zs
-    chunks = halves([s.shape for s in shards])
+    chunks = pieces([s.shape for s in shards])
     count = len(chunks)
 
     def steps(ins, outs, scratch):
@@ -677,7 +685,7 @@
             for kind in range(3, 10):
                 hop(t, kind).wait_send()
 
-        return staged(count, [(0, begin), (2, first), (3, second), (4, third), (5, finish)])
+        return staged(count, [(0, begin), (LAG + 1, first), (2 * LAG + 1, second), (3 * LAG + 1, third), (4 * LAG + 1, finish)])
 
     shapes = [jax.ShapeDtypeStruct((everyone,) + s.shape, s.dtype) for s in shards]
     scratch = [DMA_SEM((count, 10)), DMA_SEM((count, 10)), DMA_SEM((count,))]
@@ -687,7 +695,7 @@
 def scatter_job(grads):
     zs, dps = lax.axis_size("ctx"), lax.axis_size("dp")
     rows = [g.shape[0] // (zs * dps) for g in grads]
-    chunks = halves([(r, g.shape[1]) for r, g in zip(rows, grads)])
+    chunks = pieces([(r, g.shape[1]) for r, g in zip(rows, grads)])
     count = len(chunks)
     inputs = [g.reshape(dps, zs * r, g.shape[1]) for r, g in zip(rows, grads)]
     scratch = [DMA_SEM((count, 10)), DMA_SEM((count, 10)), DMA_SEM((count, 4))]
@@ -792,7 +800,7 @@
             for k in range(1, zs):
                 along_z(t, k).wait_send()
 
-        return staged(count, [(0, begin), (1, first), (2, second), (3, third), (4, finish)])
+        return staged(count, [(0, begin), (LAG, first), (2 * LAG, second), (3 * LAG, third), (4 * LAG, finish)])
 
     shapes = [jax.ShapeDtypeStruct((r, g.shape[1]), FLOAT) for r, g in zip(rows, grads)]
     out_specs = [pl.BlockSpec(s.shape, lambda *_: (0, 0)) for s in shapes]
@@ -905,7 +913,9 @@
     return [t[3] for t in sorted(tagged, key=lambda t: t[:3])]
 
 
-def carry(jobs, collective_id, name, kernel=None, grid=1, args=(), in_specs=(), out_shape=(), out_specs=(), scratch=(), cost=None):
+def carry(
+    jobs, collective_id, name, kernel=None, grid=1, slots=1, args=(), in_specs=(), out_shape=(), out_specs=(), scratch=(), cost=None
+):
     sizes = [(len(j[0]), len(j[2]), len(j[4])) for j in jobs]
 
     def body(*refs):
@@ -927,23 +937,37 @@
                 step()
             return
         turn = pl.program_id(0)
-        for g in range(grid if jobs else 0):
-
-            @pl.when(turn == g)
+        calls = grid * slots
+        early = min(len(steps), calls * PER_POLL)
+        called = [0]
+
+        def poll():
+            slot = called[0]
+            called[0] += 1
+            for g in range(grid):
+                k = g * slots + slot
+                some = steps[k * early // calls : (k + 1) * early // calls]
+                if some:
+
+                    @pl.when(turn == g)
+                    def _():
+                        for step in some:
+                            step()
+
+        if jobs:
+
+            @pl.when(turn == 0)
             def _():
-                if g == 0:
-                    greet()
-                for step in steps[g * len(steps) // (grid + 1) : (g + 1) * len(steps) // (grid + 1)]:
+                greet()
+
+        kernel(poll, *mine_in, *mine_out, *mine_scratch)
+        assert called[0] == slots
+        if steps[early:]:
+
+            @pl.when(turn == grid - 1)
+            def _():
+                for step in steps[early:]:
                     step()
-
-        kernel(*mine_in, *mine_out, *mine_scratch)
-        if not jobs:
-            return
-
-        @pl.when(turn == grid - 1)
-        def _():
-            for step in steps[grid * len(steps) // (grid + 1) :]:
-                step()
 
     flat = lambda k: [v for j in jobs for v in j[k]]
     got = pl.pallas_call(
@@ -989,7 +1013,7 @@
     return how(how(grouped, axis=0), axis=0, keepdims=True)
 
 
-def attend_fwd_kernel(causal, q_ref, k0_ref, v0_ref, k1_ref, v1_ref, bias_ref, o_ref, lse_ref, s_ref, p_ref):
+def attend_fwd_kernel(causal, poll, q_ref, k0_ref, v0_ref, k1_ref, v1_ref, bias_ref, o_ref, lse_ref, s_ref, p_ref):
     rows = q_ref.shape[0]
     k_refs = (k0_ref, k1_ref)
     v_all = jnp.concatenate([v0_ref[...], v1_ref[...]], axis=0)
@@ -1006,6 +1030,7 @@
             peak = fold_rows(s, jnp.max)
             peak = jnp.maximum(top[:, c:], peak)
             top = jnp.concatenate([top[:, :c], peak], axis=1) if c else peak
+        poll()
         total = jnp.zeros((1, rows), FLOAT)
         for half, r, n, c in key_chunks(rows, causal):
             p = jnp.exp2(s_ref[pl.ds(half * rows + r, n), c:] - top[:, c:])
@@ -1016,6 +1041,7 @@
                 p_ref[pl.ds(half * rows + r, n), :c] = jnp.zeros((n, c), BRAIN)
         o_t = jnp.dot(v_t[head * HEAD_DIM : (head + 1) * HEAD_DIM], p_ref[...], preferred_element_type=FLOAT)
         out_t.append(o_t / total)
+        poll()
         lse_ref[0, pl.ds(head, 1), :] = top + jnp.log(total) * LOG2E
     o_ref[...] = jnp.concatenate(out_t, axis=0).T.astype(o_ref.dtype)
 
@@ -1031,6 +1057,7 @@
         "attend_fwd",
         kernel=functools.partial(attend_fwd_kernel, causal),
         grid=pair_count,
+        slots=4,
         args=(queries, pairs, pairs, pairs_other, pairs_other, bias),
         in_specs=[
             spec(q_col), spec(kv_col), spec(kv_col + pair_count), spec(0), spec(pair_count),
@@ -1045,7 +1072,7 @@
 
 
 def attend_bwd_kernel(
-    causal, q_ref, k0_ref, v0_ref, k1_ref, v1_ref, bias_ref, o_ref, do_ref, lse_ref,
+    causal, poll, q_ref, k0_ref, v0_ref, k1_ref, v1_ref, bias_ref, o_ref, do_ref, lse_ref,
     dq_ref, dk0_ref, dv0_ref, dk1_ref, dv1_ref, ds_ref,
 ):
     rows = q_ref.shape[0]
@@ -1077,6 +1104,7 @@
             dv = dv_part if dv is None else dv + dv_part
         dk_refs[half][pl.ds(r, n), :] = (dk * scale).astype(dk_refs[half].dtype)
         dv_refs[half][pl.ds(r, n), :] = dv.astype(dv_refs[half].dtype)
+        poll()
     for head in range(2):
         dq_t.append(jnp.dot(k_t[head * HEAD_DIM : (head + 1) * HEAD_DIM], ds_ref[head], preferred_element_type=FLOAT))
     dq_ref[...] = (jnp.concatenate(dq_t, axis=0) * scale).T.astype(dq_ref.dtype)
@@ -1095,6 +1123,7 @@
         "attend_bwd",
         kernel=functools.partial(attend_bwd_kernel, causal),
         grid=pair_count,
+        slots=len(key_chunks(rows, causal)),
         args=(queries, pairs, pairs, pairs_other, pairs_other, bias, attended, grad_attended, lse),
         in_specs=[
             spec(q_col), spec(kv_col), spec(kv_col + pair_count), spec(0), spec(pair_count),
@@ -1127,20 +1156,68 @@
     return own.reshape(-1), jnp.concatenate([own.reshape(-1), other.reshape(-1)])
 
 
+SMALL = 32
+
+
 def pack_small(enc_bias, dec_bias, enc_gain, dec_gain, enc_up_bias, dec_up_bias):
     rows = enc_bias.shape[0]
-    parts = [enc_bias, dec_bias, enc_gain, dec_gain, enc_up_bias.reshape(rows, -1), dec_up_bias.reshape(rows, -1)]
-    width = sum(p.shape[1] for p in parts)
-    parts.append(jnp.zeros((rows, PAIR - width), parts[0].dtype))
-    return jnp.concatenate(parts, axis=1)
-
-
-def unpack_small(packed):
+    parts = [enc_bias, dec_bias, enc_gain, dec_gain]
+    left = jnp.pad(jnp.concatenate(parts, axis=1), ((0, 0), (0, SMALL - sum(p.shape[1] for p in parts))))
+    right = jnp.pad(jnp.stack([enc_up_bias, dec_up_bias]), ((0, rows - 2), (0, PAIR - SMALL - enc_up_bias.shape[0])))
+    return jnp.concatenate([left, right], axis=1)
+
+
+def unpack_small(packed, width):
     cuts, at = [], 0
-    for width in (6, 10, 2, 3, 4, 4):
-        cuts.append(packed[:, at : at + width])
-        at += width
-    return cuts[0], cuts[1], cuts[2], cuts[3], cuts[4].reshape(-1), cuts[5].reshape(-1)
+    for count in (6, 10, 2, 3):
+        cuts.append(packed[..., at : at + count])
+        at += count
+    return cuts + [packed[..., 0, SMALL : SMALL + width], packed[..., 1, SMALL : SMALL + width]]
+
+
+def small_grads(rows, enc_up_bias, dec_up_bias, shards):
+    left = jnp.pad(jnp.concatenate(rows, axis=0), ((0, SMALL - len(rows)), (0, 0))).T.reshape(shards, -1, SMALL)
+    up = jnp.stack([v.reshape(shards, -1) for v in (enc_up_bias, dec_up_bias)], axis=1)
+    right = jnp.pad(up, ((0, 0), (0, left.shape[1] - 2), (0, PAIR - SMALL - up.shape[2])))
+    return jnp.concatenate([left, right], axis=2).reshape(-1, PAIR)
+
+
+def sums(values):
+    return jnp.sum(values, axis=0, keepdims=True, dtype=FLOAT)
+
+
+def norm_grad(grad, summed, gain_row):
+    center = summed - jnp.mean(summed, axis=-1, keepdims=True)
+    inverse = lax.rsqrt(jnp.mean(center * center, axis=-1, keepdims=True) + EPS)
+    unit = center * inverse
+    scaled = grad * gain_row
+    back = scaled - jnp.mean(scaled, axis=-1, keepdims=True) - unit * jnp.mean(scaled * unit, axis=-1, keepdims=True)
+    return inverse * back, sums(grad * unit), sums(grad)
+
+
+def project_grad(grad_norm, attended, summed, out_w, gain_row):
+    grad_summed, grad_gain, grad_shift = norm_grad(grad_norm, summed, gain_row)
+    grad_branch = grad_summed.astype(BRAIN)
+    return (
+        grad_summed,
+        matmul_right(grad_branch, out_w).astype(BRAIN),
+        (matmul_left(attended, grad_branch), sums(grad_branch), grad_gain, grad_shift),
+    )
+
+
+def ffn_grad(grad_norm, retained, up_w, down_w, gain_row):
+    first_bf, lifted, activated, summed = retained
+    grad_summed, grad_gain, grad_shift = norm_grad(grad_norm, summed, gain_row)
+    grad_branch = grad_summed.astype(BRAIN)
+    grad_act = matmul_right(grad_branch, down_w)
+    grad_lifted = jax.vjp(gelu_exact, lifted)[1](grad_act)[0].astype(BRAIN)
+    return (
+        grad_summed + matmul_right(grad_lifted, up_w),
+        (
+            matmul_left(first_bf, grad_lifted), sums(grad_lifted),
+            matmul_left(activated, grad_branch), sums(grad_branch), grad_gain, grad_shift,
+        ),
+    )
 
 
 def with_sibling(own_keys, own_values, other_keys, other_values):
@@ -1162,7 +1239,7 @@
     _, ((enc_t, dec_t, seg_other, ret_other), near) = carry(
         [spread_job([enc_in, dec_in], [segments, retrieved]), gather_job([enc_qkv, dec_qkv, small, enc_out, dec_out])], 0, "begin"
     )
-    w_enc_qkv, w_dec_qkv, smalls, w_enc_out, w_dec_out = map(matrix, near)
+    w_enc_qkv, w_dec_qkv, _, w_enc_out, w_dec_out = map(matrix, near)
     zs = enc_t.shape[0]
     rows = zs * BLOCK
     enc_t, dec_t = enc_t.reshape(rows, D), dec_t.reshape(rows, D)
@@ -1177,14 +1254,16 @@
     member = jnp.any(pos_k[:, None, None] == ret_own[None], axis=-1)
     cross_mask = jnp.broadcast_to(jnp.where(member, 0.0, NEG).astype(FLOAT)[:, :, None], (2 * rows, zs, BLOCK)).reshape(2 * rows, rows)
 
-    b_enc, b_dec, g_enc, g_dec, enc_ub, dec_ub = unpack_small(smalls)
-    eb, db, eg, dg = (v.astype(FLOAT).T for v in (b_enc, b_dec, g_enc, g_dec))
-    enc_ub, dec_ub = enc_ub.astype(FLOAT), dec_ub.astype(FLOAT)
-    zero_row = jnp.zeros((D,), FLOAT)
-
-    e_proj = (matmul(enc_t, w_enc_qkv) + jnp.concatenate([eb[0], zero_row, eb[1]])).astype(BRAIN)
+    shards = near[2].shape[0]
+    b_enc, b_dec, g_enc, g_dec, enc_ub, dec_ub = unpack_small(near[2], enc_up_bias.shape[0])
+    across = lambda v: jnp.swapaxes(v.reshape(D, -1), 0, 1).astype(FLOAT)
+    eb, db, eg, dg = ([row[i : i + 1] for i in range(row.shape[0])] for row in map(across, (b_enc, b_dec, g_enc, g_dec)))
+    enc_ub, dec_ub = (v.reshape(1, -1).astype(FLOAT) for v in (enc_ub, dec_ub))
+    zero_row = jnp.zeros((1, D), FLOAT)
+
+    e_proj = (matmul(enc_t, w_enc_qkv) + jnp.concatenate([eb[0], zero_row, eb[1]], axis=1)).astype(BRAIN)
     e_other = to_sibling(e_proj[:, D:])
-    d_proj = (matmul(dec_t, w_dec_qkv) + jnp.concatenate([db[0], zero_row, db[1]])).astype(BRAIN)
+    d_proj = (matmul(dec_t, w_dec_qkv) + jnp.concatenate([db[0], zero_row, db[1]], axis=1)).astype(BRAIN)
     d_other = to_sibling(d_proj[:, D:])
     e_att, e_lse, (far,) = attention_forward(
         e_proj, 0, e_proj, D // PAIR, e_other, enc_mask, False, [gather_job([enc_up, enc_down])], 1
@@ -1200,7 +1279,7 @@
     d_first, d_sum = project_forward(d_att, dec_t.astype(FLOAT), w_dec_out, db[2], dg[0], db[7])
     first_bf = d_first.astype(BRAIN)
     cross_queries = (matmul(first_bf, w_cross_q) + db[3]).astype(BRAIN)
-    mem_pairs = (matmul(memory, w_cross_kv) + jnp.concatenate([zero_row, db[4]])).astype(BRAIN)
+    mem_pairs = (matmul(memory, w_cross_kv) + jnp.concatenate([zero_row, db[4]], axis=1)).astype(BRAIN)
     mem_other = to_sibling(mem_pairs)
     crossed, cross_lse, ((enc_c, dec_c), far) = attention_forward(
         cross_queries, 0, mem_pairs, 0, mem_other, cross_mask, False, [spread_job([enc_cot, dec_cot]), gather_job([dec_up, dec_down])], 3
@@ -1210,51 +1289,51 @@
     second, second_sum = project_forward(crossed, d_first, w_cross_out, db[5], dg[1], db[8])
     dec_final, d_ffn = ffn_forward(second, w_dec_up, dec_ub, w_dec_down, db[6], dg[2], db[9])
     low = lambda *grads: [g.astype(BRAIN) for g in grads]
-    grad_second, (g_dec_up, g_dec_ub, g_dec_down, g_db6, g_dg2, g_db9) = ffn_backward(
-        dec_c.astype(FLOAT), d_ffn, w_dec_up, w_dec_down, dg[2], db[9]
-    )
-    grad_first, grad_crossed, (g_cross_out, g_db5, g_dg1, g_db8) = project_backward(
-        grad_second, crossed, second_sum, w_cross_out, dg[1], db[8]
+    grad_second, (g_dec_up, g_dec_ub, g_dec_down, g_db6, g_dg2, g_db9) = ffn_grad(
+        dec_c.astype(FLOAT), d_ffn, w_dec_up, w_dec_down, dg[2]
+    )
+    grad_first, grad_crossed, (g_cross_out, g_db5, g_dg1, g_db8) = project_grad(
+        grad_second, crossed, second_sum, w_cross_out, dg[1]
     )
     (g_cq, dk, dv, dk_o, dv_o), ((enc_hidden, dec_hidden), (r_dec_up, r_dec_down)) = attention_backward(
         cross_queries, 0, mem_pairs, 0, mem_other, cross_mask, False, crossed, grad_crossed, cross_lse,
         [collect_job([memory, dec_final.astype(BRAIN)]), scatter_job(low(g_dec_up, g_dec_down))], 4,
     )
     own_memory = with_sibling(dk, dv, dk_o, dv_o)
-    g_cross_q, g_db3 = matmul_left(first_bf, g_cq), column_sum(g_cq)
+    g_cross_q, g_db3 = matmul_left(first_bf, g_cq), sums(g_cq)
     grad_first = grad_first + matmul_right(g_cq, w_cross_q)
     memory_grad = matmul_right(own_memory, w_cross_kv)
-    g_cross_kv, g_db4 = matmul_left(memory, own_memory), column_sum(own_memory[:, D:])
-    grad_dec, grad_d_att, (g_dec_out, g_db2, g_dg0, g_db7) = project_backward(grad_first, d_att, d_sum, w_dec_out, dg[0], db[7])
+    g_cross_kv, g_db4 = matmul_left(memory, own_memory), sums(own_memory[:, D:])
+    grad_dec, grad_d_att, (g_dec_out, g_db2, g_dg0, g_db7) = project_grad(grad_first, d_att, d_sum, w_dec_out, dg[0])
     (dq, dk, dv, dk_o, dv_o), ((r_cross_out, r_cross_kv, r_cross_q, r_dec_out),) = attention_backward(
         d_proj, 0, d_proj, D // PAIR, d_other, dec_mask, True, d_att, grad_d_att, d_lse,
         [scatter_job(low(g_cross_out, g_cross_kv, g_cross_q, g_dec_out))], 5,
     )
     d_slope = jnp.concatenate([dq, with_sibling(dk, dv, dk_o, dv_o)], axis=1)
     grad_dec = grad_dec + matmul_right(d_slope, w_dec_qkv)
-    g_dec_qkv, d_slope_sum = matmul_left(dec_t, d_slope), column_sum(d_slope)
-    grad_e_first, (g_enc_up, g_enc_ub, g_enc_down, g_eb3, g_eg1, g_eb5) = ffn_backward(
-        enc_c.astype(FLOAT) + memory_grad, e_ffn, w_enc_up, w_enc_down, eg[1], eb[5]
-    )
-    grad_enc, grad_e_att, (g_enc_out, g_eb2, g_eg0, g_eb4) = project_backward(grad_e_first, e_att, e_sum, w_enc_out, eg[0], eb[4])
+    g_dec_qkv, d_slope_sum = matmul_left(dec_t, d_slope), sums(d_slope)
+    grad_e_first, (g_enc_up, g_enc_ub, g_enc_down, g_eb3, g_eg1, g_eb5) = ffn_grad(
+        enc_c.astype(FLOAT) + memory_grad, e_ffn, w_enc_up, w_enc_down, eg[1]
+    )
+    grad_enc, grad_e_att, (g_enc_out, g_eb2, g_eg0, g_eb4) = project_grad(grad_e_first, e_att, e_sum, w_enc_out, eg[0])
     (dq, dk, dv, dk_o, dv_o), ((dec_home,), (r_enc_up, r_enc_down)) = attention_backward(
         e_proj, 0, e_proj, D // PAIR, e_other, enc_mask, False, e_att, grad_e_att, e_lse,
         [collect_job(low(grad_dec)), scatter_job(low(g_enc_up, g_enc_down))], 6,
     )
     e_slope = jnp.concatenate([dq, with_sibling(dk, dv, dk_o, dv_o)], axis=1)
     grad_enc = grad_enc + matmul_right(e_slope, w_enc_qkv)
-    g_enc_qkv, e_slope_sum = matmul_left(enc_t, e_slope), column_sum(e_slope)
-
-    g_eb = jnp.stack([e_slope_sum[:D], e_slope_sum[2 * D :], g_eb2, g_eb3, g_eb4, g_eb5], axis=1)
-    g_db = jnp.stack(
-        [d_slope_sum[:D], d_slope_sum[2 * D :], g_db2, g_db3, g_db4, g_db5, g_db6, g_db7, g_db8, g_db9], axis=1
-    )
-    g_eg, g_dg = jnp.stack([g_eg0, g_eg1], axis=1), jnp.stack([g_dg0, g_dg1, g_dg2], axis=1)
-    g_small = pack_small(g_eb, g_db, g_eg, g_dg, g_enc_ub, g_dec_ub)
+    g_enc_qkv, e_slope_sum = matmul_left(enc_t, e_slope), sums(e_slope)
+
+    g_small = small_grads(
+        [e_slope_sum[:, :D], e_slope_sum[:, 2 * D :], g_eb2, g_eb3, g_eb4, g_eb5]
+        + [d_slope_sum[:, :D], d_slope_sum[:, 2 * D :], g_db2, g_db3, g_db4, g_db5, g_db6, g_db7, g_db8, g_db9]
+        + [g_eg0, g_eg1, g_dg0, g_dg1, g_dg2],
+        g_enc_ub, g_dec_ub, shards,
+    )
     _, ((enc_home,), (r_dec_qkv, r_enc_out, r_enc_qkv, r_small)) = carry(
         [collect_job(low(grad_enc)), scatter_job(low(g_dec_qkv, g_enc_out, g_enc_qkv, g_small))], 7, "end"
     )
-    r_eb, r_db, r_eg, r_dg, r_enc_ub, r_dec_ub = unpack_small(r_small)
+    r_eb, r_db, r_eg, r_dg, r_enc_ub, r_dec_ub = unpack_small(r_small, enc_up_bias.shape[0])
     return (
         enc_hidden, dec_hidden, enc_home.astype(FLOAT), dec_home.astype(FLOAT),
         r_enc_qkv, r_enc_out, r_enc_up, r_enc_down, r_eb, r_enc_ub, r_eg,

time: 804 us -> 717 us (0.89)
  local copies, waits for them, and re-layouts: 81.7 us -> 41.5 us
  Pallas kernels: 533 us -> 495 us
    concatenate x26 -> x3, local copies, waits for them, and re-layouts: 38.9 us -> 0.17 us  [the longest x1 0.14 us: small_grads(): jnp.concatenate(rows, axis=0)]
    pallas_call x8, Pallas kernels: 533 us -> 495 us  [carry(): pl.pallas_call(body, grid=(grid,), out_shape=list(out_shape) + flat(2), i...]
    unnamed x243 -> x201, local copies, waits for them, and re-layouts: 28.1 us -> 30.8 us
  transfers between devices with their start and end apart: 6 -> 6, of which waited for: 0 -> 0; matrix products, arithmetic and copies ran while one was open for 12% -> 10% of each run, Pallas kernels for 7% -> 8%
where the time goes in v3:
time: 717 us; the launch traced here: 710 us
  Pallas kernels  495 us (69%)
  matrix products  138 us (19%)
  local copies, waits for them, and re-layouts  41.5 us (6%)
  other arithmetic  31 us (4%)
    pallas_call x8, Pallas kernels, carry(): pl.pallas_call(body, grid=(grid,), out_shape=list(out_shape) + flat(2), i...  495 us
    dot_general x11, matrix products, matmul(): return jnp.dot(left_side, right_side, preferred_element_type=FLOAT)  60.6 us
    dot_general x11, matrix products, matmul_right(): lax.dot_general(left_side, right_side, (((1,), (1,)), ((), ())), preferre...  41.1 us
    dot_general x11, matrix products, matmul_left(): lax.dot_general(left_side, right_side, (((0,), (0,)), ((), ())), preferre...  36.7 us
    unnamed x201, local copies, waits for them, and re-layouts  30.8 us
  transfers between devices with their start and end apart: 6, of which 0 were waited for; matrix products, arithmetic and copies ran while one was open for 10% of the time, Pallas kernels for 8%

profile of v3, /device:TPU:0, one launch (start us, length us, event | category | flops | bytes accessed | tf_op | source)
XLA Modules:
  0.0 709.7 jit_solution(12987037521239820098)
XLA Ops:
  5.2 79.1 %begin.1 = (bf16[4,128,768]{2,1,0:T(8,128)(2,1)}, bf16[4,128,768]{2,1,0:T(8,128)(2,1)}, s32[2,1024]{1,0:T(2,128)}, s32[2,8,512]{2,1,0:T(8,128)}, bf16[32,24,2304...) custom-call(bf16[2,256,768]{2,1,0:T(8,128)(2,1)} %refs_0_.1, ...), custom_call_target="tpu_custom_call" | custom-call | tf_op jit(solution)/shard_map/begin/pallas_call | solution.py:973
  87.0 4.2 fusion.13.refs_0_.refs_1_.refs_2_
  102.7 56.1 %attend_fwd.4 = (bf16[512,768]{1,0:T(8,128)(2,1)}, f32[6,8,512]{2,1,0:T(8,128)}, bf16[32,24,3072]{2,1,0:T(8,128)(2,1)}, bf16[32,96,768]{2,1,0:T(8,128)(2,1)}) custom-call(bf16[512,2304]{1,0:T(8,128)(2,1)} %copy-done, bf16[512,2304]{1,0:T(8,128)(2,1)} %copy-done, bf16[512,2304]{1,0:T(8,128)(2,1)} %copy-done, ...), custom_call_target="tpu_custom_call" | custom-call | flops 3221225472 | bytes 7864320 | tf_op jit(solution)/shard_map/attend_fwd/pallas_call | solution.py:973
  158.9 2.2 fusion.81
  161.4 18.3 %multiply_convert_fusion.1 = (bf16[512,3072]{1,0:T(8,128)(2,1)S(1)}, f32[512,3072]{1,0:T(8,128)}, f32[512,3072]{1,0:T(8,128)}) fusion(f32[3072]{0:T(1024)S(1)} %reshape.411, bf16[768,3072]{1,0:T(8,128)(2,1)S(1)} %bitcast.180, f32[512,768]{1,0:T(8,128)S(1)} %get-tuple-element.273, f32[768]{0:T(1024)S(1)} %get-tuple-element.293, ...), kind=kOutput, calls=%fused_computation.20 | convolution fusion | flops 2521694208 | bytes 22042624 | tf_op jit(solution)/shard_map/dot_general | solution.py:23
  179.8 2.8 fusion.82
  185.3 37.6 %attend_fwd.3 = (bf16[512,768]{1,0:T(8,128)(2,1)}, f32[6,8,512]{2,1,0:T(8,128)}, bf16[32,24,1536]{2,1,0:T(8,128)(2,1)}, bf16[32,24,768]{2,1,0:T(8,128)(2,1)}, bf16[32,24,768]{2,1,0:T(8,128)(2,1)}) custom-call(bf16[512,2304]{1,0:T(8,128)(2,1)} %copy-done.1, bf16[512,2304]{1,0:T(8,128)(2,1)} %copy-done.1, bf16[512,2304]{1,0:T(8,128)(2,1)} %copy-done.1, ...), custom_call_target="tpu_custom_call" | custom-call | flops 3221225472 | bytes 7864320 | tf_op jit(solution)/shard_map/attend_fwd/pallas_call | solution.py:973
  222.9 4.5 fusion.17.refs_1_.refs_2_
  234.8 79.8 %attend_fwd.5 = (bf16[512,768]{1,0:T(8,128)(2,1)}, f32[6,8,512]{2,1,0:T(8,128)}, bf16[4,128,768]{2,1,0:T(8,128)(2,1)}, bf16[4,128,768]{2,1,0:T(8,128)(2,1)}, bf1...) custom-call(bf16[512,768]{1,0:T(8,128)(2,1)} %add_convert_fusion.6.refs_0_, ...), custom_call_target="tpu_custom_call" | custom-call | flops 3221225472 | bytes 7864320 | tf_op jit(solution)/shard_map/attend_fwd/pallas_call | solution.py:973
  316.2 2.6 fusion.83
  319.2 18.6 %multiply_convert_fusion = (bf16[512,3072]{1,0:T(8,128)(2,1)S(1)}, f32[512,3072]{1,0:T(8,128)}, f32[512,3072]{1,0:T(8,128)}) fusion(f32[3072]{0:T(1024)S(1)} %reshape.412, bf16[768,3072]{1,0:T(8,128)(2,1)S(1)} %bitcast.212, f32[512,768]{1,0:T(8,128)S(1)} %get-tuple-element.278, f32[768]{0:T(1024)S(1)} %get-tuple-element.216, ...), kind=kOutput, calls=%fused_computation.7 | convolution fusion | flops 2521694208 | bytes 22042624 | tf_op jit(solution)/shard_map/dot_general | solution.py:23
  337.7 2.8 fusion.84
  343.9 4.3 convolution_convert_fusion.4
  348.2 8.7 %fusion.85 = (bf16[3072]{0:T(1024)(128)(2,1)S(1)}, bf16[512,3072]{1,0:T(8,128)(2,1)S(1)}) fusion(f32[512,3072]{1,0:T(8,128)} %get-tuple-element.243, bf16[3072,768]{1,0:T(8,128)(2,1)} %bitcast.214, f32[512,768]{1,0:T(8,128)S(1)} %get-tuple-element.233, f32[512,3072]{1,0:T(8,128)} %get-tuple-element.279, f32[3072]{0:T(1024)S(1)} %reshape.412), kind=kOutput, calls=%fused_computation.241 | convolution fusion | flops 2441475072 | bytes 22038528 | tf_op jit(solution)/shard_map/dot_general | solution.py:33
  357.0 3.1 multiply_reduce_fusion
  360.1 4.8 convolution_convert_fusion.5
  368.4 73.9 %attend_bwd.3 = (bf16[512,768]{1,0:T(8,128)(2,1)}, f32[512,768]{1,0:T(8,128)}, f32[512,768]{1,0:T(8,128)}, bf16[512,768]{1,0:T(8,128)(2,1)}, bf16[512,768]{1,0:T...) custom-call(bf16[512,768]{1,0:T(8,128)(2,1)} %add_convert_fusion.6.r, ...), custom_call_target="tpu_custom_call" | custom-call | flops 8053063680 | bytes 14155776 | tf_op jit(solution)/shard_map/attend_bwd/pallas_call | solution.py:973
  442.3 3.8 multiply_reduce_fusion.1
  457.6 2.8 convolution_convert_fusion.6
  463.1 8.3 %fusion.86 = (bf16[3072]{0:T(1024)(128)(2,1)S(1)}, bf16[512,3072]{1,0:T(8,128)(2,1)S(1)}) fusion(f32[512,3072]{1,0:T(8,128)} %get-tuple-element.245, bf16[3072,768]{1,0:T(8,128)(2,1)S(1)} %bitcast.189, f32[512,768]{1,0:T(8,128)S(1)} %get-tuple-element.239, f32[512,3072]{1,0:T(8,128)} %get-tuple-element.274, f32[3072]{0:T(1024)S(1)} %reshape.411), kind=kOutput, calls=%fused_computation.242 | convolution fusion | flops 2441475072 | bytes 22038528 | tf_op jit(solution)/shard_map/dot_general | solution.py:33
  471.5 4.2 multiply_reduce_fusion.3
  475.6 46.4 %attend_bwd.4 = (bf16[512,768]{1,0:T(8,128)(2,1)}, f32[512,768]{1,0:T(8,128)}, f32[512,768]{1,0:T(8,128)}, bf16[512,768]{1,0:T(8,128)(2,1)}, bf16[512,768]{1,0:T...) custom-call(bf16[512,2304]{1,0:T(8,128)(2,1)} %copy-done.1, ...), custom_call_target="tpu_custom_call" | custom-call | flops 8053063680 | bytes 14155776 | tf_op jit(solution)/shard_map/attend_bwd/pallas_call | solution.py:973
  527.5 4.3 convolution_convert_fusion.2
  531.8 5.2 convolution_convert_fusion.3
  540.3 2.9 add_convert_fusion.3
  543.2 64.4 %attend_bwd.5 = (bf16[512,768]{1,0:T(8,128)(2,1)}, f32[512,768]{1,0:T(8,128)}, f32[512,768]{1,0:T(8,128)}, bf16[512,768]{1,0:T(8,128)(2,1)}, bf16[512,768]{1,0:T...) custom-call(bf16[512,2304]{1,0:T(8,128)(2,1)} %copy-done, ...), custom_call_target="tpu_custom_call" | custom-call | flops 8053063680 | bytes 14155776 | tf_op jit(solution)/shard_map/attend_bwd/pallas_call | solution.py:973
  607.6 2.6 pad_maximum_fusion.4
  617.3 3.8 convolution_convert_fusion.1
  623.8 2.9 add_convert_fusion.2
  627.8 3.9 convolution_convert_fusion
  632.9 57.6 %end.1 = (bf16[2,256,768]{2,1,0:T(8,128)(2,1)}, f32[24,2304]{1,0:T(8,128)}, f32[24,768]{1,0:T(8,128)}, f32[24,2304]{1,0:T(8,128)}, f32[24,128]{1,0:T(8,128)}) custom-call(bf16[4,128,768]{2,1,0:T(8,128)(2,1)} %bitcast.163, bf16[8,96,2304]{2,1,0:T(8,128)(2,1)} %bitcast.156, bf16[8,96,768]{2,1,0:T(8,128)(2,1)} %bitcast.155, bf16[8,96,2304]{2,1,0:T(8,128)(2,1)} %bitcast.157, ...), custom_call_target="tpu_custom_call" | custom-call | tf_op jit(solution)/shard_map/end/pallas_call | solution.py:973
  697.6 2.4 convert_element_type.323
  (350 shorter events, 88.2 us)
Async XLA Ops:
  86.9 92.9 %copy-start.55 = (f32[768]{0:T(1024)}, f32[768]{0:T(1024)S(1)}, u32[]{:S(2)}) copy-start(f32[768]{0:T(1024)S(1)} %get-tuple-element.293) | copy-start | bytes 9220
  87.0 5.8 copy-start.60
  92.4 10.3 %collective-permute-start.1 = (bf16[512,1536]{1,0:T(8,128)(2,1)}, bf16[512,1536]{1,0:T(8,128)(2,1)}, u32[]{:S(2)}, u32[]{:S(2)}) collective-permute-start(bf16[512,1536]{1,0:T(8,128)(2,1)} %slice.207), channel_id=1, source_target_pairs={{0,4},{4,0},{8,12},{12,8},{16,20},{20,16},{24,28},{28,24},{1,5},{5... | collective-permute-start | bytes 4718600 | tf_op jit(solution)/shard_map/ppermute | solution.py:1143
  96.8 87.3 %collective-permute-start = (bf16[512,1536]{1,0:T(8,128)(2,1)}, bf16[512,1536]{1,0:T(8,128)(2,1)S(1)}, u32[]{:S(2)}, u32[]{:S(2)}) collective-permute-start(bf16[512,1536]{1,0:T(8,128)(2,1)} %slice.198), channel_id=1, source_target_pairs={{0,4},{4,0},{8,12},{12,8},{16,20},{20,16},{24,28},{28,24},{1,5},{5... | collective-permute-start | bytes 4718600 | tf_op jit(solution)/shard_map/ppermute | solution.py:1143
  102.7 56.1 %copy-start.63 = (bf16[32,24,768]{2,1,0:T(8,128)(2,1)S(1)}, bf16[32,24,768]{2,1,0:T(8,128)(2,1)}, u32[]{:S(2)}) copy-start(bf16[32,24,768]{2,1,0:T(8,128)(2,1)} %get-tuple-element.86) | copy-start | bytes 3538948
  102.7 56.1 %copy-start.70 = (bf16[4,128,768]{2,1,0:T(8,128)(2,1)S(1)}, bf16[4,128,768]{2,1,0:T(8,128)(2,1)}, u32[]{:S(2)}) copy-start(bf16[4,128,768]{2,1,0:T(8,128)(2,1)} %get-tuple-element.82) | copy-start | bytes 2359300
  158.9 20.9 %slice-start.2 = ((s8[4718592]{0:T(1024)(128)(4,1)}), s8[4194304]{0:T(1024)(128)(4,1)S(1)}, s32[]{:S(2)}) async-start(s8[4718592]{0:T(1024)(128)(4,1)} %bitcast.184), calls=%async_computation.2 | async-start | bytes 8388608
  161.0 18.8 %copy-start.8 = (f32[512,768]{1,0:T(8,128)}, f32[512,768]{1,0:T(8,128)S(1)}, u32[]{:S(2)}) copy-start(f32[512,768]{1,0:T(8,128)S(1)} %get-tuple-element.273) | copy-start | bytes 4718596
  161.4 18.4 %slice-start.3 = ((s8[4718592]{0:T(1024)(128)(4,1)}), s8[524288]{0:T(1024)(128)(4,1)S(1)}, s32[]{:S(2)}) async-start(s8[4718592]{0:T(1024)(128)(4,1)} %bitcast.184), calls=%async_computation.3 | async-start | bytes 1048576
  227.4 7.4 %collective-permute-start.2 = (bf16[512,1536]{1,0:T(8,128)(2,1)}, bf16[512,1536]{1,0:T(8,128)(2,1)}, u32[]{:S(2)}, u32[]{:S(2)}) collective-permute-start(bf16[512,1536]{1,0:T(8,128)(2,1)} %fusion.17.refs_1_.refs_2_), channel_id=1, source_target_pairs={{0,4},{4,0},{8,12},{12,8},{16,20},{20,16},{24,28},{28,24},{1,5},{5... | collective-permute-start | bytes 4718600 | tf_op jit(solution)/shard_map/ppermute | solution.py:1143
  232.6 83.6 %copy-start.11 = (f32[512,768]{1,0:T(8,128)}, f32[512,768]{1,0:T(8,128)S(1)}, u32[]{:S(2)}) copy-start(f32[512,768]{1,0:T(8,128)S(1)} %get-tuple-element.271) | copy-start | bytes 4718596
  316.2 21.6 %slice-start.8 = ((s8[4718592]{0:T(1024)(128)(4,1)}), s8[4194304]{0:T(1024)(128)(4,1)S(1)}, s32[]{:S(2)}) async-start(s8[4718592]{0:T(1024)(128)(4,1)} %bitcast.215), calls=%async_computation.8 | async-start | bytes 8388608
  319.2 18.6 %slice-start.9 = ((s8[4718592]{0:T(1024)(128)(4,1)}), s8[524288]{0:T(1024)(128)(4,1)S(1)}, s32[]{:S(2)}) async-start(s8[4718592]{0:T(1024)(128)(4,1)} %bitcast.215), calls=%async_computation.9 | async-start | bytes 1048576
  446.3 10.2 %collective-permute-start.3 = (bf16[512,1536]{1,0:T(8,128)(2,1)S(1)}, bf16[512,1536]{1,0:T(8,128)(2,1)S(1)}, u32[]{:S(2)}, u32[]{:S(2)}) collective-permute-start(bf16[512,1536]{1,0:T(8,128)(2,1)S(1)} %pad_maximum_fusion.2), channel_id=1, source_target_pairs={{0,4},{4,0},{8,12},{12,8},{16,20},{20,16},{24,28},{28,24},{1,5},{5... | collective-permute-start | bytes 4718600 | tf_op jit(solution)/shard_map/ppermute | solution.py:1143
  457.6 5.4 slice-start.4
  462.4 9.1 %slice-start = ((s8[4718592]{0:T(1024)(128)(4,1)}), s8[524288]{0:T(1024)(128)(4,1)S(1)}, s32[]{:S(2)}) async-start(s8[4718592]{0:T(1024)(128)(4,1)} %bitcast.181), calls=%async_computation | async-start | bytes 1048576
  463.0 8.4 %copy-start.20 = (f32[512,768]{1,0:T(8,128)}, f32[512,768]{1,0:T(8,128)S(1)}, u32[]{:S(2)}) copy-start(f32[512,768]{1,0:T(8,128)S(1)} %get-tuple-element.239) | copy-start | bytes 4718596
  463.0 8.4 %copy-start.9 = (f32[512,768]{1,0:T(8,128)S(1)}, f32[512,768]{1,0:T(8,128)}, u32[]{:S(2)}) copy-start(f32[512,768]{1,0:T(8,128)} %copy-done.8) | copy-start | bytes 4718596
  463.1 8.4 %slice-start.1 = ((s8[4718592]{0:T(1024)(128)(4,1)}), s8[4194304]{0:T(1024)(128)(4,1)S(1)}, s32[]{:S(2)}) async-start(s8[4718592]{0:T(1024)(128)(4,1)} %bitcast.181), calls=%async_computation.1 | async-start | bytes 8388608
  523.7 13.2 %collective-permute-start.4 = (bf16[512,1536]{1,0:T(8,128)(2,1)S(1)}, bf16[512,1536]{1,0:T(8,128)(2,1)S(1)}, u32[]{:S(2)}, u32[]{:S(2)}) collective-permute-start(bf16[512,1536]{1,0:T(8,128)(2,1)S(1)} %pad_maximum_fusion.3), channel_id=1, source_target_pairs={{0,4},{4,0},{8,12},{12,8},{16,20},{20,16},{24,28},{28,24},{1,5},{5... | collective-permute-start | bytes 4718600 | tf_op jit(solution)/shard_map/ppermute | solution.py:1143
  531.8 5.2 copy-start.24
  531.8 5.2 copy-start.25
  537.3 5.8 copy-start.13
  610.2 10.9 %collective-permute-start.5 = (bf16[512,1536]{1,0:T(8,128)(2,1)}, bf16[512,1536]{1,0:T(8,128)(2,1)}, u32[]{:S(2)}, u32[]{:S(2)}) collective-permute-start(bf16[512,1536]{1,0:T(8,128)(2,1)} %pad_maximum_fusion.4), channel_id=1, source_target_pairs={{0,4},{4,0},{8,12},{12,8},{16,20},{20,16},{24,28},{28,24},{1,5},{5... | collective-permute-start | bytes 4718600 | tf_op jit(solution)/shard_map/ppermute | solution.py:1143
  690.5 9.5 %copy-start.31 = (bf16[2,256,768]{2,1,0:T(8,128)(2,1)S(1)}, bf16[2,256,768]{2,1,0:T(8,128)(2,1)}, u32[]{:S(2)}) copy-start(bf16[2,256,768]{2,1,0:T(8,128)(2,1)} %get-tuple-element.317) | copy-start | bytes 2359300
  690.5 10.4 %copy-start.30 = (bf16[2,256,768]{2,1,0:T(8,128)(2,1)S(1)}, bf16[2,256,768]{2,1,0:T(8,128)(2,1)}, u32[]{:S(2)}) copy-start(bf16[2,256,768]{2,1,0:T(8,128)(2,1)} %get-tuple-element.318) | copy-start | bytes 2359300
  700.0 4.6 copy-start.45
  700.9 5.0 copy-start.50
  700.9 5.6 copy-start.47
  700.9 6.3 copy-start.49
  700.9 6.9 copy-start.42
  701.8 6.7 copy-start.41
  (63 other events, 164.2 us)

commit v4 on v3

--- a/solution.py
+++ b/solution.py
@@ -596,19 +596,20 @@
         for lag, fn in stages:
             if 0 <= turn - lag < count:
                 steps.append(functools.partial(fn, turn - lag))
-    return steps
+    return [(REACH * k / len(steps), step) for k, step in enumerate(steps)]
 
 
 CHUNK = 24 * 512
-PER_POLL = 4
+BIG_CHUNK = 24 * 768
+REACH = 1.0
 LAG = 3
 
 
-def pieces(shapes):
+def pieces(shapes, chunk=None):
     chunks = []
     for i, (rows, n) in enumerate(shapes):
         columns = n // PAIR
-        count = max(1, min(columns, -(-rows * n // CHUNK)))
+        count = max(1, min(columns, -(-rows * n // (chunk or CHUNK))))
         at = 0
         for k in range(count):
             width = (columns * (k + 1) // count - columns * k // count) * PAIR
@@ -617,10 +618,10 @@
     return chunks
 
 
-def gather_job(shards):
+def gather_job(shards, chunk=None):
     zs = lax.axis_size("ctx")
     everyone = lax.axis_size("dp") * zs
-    chunks = pieces([s.shape for s in shards])
+    chunks = pieces([s.shape for s in shards], chunk)
     count = len(chunks)
 
     def steps(ins, outs, scratch):
@@ -631,28 +632,25 @@
             i, at, width, _ = chunks[t]
             return ins[i].at[:, pl.ds(at, width)]
 
-        def rows_of(t, dp_at, z_at=None):
+        def rows_of(t, y_at, x_at, *z_at):
             i, at, width, _ = chunks[t]
-            where = pl.ds(dp_at * zs, zs) if z_at is None else dp_at * zs + z_at
-            return outs[i].at[where, :, pl.ds(at, width)]
+            return outs[i].at[(y_at, x_at, core) + (z_at or (slice(None),)) + (slice(None), pl.ds(at, width))]
 
         def keep(t):
-            return pltpu.make_async_copy(own_part(t), rows_of(t, dp, z), local.at[t])
+            return pltpu.make_async_copy(own_part(t), rows_of(t, y, x, z), local.at[t])
 
         def along_z(t, k):
-            return remote(own_part(t), rows_of(t, dp, z), send.at[t, k - 1], recv.at[t, k - 1], dp, lax.rem(z + k, zs))
+            return remote(own_part(t), rows_of(t, y, x, z), send.at[t, k - 1], recv.at[t, k - 1], dp, lax.rem(z + k, zs))
 
         def hop(t, kind):
-            order = chunks[t][3]
-            near = (y, 1 - x) if order == 0 else (1 - y, x)
-            far = (1 - y, x) if order == 0 else (y, 1 - x)
-            block, to = {
-                3: ((y, x), near), 4: ((y, x), far), 5: (near, far),
-                6: ((y, x), None), 7: (near, None), 8: (far, None), 9: ((1 - y, 1 - x), None),
+            near, far = dp_of(y, 1 - x, core), dp_of(1 - y, x, core)
+            both = rows_of(t, y, slice(None))
+            if chunks[t][3]:
+                near, far, both = far, near, rows_of(t, slice(None), x)
+            part, to = {
+                3: (rows_of(t, y, x), near), 4: (both, far), 5: (rows_of(t, slice(None), slice(None)), dp_of(y, x, 1 - core)),
             }[kind]
-            dp_to = dp_of(y, x, 1 - core) if to is None else dp_of(to[0], to[1], core)
-            part = rows_of(t, dp_of(block[0], block[1], core))
-            return remote(part, part, send.at[t, kind], recv.at[t, kind], dp_to, z)
+            return remote(part, part, send.at[t, kind], recv.at[t, kind], to, z)
 
         def begin(t):
             keep(t).start()
@@ -663,32 +661,27 @@
             keep(t).wait()
             for k in range(1, zs):
                 along_z(t, k).wait_recv()
-            for kind in (3, 4, 6):
-                hop(t, kind).start()
+            hop(t, 3).start()
 
         def second(t):
             hop(t, 3).wait_recv()
-            for kind in (5, 7):
-                hop(t, kind).start()
+            hop(t, 4).start()
 
         def third(t):
             hop(t, 4).wait_recv()
-            hop(t, 8).start()
+            hop(t, 5).start()
+
+        def finish(t):
             hop(t, 5).wait_recv()
-            hop(t, 9).start()
-
-        def finish(t):
-            for kind in range(6, 10):
-                hop(t, kind).wait_recv()
             for k in range(1, zs):
                 along_z(t, k).wait_send()
-            for kind in range(3, 10):
+            for kind in range(3, 6):
                 hop(t, kind).wait_send()
 
         return staged(count, [(0, begin), (LAG + 1, first), (2 * LAG + 1, second), (3 * LAG + 1, third), (4 * LAG + 1, finish)])
 
-    shapes = [jax.ShapeDtypeStruct((everyone,) + s.shape, s.dtype) for s in shards]
-    scratch = [DMA_SEM((count, 10)), DMA_SEM((count, 10)), DMA_SEM((count,))]
+    shapes = [jax.ShapeDtypeStruct((everyone // (4 * zs * 2) * 2, 2, 2, zs) + s.shape, s.dtype) for s in shards]
+    scratch = [DMA_SEM((count, 6)), DMA_SEM((count, 6)), DMA_SEM((count,))]
     return shards, [ANY] * len(shards), shapes, [ANY] * len(shards), scratch, steps
 
 
@@ -697,12 +690,12 @@
     rows = [g.shape[0] // (zs * dps) for g in grads]
     chunks = pieces([(r, g.shape[1]) for r, g in zip(rows, grads)])
     count = len(chunks)
-    inputs = [g.reshape(dps, zs * r, g.shape[1]) for r, g in zip(rows, grads)]
-    scratch = [DMA_SEM((count, 10)), DMA_SEM((count, 10)), DMA_SEM((count, 4))]
+    inputs = [g.reshape(dps // 4, 2, 2, zs * r, g.shape[1]) for r, g in zip(rows, grads)]
+    scratch = [DMA_SEM((count, 6)), DMA_SEM((count, 6)), DMA_SEM((count,))]
     for i, _, width, _ in chunks:
         scratch += [
-            pltpu.VMEM((4, zs * rows[i], width), BRAIN),
-            pltpu.VMEM((4, zs * rows[i], width), BRAIN),
+            pltpu.VMEM((2, 2, zs * rows[i], width), BRAIN),
+            pltpu.VMEM((2, 2, zs * rows[i], width), BRAIN),
             pltpu.VMEM((2, zs * rows[i], width), BRAIN),
             pltpu.VMEM((zs * rows[i], width), BRAIN),
             pltpu.VMEM((zs, rows[i], width), BRAIN),
@@ -714,64 +707,59 @@
         dp, z, core, x, y = spot()
         buffers = [scratch[3 + 6 * t : 9 + 6 * t] for t in range(count)]
 
-        def source(t, dp_at):
+        def source(t, core_at):
             i, at, width, _ = chunks[t]
-            return ins[i].at[dp_at, :, pl.ds(at, width)]
-
-        def load(t, b):
-            return pltpu.make_async_copy(source(t, dp_of(b // 2, b % 2, core)), buffers[t][0].at[b], local.at[t, b])
-
-        def to_core(t, b):
-            return remote(
-                source(t, dp_of(b // 2, b % 2, 1 - core)), buffers[t][1].at[b], send.at[t, b], recv.at[t, b], dp_of(y, x, 1 - core), z
-            )
-
-        def wide(t, j):
+            return ins[i].at[:, :, core_at, :, pl.ds(at, width)]
+
+        def load(t):
+            return pltpu.make_async_copy(source(t, core), buffers[t][0], local.at[t])
+
+        def to_core(t):
+            return remote(source(t, 1 - core), buffers[t][1], send.at[t, 0], recv.at[t, 0], dp_of(y, x, 1 - core), z)
+
+        def wide(t):
             if chunks[t][3] == 0:
-                block, to = (1 - y) * 2 + j, (1 - y, x)
+                part, to = buffers[t][0].at[1 - y], dp_of(1 - y, x, core)
             else:
-                block, to = j * 2 + 1 - x, (y, 1 - x)
-            return remote(
-                buffers[t][0].at[block], buffers[t][2].at[j], send.at[t, 4 + j], recv.at[t, 4 + j], dp_of(to[0], to[1], core), z
-            )
+                part, to = buffers[t][0].at[:, 1 - x], dp_of(y, 1 - x, core)
+            return remote(part, buffers[t][2], send.at[t, 1], recv.at[t, 1], to, z)
 
         def narrow(t):
-            block, to = (y * 2 + 1 - x, (y, 1 - x)) if chunks[t][3] == 0 else ((1 - y) * 2 + x, (1 - y, x))
-            return remote(
-                buffers[t][0].at[block], buffers[t][3], send.at[t, 6], recv.at[t, 6], dp_of(to[0], to[1], core), z
-            )
+            if chunks[t][3] == 0:
+                part, to = buffers[t][0].at[y, 1 - x], dp_of(y, 1 - x, core)
+            else:
+                part, to = buffers[t][0].at[1 - y, x], dp_of(1 - y, x, core)
+            return remote(part, buffers[t][3], send.at[t, 2], recv.at[t, 2], to, z)
 
         def along_z(t, k):
             z_to = lax.rem(z + k, zs)
-            return remote(buffers[t][4].at[z_to], buffers[t][5].at[k - 1], send.at[t, 6 + k], recv.at[t, 6 + k], dp, z_to)
+            return remote(buffers[t][4].at[z_to], buffers[t][5].at[k - 1], send.at[t, 2 + k], recv.at[t, 2 + k], dp, z_to)
 
         def add_into(target, other):
             total, width = target.shape
 
             def some(r, _):
                 at = pl.ds(pl.multiple_of(r * 32, 32), 32)
-                target[at, :] = (target[at, :].astype(FLOAT) + other[at, :].astype(FLOAT)).astype(BRAIN)
+                target[at, :] = target[at, :] + other[at, :]
                 return 0
 
             lax.fori_loop(0, total // 32, some, 0)
 
         def begin(t):
+            to_core(t).start()
+            load(t).start()
+
+        def first(t):
+            load(t).wait()
+            to_core(t).wait_recv()
             for b in range(4):
-                to_core(t, b).start()
-                load(t, b).start()
-
-        def first(t):
-            for b in range(4):
-                load(t, b).wait()
-                to_core(t, b).wait_recv()
-                add_into(buffers[t][0].at[b], buffers[t][1].at[b])
+                add_into(buffers[t][0].at[b // 2, b % 2], buffers[t][1].at[b // 2, b % 2])
+            wide(t).start()
+
+        def second(t):
+            wide(t).wait_recv()
             for j in range(2):
-                wide(t, j).start()
-
-        def second(t):
-            for j in range(2):
-                wide(t, j).wait_recv()
-                block = y * 2 + j if chunks[t][3] == 0 else j * 2 + x
+                block = (y, j) if chunks[t][3] == 0 else (j, x)
                 add_into(buffers[t][0].at[block], buffers[t][2].at[j])
             narrow(t).start()
 
@@ -780,7 +768,7 @@
             r = rows[chunks[t][0]]
             for s in range(zs):
                 at = pl.ds(s * r, r)
-                mine = buffers[t][0][y * 2 + x, at, :].astype(FLOAT)
+                mine = buffers[t][0][y, x, at, :].astype(FLOAT)
                 buffers[t][4][s] = (mine + buffers[t][3][at, :].astype(FLOAT)).astype(BRAIN)
             for k in range(1, zs):
                 along_z(t, k).start()
@@ -792,10 +780,8 @@
                 along_z(t, k).wait_recv()
                 total = total + buffers[t][5][k - 1].astype(FLOAT)
             outs[i][:, pl.ds(at, width)] = total
-            for b in range(4):
-                to_core(t, b).wait_send()
-            for j in range(2):
-                wide(t, j).wait_send()
+            to_core(t).wait_send()
+            wide(t).wait_send()
             narrow(t).wait_send()
             for k in range(1, zs):
                 along_z(t, k).wait_send()
@@ -807,7 +793,7 @@
     return inputs, [ANY] * len(grads), shapes, out_specs, scratch, steps
 
 
-def spread_job(tokens, ints=()):
+def spread_job(tokens, ints=(), start=0.0):
     zs, count, int_count = lax.axis_size("ctx"), len(tokens), len(ints)
 
     def steps(ins, outs, scratch):
@@ -851,7 +837,7 @@
                 for i in range(int_count):
                     swap(i).wait()
 
-        return [functools.partial(begin, t) for t in range(count)] + [functools.partial(finish, t) for t in range(count)]
+        return [(start, functools.partial(begin, t)) for t in range(count)] + [(1.0, functools.partial(finish, t)) for t in range(count)]
 
     shapes = [jax.ShapeDtypeStruct((zs, BLOCK, D), t.dtype) for t in tokens]
     shapes += [jax.ShapeDtypeStruct(i.shape, i.dtype) for i in ints]
@@ -898,7 +884,7 @@
                         target = outs[t].at[i, pl.ds(h * BLOCK, BLOCK)]
                         remote(target, target, send.at[t, 0], recv.at[t, 2 * i + h], pair + 1 - core, z).wait_recv()
 
-        return [functools.partial(begin, t) for t in range(count)] + [functools.partial(finish, t) for t in range(count)]
+        return [(0.0, functools.partial(begin, t)) for t in range(count)] + [(1.0, functools.partial(finish, t)) for t in range(count)]
 
     inputs = [b.reshape(zs, BLOCK, D) for b in blocks]
     shapes = [jax.ShapeDtypeStruct((2, 2 * BLOCK, D), b.dtype) for b in blocks]
@@ -907,10 +893,8 @@
 
 
 def merge(lists):
-    tagged = []
-    for order, steps in enumerate(lists):
-        tagged += [((k + 0.5) / len(steps), order, k, step) for k, step in enumerate(steps)]
-    return [t[3] for t in sorted(tagged, key=lambda t: t[:3])]
+    tagged = [(place, order, k, step) for order, steps in enumerate(lists) for k, (place, step) in enumerate(steps)]
+    return [(t[0], t[3]) for t in sorted(tagged, key=lambda t: t[:3])]
 
 
 def carry(
@@ -933,12 +917,11 @@
         steps = merge([j[5](i, o, s) for j, i, o, s in zip(jobs, job_in, job_out, job_scratch)])
         if kernel is None:
             greet()
-            for step in steps:
+            for _, step in steps:
                 step()
             return
         turn = pl.program_id(0)
         calls = grid * slots
-        early = min(len(steps), calls * PER_POLL)
         called = [0]
 
         def poll():
@@ -946,7 +929,7 @@
             called[0] += 1
             for g in range(grid):
                 k = g * slots + slot
-                some = steps[k * early // calls : (k + 1) * early // calls]
+                some = [step for at, step in steps if k <= at * calls < k + 1]
                 if some:
 
                     @pl.when(turn == g)
@@ -962,11 +945,12 @@
 
         kernel(poll, *mine_in, *mine_out, *mine_scratch)
         assert called[0] == slots
-        if steps[early:]:
+        last = [step for at, step in steps if at >= 1.0]
+        if last:
 
             @pl.when(turn == grid - 1)
             def _():
-                for step in steps[early:]:
+                for step in last:
                     step()
 
     flat = lambda k: [v for j in jobs for v in j[k]]
@@ -1143,6 +1127,187 @@
     return lax.ppermute(values, "dp", [(i, i ^ 1) for i in range(count)])
 
 
+ERF_TOP = (
+    -2.72614225801306e-10, 2.77068142495902e-08, -2.10102402082508e-06, -5.69250639462346e-05,
+    -7.34990630326855e-04, -2.95459980854025e-03, -1.60960333262415e-02,
+)
+ERF_LOW = (-1.45660718464996e-05, -2.13374055278905e-04, -1.68282697438203e-03, -7.37332916720468e-03, -1.42647390514189e-02)
+FF_TILE = 512
+
+
+def horner(values, factors):
+    total = jnp.full_like(values, factors[0])
+    for factor in factors[1:]:
+        total = total * values + factor
+    return total
+
+
+def gelu_pair(x):
+    arg = jnp.clip(x * 0.7071067811865476, -4.0, 4.0)
+    square = arg * arg
+    below = 0.5 + 0.5 * (arg * horner(square, ERF_TOP) / horner(square, ERF_LOW))
+    return x * below, below + x * (0.3989422804014327 * jnp.exp(-0.5 * x * x))
+
+
+def tn_dot(a, b):
+    return lax.dot_general(a, b, (((0,), (0,)), ((), ())), preferred_element_type=FLOAT)
+
+
+def ffn_end(residual, branch, gain, shift):
+    summed = residual + branch
+    return summed, layer_norm(summed, gain, shift)
+
+
+def ffn_fwd_kernel(
+    tiles, poll, first_ref, up_ref, ub_ref, down_ref, db_ref, gain_ref, shift_ref,
+    act_ref, slope_ref, sum_ref, out_ref, acc, low,
+):
+    g = pl.program_id(0)
+
+    @pl.when(g == 0)
+    def _():
+        low[...] = first_ref[...].astype(BRAIN)
+        acc[...] = jnp.zeros_like(acc)
+
+    lifted = jnp.dot(low[...], up_ref[...], preferred_element_type=FLOAT) + ub_ref[...]
+    poll()
+    act, slope = gelu_pair(lifted)
+    act = act.astype(BRAIN)
+    act_ref[...], slope_ref[...] = act, slope.astype(BRAIN)
+    poll()
+    acc[...] += jnp.dot(act, down_ref[...], preferred_element_type=FLOAT)
+    poll()
+
+    @pl.when(g == tiles - 1)
+    def _():
+        summed, final = ffn_end(first_ref[...], acc[...] + db_ref[...], gain_ref[...], shift_ref[...])
+        sum_ref[...] = summed
+        out_ref[...] = final.astype(BRAIN)
+
+
+def ffn_bwd_start(grad, summed, gain, acc, branch, dgain_ref, dshift_ref, ddb_ref):
+    grad_summed, dgain, dshift = norm_grad(grad, summed, gain)
+    acc[...] = grad_summed
+    branch[...] = grad_summed.astype(BRAIN)
+    dgain_ref[...], dshift_ref[...] = dgain, dshift
+    ddb_ref[...] = sums(branch[...])
+
+
+def ffn_bwd_tile(poll, first, up, down, act, slope, branch, acc, dup_ref, dub_ref, ddown_ref):
+    lift = (nt_dot(branch, down) * slope.astype(FLOAT)).astype(BRAIN)
+    dub_ref[...] = sums(lift)
+    poll()
+    ddown_ref[...] = tn_dot(act, branch).astype(BRAIN)
+    poll()
+    dup_ref[...] = tn_dot(first, lift).astype(BRAIN)
+    acc[...] += nt_dot(lift, up)
+    poll()
+
+
+def ffn_bwd_kernel(
+    tiles, poll, first_ref, up_ref, down_ref, gain_ref, grad_ref, act_ref, slope_ref, sum_ref,
+    dfirst_ref, dup_ref, dub_ref, ddown_ref, ddb_ref, dgain_ref, dshift_ref, acc, branch, low,
+):
+    g = pl.program_id(0)
+
+    @pl.when(g == 0)
+    def _():
+        low[...] = first_ref[...].astype(BRAIN)
+        ffn_bwd_start(grad_ref[...], sum_ref[...], gain_ref[...], acc, branch, dgain_ref, dshift_ref, ddb_ref)
+
+    ffn_bwd_tile(
+        poll, low[...], up_ref[...], down_ref[...], act_ref[...], slope_ref[...], branch[...], acc, dup_ref, dub_ref, ddown_ref
+    )
+
+    @pl.when(g == tiles - 1)
+    def _():
+        dfirst_ref[...] = acc[...]
+
+
+def ffn_both_kernel(
+    tiles, poll, first_ref, up_ref, ub_ref, down_ref, db_ref, gain_ref, shift_ref, cot_ref,
+    out_ref, dfirst_ref, dup_ref, dub_ref, ddown_ref, ddb_ref, dgain_ref, dshift_ref, acc, branch, low, act_sc, slope_sc,
+):
+    g = pl.program_id(0)
+
+    @pl.when(g == 0)
+    def _():
+        low[...] = first_ref[...].astype(BRAIN)
+        acc[...] = jnp.zeros_like(acc)
+
+    poll()
+
+    @pl.when(g < tiles)
+    def _():
+        lifted = jnp.dot(low[...], up_ref[...], preferred_element_type=FLOAT) + ub_ref[...]
+        act, slope = gelu_pair(lifted)
+        act = act.astype(BRAIN)
+        act_sc[g], slope_sc[g] = act, slope.astype(BRAIN)
+        acc[...] += jnp.dot(act, down_ref[...], preferred_element_type=FLOAT)
+
+    @pl.when(g == tiles - 1)
+    def _():
+        summed, final = ffn_end(first_ref[...], acc[...] + db_ref[...], gain_ref[...], shift_ref[...])
+        out_ref[...] = final.astype(BRAIN)
+        ffn_bwd_start(cot_ref[...].astype(FLOAT), summed, gain_ref[...], acc, branch, dgain_ref, dshift_ref, ddb_ref)
+
+    poll()
+
+    @pl.when(g >= tiles)
+    def _():
+        ffn_bwd_tile(
+            lambda: None, low[...], up_ref[...], down_ref[...], act_sc[g - tiles], slope_sc[g - tiles], branch[...], acc,
+            dup_ref, dub_ref, ddown_ref,
+        )
+
+    @pl.when(g == 2 * tiles - 1)
+    def _():
+        dfirst_ref[...] = acc[...]
+
+    poll()
+
+
+def ffn_call(mode, jobs, collective_id, first, up, ub, down, db, gain, shift, extra):
+    rows, width = first.shape
+    tiles = up.shape[1] // FF_TILE
+    grid = 2 * tiles if mode == "both" else tiles
+    at = (lambda g: lax.rem(g, tiles)) if mode == "both" else (lambda g: g)
+    late = (lambda g: jnp.maximum(g - tiles, 0)) if mode == "both" else (lambda g: g)
+    whole = lambda r: pl.BlockSpec((r, width), lambda g: (0, 0))
+    column = lambda r, to: pl.BlockSpec((r, FF_TILE), lambda g: (0, to(g)))
+    row = lambda to: pl.BlockSpec((FF_TILE, width), lambda g: (to(g), 0))
+    shape = jax.ShapeDtypeStruct
+    acc, low = pltpu.VMEM((rows, width), FLOAT), pltpu.VMEM((rows, width), BRAIN)
+    up_spec, ub_spec, down_spec = column(width, at), column(1, at), row(at)
+    grad_shapes = [shape((rows, width), FLOAT), shape(up.shape, BRAIN), shape(ub.shape, FLOAT), shape(down.shape, BRAIN)]
+    grad_shapes += [shape((1, width), FLOAT)] * 3
+    grad_specs = [whole(rows), column(width, late), column(1, late), row(late), whole(1), whole(1), whole(1)]
+    if mode == "fwd":
+        kernel, args = ffn_fwd_kernel, (first, up, ub, down, db, gain, shift)
+        in_specs = [whole(rows), up_spec, ub_spec, down_spec, whole(1), whole(1), whole(1)]
+        out_shape = [shape((rows, up.shape[1]), BRAIN)] * 2 + [shape((rows, width), FLOAT), shape((rows, width), BRAIN)]
+        out_specs = [column(rows, at), column(rows, at), whole(rows), whole(rows)]
+        scratch = [acc, low]
+    elif mode == "bwd":
+        grad, act, slope, summed = extra
+        kernel, args = ffn_bwd_kernel, (first, up, down, gain, grad, act, slope, summed)
+        in_specs = [whole(rows), up_spec, down_spec, whole(1), whole(rows), column(rows, at), column(rows, at), whole(rows)]
+        out_shape, out_specs, scratch = grad_shapes, grad_specs, [acc, low, low]
+    else:
+        kernel, args = ffn_both_kernel, (first, up, ub, down, db, gain, shift) + tuple(extra)
+        in_specs = [whole(rows), up_spec, ub_spec, down_spec, whole(1), whole(1), whole(1), whole(rows)]
+        out_shape, out_specs = [shape((rows, width), BRAIN)] + grad_shapes, [whole(rows)] + grad_specs
+        kept = pltpu.VMEM((tiles, rows, FF_TILE), BRAIN)
+        scratch = [acc, low, low, kept, kept]
+    flops = 4 * rows * width * up.shape[1] * {"fwd": 1, "bwd": 2, "both": 3}[mode]
+    return carry(
+        list(jobs), collective_id, "ffn_" + mode,
+        kernel=functools.partial(kernel, tiles), grid=grid, slots=3, args=args, in_specs=in_specs, out_shape=out_shape,
+        out_specs=out_specs, scratch=scratch,
+        cost=pl.CostEstimate(flops=flops, bytes_accessed=4 * width * up.shape[1] + 16 * rows * width, transcendentals=rows * up.shape[1]),
+    )
+
+
 def own_blocks(per_block, core):
     zs = per_block.shape[0] // 2
     both = per_block.reshape((zs, 2) + per_block.shape[1:])
@@ -1205,28 +1370,13 @@
     )
 
 
-def ffn_grad(grad_norm, retained, up_w, down_w, gain_row):
-    first_bf, lifted, activated, summed = retained
-    grad_summed, grad_gain, grad_shift = norm_grad(grad_norm, summed, gain_row)
-    grad_branch = grad_summed.astype(BRAIN)
-    grad_act = matmul_right(grad_branch, down_w)
-    grad_lifted = jax.vjp(gelu_exact, lifted)[1](grad_act)[0].astype(BRAIN)
-    return (
-        grad_summed + matmul_right(grad_lifted, up_w),
-        (
-            matmul_left(first_bf, grad_lifted), sums(grad_lifted),
-            matmul_left(activated, grad_branch), sums(grad_branch), grad_gain, grad_shift,
-        ),
-    )
-
-
 def with_sibling(own_keys, own_values, other_keys, other_values):
     got = to_sibling(jnp.concatenate([other_keys, other_values], axis=1)).astype(FLOAT)
     return (jnp.concatenate([own_keys, own_values], axis=1) + got).astype(BRAIN)
 
 
 def matrix(gathered):
-    return gathered.reshape(-1, gathered.shape[2])
+    return gathered.reshape(-1, gathered.shape[-1])
 
 
 def fast_body(
@@ -1236,13 +1386,17 @@
 ):
     dp, z, core = place()
     small = pack_small(enc_bias, dec_bias, enc_gain, dec_gain, enc_up_bias, dec_up_bias)
-    _, ((enc_t, dec_t, seg_other, ret_other), near) = carry(
-        [spread_job([enc_in, dec_in], [segments, retrieved]), gather_job([enc_qkv, dec_qkv, small, enc_out, dec_out])], 0, "begin"
-    )
-    w_enc_qkv, w_dec_qkv, _, w_enc_out, w_dec_out = map(matrix, near)
+    weights = [enc_qkv, enc_out, small, enc_up, enc_down, dec_qkv, dec_out, cross_kv, cross_q, cross_out, dec_up, dec_down]
+    _, ((enc_t, seg_other, ret_other), near) = carry(
+        [spread_job([enc_in], [segments, retrieved], 0.3), gather_job(weights, BIG_CHUNK)], 0, "begin"
+    )
+    (
+        w_enc_qkv, w_enc_out, _, w_enc_up, w_enc_down, w_dec_qkv,
+        w_dec_out, w_cross_kv, w_cross_q, w_cross_out, w_dec_up, w_dec_down,
+    ) = map(matrix, near)
     zs = enc_t.shape[0]
     rows = zs * BLOCK
-    enc_t, dec_t = enc_t.reshape(rows, D), dec_t.reshape(rows, D)
+    enc_t = enc_t.reshape(rows, D)
     here = z // 2 == core
     seg = lax.dynamic_index_in_dim(jnp.where(here, segments, seg_other), lax.rem(z, 2), 0, keepdims=False)
     ret = lax.dynamic_index_in_dim(jnp.where(here, retrieved, ret_other), lax.rem(z, 2), 0, keepdims=False)
@@ -1254,8 +1408,9 @@
     member = jnp.any(pos_k[:, None, None] == ret_own[None], axis=-1)
     cross_mask = jnp.broadcast_to(jnp.where(member, 0.0, NEG).astype(FLOAT)[:, :, None], (2 * rows, zs, BLOCK)).reshape(2 * rows, rows)
 
-    shards = near[2].shape[0]
-    b_enc, b_dec, g_enc, g_dec, enc_ub, dec_ub = unpack_small(near[2], enc_up_bias.shape[0])
+    near_small = near[2].reshape((-1,) + near[2].shape[-2:])
+    shards = near_small.shape[0]
+    b_enc, b_dec, g_enc, g_dec, enc_ub, dec_ub = unpack_small(near_small, enc_up_bias.shape[0])
     across = lambda v: jnp.swapaxes(v.reshape(D, -1), 0, 1).astype(FLOAT)
     eb, db, eg, dg = ([row[i : i + 1] for i in range(row.shape[0])] for row in map(across, (b_enc, b_dec, g_enc, g_dec)))
     enc_ub, dec_ub = (v.reshape(1, -1).astype(FLOAT) for v in (enc_ub, dec_ub))
@@ -1263,41 +1418,41 @@
 
     e_proj = (matmul(enc_t, w_enc_qkv) + jnp.concatenate([eb[0], zero_row, eb[1]], axis=1)).astype(BRAIN)
     e_other = to_sibling(e_proj[:, D:])
+    e_att, e_lse, ((dec_t,),) = attention_forward(
+        e_proj, 0, e_proj, D // PAIR, e_other, enc_mask, False, [spread_job([dec_in])], 1
+    )
+    dec_t = dec_t.reshape(rows, D)
     d_proj = (matmul(dec_t, w_dec_qkv) + jnp.concatenate([db[0], zero_row, db[1]], axis=1)).astype(BRAIN)
     d_other = to_sibling(d_proj[:, D:])
-    e_att, e_lse, (far,) = attention_forward(
-        e_proj, 0, e_proj, D // PAIR, e_other, enc_mask, False, [gather_job([enc_up, enc_down])], 1
-    )
-    w_enc_up, w_enc_down = map(matrix, far)
-    d_att, d_lse, (far,) = attention_forward(
-        d_proj, 0, d_proj, D // PAIR, d_other, dec_mask, True, [gather_job([cross_kv, cross_q, cross_out])], 2
-    )
-    w_cross_kv, w_cross_q, w_cross_out = map(matrix, far)
+    d_att, d_lse, _ = attention_forward(
+        d_proj, 0, d_proj, D // PAIR, d_other, dec_mask, True
+    )
     e_first, e_sum = project_forward(e_att, enc_t.astype(FLOAT), w_enc_out, eb[2], eg[0], eb[4])
-    enc_final, e_ffn = ffn_forward(e_first, w_enc_up, enc_ub, w_enc_down, eb[3], eg[1], eb[5])
-    memory = enc_final.astype(BRAIN)
+    (e_act, e_slope, e_sum2, memory), ((dec_c,),) = ffn_call(
+        "fwd", [spread_job([dec_cot])], 8, e_first, w_enc_up, enc_ub, w_enc_down, eb[3], eg[1], eb[5], ()
+    )
+    dec_c = dec_c.reshape(rows, D)
     d_first, d_sum = project_forward(d_att, dec_t.astype(FLOAT), w_dec_out, db[2], dg[0], db[7])
     first_bf = d_first.astype(BRAIN)
     cross_queries = (matmul(first_bf, w_cross_q) + db[3]).astype(BRAIN)
     mem_pairs = (matmul(memory, w_cross_kv) + jnp.concatenate([zero_row, db[4]], axis=1)).astype(BRAIN)
     mem_other = to_sibling(mem_pairs)
-    crossed, cross_lse, ((enc_c, dec_c), far) = attention_forward(
-        cross_queries, 0, mem_pairs, 0, mem_other, cross_mask, False, [spread_job([enc_cot, dec_cot]), gather_job([dec_up, dec_down])], 3
-    )
-    enc_c, dec_c = enc_c.reshape(rows, D), dec_c.reshape(rows, D)
-    w_dec_up, w_dec_down = map(matrix, far)
+    crossed, cross_lse, _ = attention_forward(
+        cross_queries, 0, mem_pairs, 0, mem_other, cross_mask, False
+    )
     second, second_sum = project_forward(crossed, d_first, w_cross_out, db[5], dg[1], db[8])
-    dec_final, d_ffn = ffn_forward(second, w_dec_up, dec_ub, w_dec_down, db[6], dg[2], db[9])
     low = lambda *grads: [g.astype(BRAIN) for g in grads]
-    grad_second, (g_dec_up, g_dec_ub, g_dec_down, g_db6, g_dg2, g_db9) = ffn_grad(
-        dec_c.astype(FLOAT), d_ffn, w_dec_up, w_dec_down, dg[2]
-    )
+    (dec_low, grad_second, g_dec_up, g_dec_ub, g_dec_down, g_db6, g_dg2, g_db9), ((enc_c,), (enc_hidden,)) = ffn_call(
+        "both", [spread_job([enc_cot]), collect_job([memory])], 9,
+        second, w_dec_up, dec_ub, w_dec_down, db[6], dg[2], db[9], (dec_c,),
+    )
+    enc_c = enc_c.reshape(rows, D)
     grad_first, grad_crossed, (g_cross_out, g_db5, g_dg1, g_db8) = project_grad(
         grad_second, crossed, second_sum, w_cross_out, dg[1]
     )
-    (g_cq, dk, dv, dk_o, dv_o), ((enc_hidden, dec_hidden), (r_dec_up, r_dec_down)) = attention_backward(
+    (g_cq, dk, dv, dk_o, dv_o), ((dec_hidden,), (r_dec_down,)) = attention_backward(
         cross_queries, 0, mem_pairs, 0, mem_other, cross_mask, False, crossed, grad_crossed, cross_lse,
-        [collect_job([memory, dec_final.astype(BRAIN)]), scatter_job(low(g_dec_up, g_dec_down))], 4,
+        [collect_job([dec_low]), scatter_job(low(g_dec_down))], 4,
     )
     own_memory = with_sibling(dk, dv, dk_o, dv_o)
     g_cross_q, g_db3 = matmul_left(first_bf, g_cq), sums(g_cq)
@@ -1305,24 +1460,25 @@
     memory_grad = matmul_right(own_memory, w_cross_kv)
     g_cross_kv, g_db4 = matmul_left(memory, own_memory), sums(own_memory[:, D:])
     grad_dec, grad_d_att, (g_dec_out, g_db2, g_dg0, g_db7) = project_grad(grad_first, d_att, d_sum, w_dec_out, dg[0])
-    (dq, dk, dv, dk_o, dv_o), ((r_cross_out, r_cross_kv, r_cross_q, r_dec_out),) = attention_backward(
+    (dq, dk, dv, dk_o, dv_o), ((r_dec_up, r_cross_out, r_cross_q),) = attention_backward(
         d_proj, 0, d_proj, D // PAIR, d_other, dec_mask, True, d_att, grad_d_att, d_lse,
-        [scatter_job(low(g_cross_out, g_cross_kv, g_cross_q, g_dec_out))], 5,
+        [scatter_job(low(g_dec_up, g_cross_out, g_cross_q))], 5,
     )
     d_slope = jnp.concatenate([dq, with_sibling(dk, dv, dk_o, dv_o)], axis=1)
     grad_dec = grad_dec + matmul_right(d_slope, w_dec_qkv)
     g_dec_qkv, d_slope_sum = matmul_left(dec_t, d_slope), sums(d_slope)
-    grad_e_first, (g_enc_up, g_enc_ub, g_enc_down, g_eb3, g_eg1, g_eb5) = ffn_grad(
-        enc_c.astype(FLOAT) + memory_grad, e_ffn, w_enc_up, w_enc_down, eg[1]
+    (grad_e_first, g_enc_up, g_enc_ub, g_enc_down, g_eb3, g_eg1, g_eb5), ((dec_home,), (r_cross_kv, r_dec_out, r_dec_qkv)) = ffn_call(
+        "bwd", [collect_job(low(grad_dec)), scatter_job(low(g_cross_kv, g_dec_out, g_dec_qkv))], 10,
+        e_first, w_enc_up, enc_ub, w_enc_down, eb[3], eg[1], eb[5], (enc_c.astype(FLOAT) + memory_grad, e_act, e_slope, e_sum2),
     )
     grad_enc, grad_e_att, (g_enc_out, g_eb2, g_eg0, g_eb4) = project_grad(grad_e_first, e_att, e_sum, w_enc_out, eg[0])
-    (dq, dk, dv, dk_o, dv_o), ((dec_home,), (r_enc_up, r_enc_down)) = attention_backward(
+    (dq, dk, dv, dk_o, dv_o), ((r_enc_up, r_enc_down),) = attention_backward(
         e_proj, 0, e_proj, D // PAIR, e_other, enc_mask, False, e_att, grad_e_att, e_lse,
-        [collect_job(low(grad_dec)), scatter_job(low(g_enc_up, g_enc_down))], 6,
-    )
-    e_slope = jnp.concatenate([dq, with_sibling(dk, dv, dk_o, dv_o)], axis=1)
-    grad_enc = grad_enc + matmul_right(e_slope, w_enc_qkv)
-    g_enc_qkv, e_slope_sum = matmul_left(enc_t, e_slope), sums(e_slope)
+        [scatter_job(low(g_enc_up, g_enc_down))], 6,
+    )
+    e_pull = jnp.concatenate([dq, with_sibling(dk, dv, dk_o, dv_o)], axis=1)
+    grad_enc = grad_enc + matmul_right(e_pull, w_enc_qkv)
+    g_enc_qkv, e_slope_sum = matmul_left(enc_t, e_pull), sums(e_pull)
 
     g_small = small_grads(
         [e_slope_sum[:, :D], e_slope_sum[:, 2 * D :], g_eb2, g_eb3, g_eb4, g_eb5]
@@ -1330,8 +1486,8 @@
         + [g_eg0, g_eg1, g_dg0, g_dg1, g_dg2],
         g_enc_ub, g_dec_ub, shards,
     )
-    _, ((enc_home,), (r_dec_qkv, r_enc_out, r_enc_qkv, r_small)) = carry(
-        [collect_job(low(grad_enc)), scatter_job(low(g_dec_qkv, g_enc_out, g_enc_qkv, g_small))], 7, "end"
+    _, ((enc_home,), (r_enc_out, r_enc_qkv, r_small)) = carry(
+        [collect_job(low(grad_enc)), scatter_job(low(g_enc_out, g_enc_qkv, g_small))], 7, "end"
     )
     r_eb, r_db, r_eg, r_dg, r_enc_ub, r_dec_ub = unpack_small(r_small, enc_up_bias.shape[0])
     return (

time: 717 us -> 663 us (0.925)
  matrix products: 138 us -> 55.4 us
  Pallas kernels: 495 us -> 525 us
    dot_general x11 -> x7, matrix products: 60.6 us -> 20.5 us  [matmul(): return jnp.dot(left_side, right_side, preferred_element_type=FLOAT)]
    pallas_call x8 -> x11, Pallas kernels: 495 us -> 525 us  [carry(): pl.pallas_call(body, grid=(grid,), out_shape=list(out_shape) + flat(2), i...]
    dot_general x11 -> x7, matrix products: 41.1 us -> 16.9 us  [matmul_right(): lax.dot_general(left_side, right_side, (((1,), (1,)), ((), ())), preferre...]
    dot_general x11 -> x7, matrix products: 36.7 us -> 18.1 us  [matmul_left(): lax.dot_general(left_side, right_side, (((0,), (0,)), ((), ())), preferre...]
    unnamed x201 -> x158, local copies, waits for them, and re-layouts: 30.8 us -> 30.3 us
  transfers between devices with their start and end apart: 6 -> 6, of which waited for: 0 -> 1; matrix products, arithmetic and copies ran while one was open for 10% -> 6% of each run, Pallas kernels for 8% -> 6%
where the time goes in v4:
time: 663 us; the launch traced here: 656 us
  Pallas kernels  525 us (79%)
  matrix products  55.4 us (8%)
  local copies, waits for them, and re-layouts  41.5 us (6%)
  other arithmetic  31.2 us (5%)
    pallas_call x11, Pallas kernels, carry(): pl.pallas_call(body, grid=(grid,), out_shape=list(out_shape) + flat(2), i...  525 us
    unnamed x158, local copies, waits for them, and re-layouts  30.3 us
    dot_general x7, matrix products, matmul(): return jnp.dot(left_side, right_side, preferred_element_type=FLOAT)  20.5 us
    dot_general x7, matrix products, matmul_left(): lax.dot_general(left_side, right_side, (((0,), (0,)), ((), ())), preferre...  18.1 us
    dot_general x7, matrix products, matmul_right(): lax.dot_general(left_side, right_side, (((1,), (1,)), ((), ())), preferre...  16.9 us
  transfers between devices with their start and end apart: 6, of which 1 were waited for; matrix products, arithmetic and copies ran while one was open for 6% of the time, Pallas kernels for 6%

profile of v4, /device:TPU:0, one launch (start us, length us, event | category | flops | bytes accessed | tf_op | source)
XLA Modules:
  0.0 656.4 jit_solution(9117118525175825812)
XLA Ops:
  5.2 165.9 %begin.1 = (bf16[4,128,768]{2,1,0:T(8,128)(2,1)}, s32[2,1024]{1,0:T(2,128)}, s32[2,8,512]{2,1,0:T(8,128)}, bf16[2,2,2,4,24,2304]{5,4,3,2,1,0:T(8,128)(2,1)}, bf1...) custom-call(bf16[2,256,768]{2,1,0:T(8,128)(2,1)} %refs_0_.1, ...), custom_call_target="tpu_custom_call" | custom-call | tf_op jit(solution)/shard_map/begin/pallas_call | solution.py:957
  174.7 4.2 fusion.refs_0_.refs_1_.refs_2_
  192.2 20.9 %attend_fwd.3 = (bf16[512,768]{1,0:T(8,128)(2,1)}, f32[6,8,512]{2,1,0:T(8,128)}, bf16[4,128,768]{2,1,0:T(8,128)(2,1)}) custom-call(bf16[512,2304]{1,0:T(8,128)(2,1)} %copy-done, bf16[512,2304]{1,0:T(8,128)(2,1)} %copy-done, bf16[512,2304]{1,0:T(8,128)(2,1)} %copy-done, bf16[512,1536]{1,0:T(8,128)(2,1)} %collective-permute-done.refs_3_.refs_4_, ...), custom_call_target="tpu_custom_call" | custom-call | flops 3221225472 | bytes 7864320 | tf_op jit(solution)/shard_map/attend_fwd/pallas_call | solution.py:957
  213.1 2.4 fusion.47
  215.7 2.0 fusion.1.refs_0_.refs_1_.refs_2_
  220.9 25.6 %ffn_fwd.1 = (bf16[512,3072]{1,0:T(8,128)(2,1)}, bf16[512,3072]{1,0:T(8,128)(2,1)}, f32[512,768]{1,0:T(8,128)}, bf16[512,768]{1,0:T(8,128)(2,1)}, bf16[4,128,768]{2,1,0:T(8,128)(2,1)}) custom-call(f32[512,768]{1,0:T(8,128)} %multiply_add_fusion.1.refs_0_, bf16[768,3072]{1,0:T(8,128)(2,1)} %bitcast.139, f32[1,3072]{1,0:T(1,128)} %reshape.375.refs_2_, ...), custom_call_target="tpu_custom_call" | custom-call | flops 4831838208 | bytes 15728640 | tf_op jit(solution)/shard_map/ffn_fwd/pallas_call | solution.py:957
  246.6 4.5 fusion.5.refs_1_.refs_2_
  251.1 12.8 %attend_fwd.4 = (bf16[512,768]{1,0:T(8,128)(2,1)}, f32[6,8,512]{2,1,0:T(8,128)}) custom-call(bf16[512,2304]{1,0:T(8,128)(2,1)} %copy-done.1, bf16[512,2304]{1,0:T(8,128)(2,1)} %copy-done.1, bf16[512,2304]{1,0:T(8,128)(2,1)} %copy-done.1, bf16[512,1536]{1,0:T(8,128)(2,1)} %collective-permute-done.1.refs_3_.refs_4_, ...), custom_call_target="tpu_custom_call" | custom-call | flops 3221225472 | bytes 7864320 | tf_op jit(solution)/shard_map/attend_fwd/pallas_call | solution.py:957
  263.9 2.6 fusion.37
  270.2 15.0 %attend_fwd.5 = (bf16[512,768]{1,0:T(8,128)(2,1)}, f32[6,8,512]{2,1,0:T(8,128)}) custom-call(bf16[512,768]{1,0:T(8,128)(2,1)} %add_convert_fusion.2.refs_0_, bf16[512,1536]{1,0:T(8,128)(2,1)} %fusion.5.refs_1_.refs_2_, bf16[512,1536]{1,0:T(8,128)(2,1)} %fusion.5.refs_1_.refs_2_, bf16[512,1536]{1,0:T(8,128)(2,1)} %collective-permute-done.2.refs_3_.refs_4_, ...), custom_call_target="tpu_custom_call" | custom-call | flops 3221225472 | bytes 7864320 | tf_op jit(solution)/shard_map/attend_fwd/pallas_call | solution.py:957
  285.2 2.9 fusion.48
  290.0 37.9 %ffn_both.1 = (bf16[512,768]{1,0:T(8,128)(2,1)}, f32[512,768]{1,0:T(8,128)}, bf16[768,3072]{1,0:T(8,128)(2,1)}, f32[1,3072]{1,0:T(1,128)}, bf16[3072,768]{1,0:T(...) custom-call(f32[512,768]{1,0:T(8,128)} %multiply_add_fusion.refs_0_,, ...), custom_call_target="tpu_custom_call" | custom-call | flops 14495514624 | bytes 15728640 | tf_op jit(solution)/shard_map/ffn_both/pallas_call | solution.py:957
  327.9 2.2 multiply_reduce_fusion
  333.1 1.8 convolution_convert_fusion.6
  335.0 50.0 %attend_bwd.3 = (bf16[512,768]{1,0:T(8,128)(2,1)}, f32[512,768]{1,0:T(8,128)}, f32[512,768]{1,0:T(8,128)}, bf16[512,768]{1,0:T(8,128)(2,1)}, bf16[512,768]{1,0:T...) custom-call(bf16[512,768]{1,0:T(8,128)(2,1)} %add_convert_fusion.2.refs_0_, ...), custom_call_target="tpu_custom_call" | custom-call | flops 8053063680 | bytes 14155776 | tf_op jit(solution)/shard_map/attend_bwd/pallas_call | solution.py:957
  385.0 3.4 multiply_reduce_fusion.1
  388.4 2.1 convolution_convert_fusion.5
  393.4 48.7 %attend_bwd.4 = (bf16[512,768]{1,0:T(8,128)(2,1)}, f32[512,768]{1,0:T(8,128)}, f32[512,768]{1,0:T(8,128)}, bf16[512,768]{1,0:T(8,128)(2,1)}, bf16[512,768]{1,0:T...) custom-call(bf16[512,2304]{1,0:T(8,128)(2,1)} %copy-done.1, bf16[512,2304]{1,0:T(8,128)(2,1)} %copy-done.1, ...), custom_call_target="tpu_custom_call" | custom-call | flops 8053063680 | bytes 14155776 | tf_op jit(solution)/shard_map/attend_bwd/pallas_call | solution.py:957
  448.7 3.9 convolution_convert_fusion.1
  452.6 2.9 add_convert_fusion.1
  456.6 2.8 convolution_convert_fusion.2
  459.5 2.6 convert_add_fusion.refs_4_
  462.0 52.4 %ffn_bwd.1 = (f32[512,768]{1,0:T(8,128)}, bf16[768,3072]{1,0:T(8,128)(2,1)}, f32[1,3072]{1,0:T(1,128)}, bf16[3072,768]{1,0:T(8,128)(2,1)}, f32[1,768]{1,0:T(1,12...) custom-call(f32[512,768]{1,0:T(8,128)} %multiply_add_fusion.1.refs_0, ...), custom_call_target="tpu_custom_call" | custom-call | flops 9663676416 | bytes 15728640 | tf_op jit(solution)/shard_map/ffn_bwd/pallas_call | solution.py:957
  514.5 2.2 multiply_reduce_fusion.2
  519.7 59.2 %attend_bwd.5 = (bf16[512,768]{1,0:T(8,128)(2,1)}, f32[512,768]{1,0:T(8,128)}, f32[512,768]{1,0:T(8,128)}, bf16[512,768]{1,0:T(8,128)(2,1)}, bf16[512,768]{1,0:T...) custom-call(bf16[512,2304]{1,0:T(8,128)(2,1)} %copy-done, bf16[512,2304]{1,0:T(8,128)(2,1)} %copy-done, ...), custom_call_target="tpu_custom_call" | custom-call | flops 8053063680 | bytes 14155776 | tf_op jit(solution)/shard_map/attend_bwd/pallas_call | solution.py:957
  578.9 2.6 pad_maximum_fusion.4
  583.4 1.8 fusion.8
  589.0 1.9 fusion.4
  591.8 2.9 add_convert_fusion
  595.8 3.8 convolution_convert_fusion
  600.8 36.4 %end.1 = (bf16[2,256,768]{2,1,0:T(8,128)(2,1)}, f32[24,768]{1,0:T(8,128)}, f32[24,2304]{1,0:T(8,128)}, f32[24,128]{1,0:T(8,128)}) custom-call(bf16[4,128,768]{2,1,0:T(8,128)(2,1)} %bitcast.126, bf16[2,2,2,96,768]{4,3,2,1,0:T(8,128)(2,1)} %bitcast.113, bf16[2,2,2,96,2304]{4,3,2,1,0:T(8,128)(2,1)} %bitcast.114, ...), custom_call_target="tpu_custom_call" | custom-call | tf_op jit(solution)/shard_map/end/pallas_call | solution.py:957
  644.3 2.5 convert_element_type.226
  (279 shorter events, 71.2 us)
Async XLA Ops:
  180.4 11.8 %collective-permute-start = (bf16[512,1536]{1,0:T(8,128)(2,1)S(1)}, bf16[512,1536]{1,0:T(8,128)(2,1)}, u32[]{:S(2)}, u32[]{:S(2)}) collective-permute-start(bf16[512,1536]{1,0:T(8,128)(2,1)S(1)} %slice.199), channel_id=1, source_target_pairs={{0,4},{4,0},{8,12},{12,8},{16,20},{20,16},{24,28},{28,24},{1,5},{5... | collective-permute-start | bytes 4718600 | tf_op jit(solution)/shard_map/ppermute | solution.py:1127
  192.2 20.9 %copy-start.56 = (bf16[2,2,2,4,24,768]{5,4,3,2,1,0:T(8,128)(2,1)S(1)}, bf16[2,2,2,4,24,768]{5,4,3,2,1,0:T(8,128)(2,1)}, u32[]{:S(2)}) copy-start(bf16[2,2,2,4,24,768]{5,4,3,2,1,0:T(8,128)(2,1)} %get-tuple-element.105) | copy-start | bytes 3538948
  219.2 31.9 %collective-permute-start.1 = (bf16[512,1536]{1,0:T(8,128)(2,1)S(1)}, bf16[512,1536]{1,0:T(8,128)(2,1)}, u32[]{:S(2)}, u32[]{:S(2)}) collective-permute-start(bf16[512,1536]{1,0:T(8,128)(2,1)S(1)} %slice.205), channel_id=1, source_target_pairs={{0,4},{4,0},{8,12},{12,8},{16,20},{20,16},{24,28},{28,24},{1,5},{5... | collective-permute-start | bytes 4718600 | tf_op jit(solution)/shard_map/ppermute | solution.py:1127
  251.0 19.2 %collective-permute-start.2 = (bf16[512,1536]{1,0:T(8,128)(2,1)}, bf16[512,1536]{1,0:T(8,128)(2,1)}, u32[]{:S(2)}, u32[]{:S(2)}) collective-permute-start(bf16[512,1536]{1,0:T(8,128)(2,1)} %fusion.5.refs_1_.refs_2_), channel_id=1, source_target_pairs={{0,4},{4,0},{8,12},{12,8},{16,20},{20,16},{24,28},{28,24},{1,5},{5... | collective-permute-start | bytes 4718600 | tf_op jit(solution)/shard_map/ppermute | solution.py:1127
  266.5 3.7 copy-start.4
  335.0 50.0 %copy-start.3 = (f32[512,768]{1,0:T(8,128)S(1)}, f32[512,768]{1,0:T(8,128)}, u32[]{:S(2)}) copy-start(f32[512,768]{1,0:T(8,128)} %copy-done.2) | copy-start | bytes 4718596
  385.0 3.4 copy-start.5
  385.0 3.4 copy-start.22
  443.7 3.5 collective-permute-start.4
  444.1 3.1 copy-start.15
  444.1 3.1 copy-start.16
  444.1 11.4 %collective-permute-start.3 = (bf16[512,1536]{1,0:T(8,128)(2,1)S(1)}, bf16[512,1536]{1,0:T(8,128)(2,1)S(1)}, u32[]{:S(2)}, u32[]{:S(2)}) collective-permute-start(bf16[512,1536]{1,0:T(8,128)(2,1)S(1)} %pad_maximum_fusion.2), channel_id=1, source_target_pairs={{0,4},{4,0},{8,12},{12,8},{16,20},{20,16},{24,28},{28,24},{1,5},{5... | collective-permute-start | bytes 4718600 | tf_op jit(solution)/shard_map/ppermute | solution.py:1127
  447.6 5.0 copy-start.8
  448.7 3.9 copy-start.54
  452.6 2.9 copy-start.14
  581.6 7.2 %collective-permute-start.5 = (bf16[512,1536]{1,0:T(8,128)(2,1)}, bf16[512,1536]{1,0:T(8,128)(2,1)}, u32[]{:S(2)}, u32[]{:S(2)}) collective-permute-start(bf16[512,1536]{1,0:T(8,128)(2,1)} %pad_maximum_fusion.4), channel_id=1, source_target_pairs={{0,4},{4,0},{8,12},{12,8},{16,20},{20,16},{24,28},{28,24},{1,5},{5... | collective-permute-start | bytes 4718600 | tf_op jit(solution)/shard_map/ppermute | solution.py:1127
  582.0 3.3 copy-start.50
  582.0 3.3 copy-start.49
  582.0 3.3 copy-start.48
  582.0 3.4 copy-start.43
  582.0 3.5 copy-start.25
  637.2 9.5 %copy-start.20 = (bf16[2,256,768]{2,1,0:T(8,128)(2,1)S(1)}, bf16[2,256,768]{2,1,0:T(8,128)(2,1)}, u32[]{:S(2)}) copy-start(bf16[2,256,768]{2,1,0:T(8,128)(2,1)} %get-tuple-element.336) | copy-start | bytes 2359300
  644.3 3.4 copy-start.21
  646.7 3.1 copy-start.32
  647.6 3.0 copy-start.31
  647.6 3.7 copy-start.33
  647.6 4.4 copy-start.39
  647.6 5.0 copy-start.38
  648.5 4.7 copy-start.35
  648.5 5.4 copy-start.37
  648.5 6.0 copy-start.30
  649.2 6.0 copy-start.29
  (40 other events, 80.6 us)

commit v5 on v4

--- a/solution.py
+++ b/solution.py
@@ -600,9 +600,10 @@
 
 
 CHUNK = 24 * 512
-BIG_CHUNK = 24 * 768
+BIG_CHUNK = 24 * 512
 REACH = 1.0
 LAG = 3
+GATHER_LAG = 4
 
 
 def pieces(shapes, chunk=None):
@@ -678,7 +679,7 @@
             for kind in range(3, 6):
                 hop(t, kind).wait_send()
 
-        return staged(count, [(0, begin), (LAG + 1, first), (2 * LAG + 1, second), (3 * LAG + 1, third), (4 * LAG + 1, finish)])
+        return staged(count, [(0, begin), (GATHER_LAG + 1, first), (2 * GATHER_LAG + 1, second), (3 * GATHER_LAG + 1, third), (4 * GATHER_LAG + 1, finish)])
 
     shapes = [jax.ShapeDtypeStruct((everyone // (4 * zs * 2) * 2, 2, 2, zs) + s.shape, s.dtype) for s in shards]
     scratch = [DMA_SEM((count, 6)), DMA_SEM((count, 6)), DMA_SEM((count,))]

time: 663 us -> 658 us (level)
  Pallas kernels: 525 us -> 518 us
where the time goes in v5:
time: 658 us; the launch traced here: 650 us
  Pallas kernels  518 us (79%)
  matrix products  55.4 us (8%)
  local copies, waits for them, and re-layouts  41.5 us (6%)
  other arithmetic  31.2 us (5%)
    pallas_call x11, Pallas kernels, carry(): pl.pallas_call(body, grid=(grid,), out_shape=list(out_shape) + flat(2), i...  518 us
    unnamed x158, local copies, waits for them, and re-layouts  30.3 us
    dot_general x7, matrix products, matmul(): return jnp.dot(left_side, right_side, preferred_element_type=FLOAT)  20.5 us
    dot_general x7, matrix products, matmul_left(): lax.dot_general(left_side, right_side, (((0,), (0,)), ((), ())), preferre...  18.1 us
    dot_general x7, matrix products, matmul_right(): lax.dot_general(left_side, right_side, (((1,), (1,)), ((), ())), preferre...  16.9 us
  transfers between devices with their start and end apart: 6, of which 1 were waited for; matrix products, arithmetic and copies ran while one was open for 6% of the time, Pallas kernels for 6%

profile of v5, /device:TPU:0, one launch (start us, length us, event | category | flops | bytes accessed | tf_op | source)
XLA Modules:
  0.0 649.7 jit_solution(15714412326081191961)
XLA Ops:
  5.2 159.2 %begin.1 = (bf16[4,128,768]{2,1,0:T(8,128)(2,1)}, s32[2,1024]{1,0:T(2,128)}, s32[2,8,512]{2,1,0:T(8,128)}, bf16[2,2,2,4,24,2304]{5,4,3,2,1,0:T(8,128)(2,1)}, bf1...) custom-call(bf16[2,256,768]{2,1,0:T(8,128)(2,1)} %refs_0_.1, ...), custom_call_target="tpu_custom_call" | custom-call | tf_op jit(solution)/shard_map/begin/pallas_call | solution.py:958
  167.9 4.2 fusion.refs_0_.refs_1_.refs_2_
  185.4 21.0 %attend_fwd.3 = (bf16[512,768]{1,0:T(8,128)(2,1)}, f32[6,8,512]{2,1,0:T(8,128)}, bf16[4,128,768]{2,1,0:T(8,128)(2,1)}) custom-call(bf16[512,2304]{1,0:T(8,128)(2,1)} %copy-done, bf16[512,2304]{1,0:T(8,128)(2,1)} %copy-done, bf16[512,2304]{1,0:T(8,128)(2,1)} %copy-done, bf16[512,1536]{1,0:T(8,128)(2,1)} %collective-permute-done.refs_3_.refs_4_, ...), custom_call_target="tpu_custom_call" | custom-call | flops 3221225472 | bytes 7864320 | tf_op jit(solution)/shard_map/attend_fwd/pallas_call | solution.py:958
  206.4 2.4 fusion.47
  209.1 2.0 fusion.1.refs_0_.refs_1_.refs_2_
  214.3 26.0 %ffn_fwd.1 = (bf16[512,3072]{1,0:T(8,128)(2,1)}, bf16[512,3072]{1,0:T(8,128)(2,1)}, f32[512,768]{1,0:T(8,128)}, bf16[512,768]{1,0:T(8,128)(2,1)}, bf16[4,128,768]{2,1,0:T(8,128)(2,1)}) custom-call(f32[512,768]{1,0:T(8,128)} %multiply_add_fusion.1.refs_0_, bf16[768,3072]{1,0:T(8,128)(2,1)} %bitcast.139, f32[1,3072]{1,0:T(1,128)} %reshape.375.refs_2_, ...), custom_call_target="tpu_custom_call" | custom-call | flops 4831838208 | bytes 15728640 | tf_op jit(solution)/shard_map/ffn_fwd/pallas_call | solution.py:958
  240.3 4.5 fusion.5.refs_1_.refs_2_
  244.7 12.8 %attend_fwd.4 = (bf16[512,768]{1,0:T(8,128)(2,1)}, f32[6,8,512]{2,1,0:T(8,128)}) custom-call(bf16[512,2304]{1,0:T(8,128)(2,1)} %copy-done.1, bf16[512,2304]{1,0:T(8,128)(2,1)} %copy-done.1, bf16[512,2304]{1,0:T(8,128)(2,1)} %copy-done.1, bf16[512,1536]{1,0:T(8,128)(2,1)} %collective-permute-done.1.refs_3_.refs_4_, ...), custom_call_target="tpu_custom_call" | custom-call | flops 3221225472 | bytes 7864320 | tf_op jit(solution)/shard_map/attend_fwd/pallas_call | solution.py:958
  257.6 2.6 fusion.37
  263.8 15.0 %attend_fwd.5 = (bf16[512,768]{1,0:T(8,128)(2,1)}, f32[6,8,512]{2,1,0:T(8,128)}) custom-call(bf16[512,768]{1,0:T(8,128)(2,1)} %add_convert_fusion.2.refs_0_, bf16[512,1536]{1,0:T(8,128)(2,1)} %fusion.5.refs_1_.refs_2_, bf16[512,1536]{1,0:T(8,128)(2,1)} %fusion.5.refs_1_.refs_2_, bf16[512,1536]{1,0:T(8,128)(2,1)} %collective-permute-done.2.refs_3_.refs_4_, ...), custom_call_target="tpu_custom_call" | custom-call | flops 3221225472 | bytes 7864320 | tf_op jit(solution)/shard_map/attend_fwd/pallas_call | solution.py:958
  278.8 2.9 fusion.48
  283.6 37.7 %ffn_both.1 = (bf16[512,768]{1,0:T(8,128)(2,1)}, f32[512,768]{1,0:T(8,128)}, bf16[768,3072]{1,0:T(8,128)(2,1)}, f32[1,3072]{1,0:T(1,128)}, bf16[3072,768]{1,0:T(...) custom-call(f32[512,768]{1,0:T(8,128)} %multiply_add_fusion.refs_0_,, ...), custom_call_target="tpu_custom_call" | custom-call | flops 14495514624 | bytes 15728640 | tf_op jit(solution)/shard_map/ffn_both/pallas_call | solution.py:958
  321.4 2.2 multiply_reduce_fusion
  326.6 1.8 convolution_convert_fusion.6
  328.4 49.7 %attend_bwd.3 = (bf16[512,768]{1,0:T(8,128)(2,1)}, f32[512,768]{1,0:T(8,128)}, f32[512,768]{1,0:T(8,128)}, bf16[512,768]{1,0:T(8,128)(2,1)}, bf16[512,768]{1,0:T...) custom-call(bf16[512,768]{1,0:T(8,128)(2,1)} %add_convert_fusion.2.refs_0_, ...), custom_call_target="tpu_custom_call" | custom-call | flops 8053063680 | bytes 14155776 | tf_op jit(solution)/shard_map/attend_bwd/pallas_call | solution.py:958
  378.2 3.4 multiply_reduce_fusion.1
  381.6 2.1 convolution_convert_fusion.5
  386.7 49.3 %attend_bwd.4 = (bf16[512,768]{1,0:T(8,128)(2,1)}, f32[512,768]{1,0:T(8,128)}, f32[512,768]{1,0:T(8,128)}, bf16[512,768]{1,0:T(8,128)(2,1)}, bf16[512,768]{1,0:T...) custom-call(bf16[512,2304]{1,0:T(8,128)(2,1)} %copy-done.1, bf16[512,2304]{1,0:T(8,128)(2,1)} %copy-done.1, ...), custom_call_target="tpu_custom_call" | custom-call | flops 8053063680 | bytes 14155776 | tf_op jit(solution)/shard_map/attend_bwd/pallas_call | solution.py:958
  442.5 3.9 convolution_convert_fusion.1
  446.4 2.9 add_convert_fusion.1
  450.5 2.8 convolution_convert_fusion.2
  453.3 2.6 convert_add_fusion.refs_4_
  455.9 52.6 %ffn_bwd.1 = (f32[512,768]{1,0:T(8,128)}, bf16[768,3072]{1,0:T(8,128)(2,1)}, f32[1,3072]{1,0:T(1,128)}, bf16[3072,768]{1,0:T(8,128)(2,1)}, f32[1,768]{1,0:T(1,12...) custom-call(f32[512,768]{1,0:T(8,128)} %multiply_add_fusion.1.refs_0, ...), custom_call_target="tpu_custom_call" | custom-call | flops 9663676416 | bytes 15728640 | tf_op jit(solution)/shard_map/ffn_bwd/pallas_call | solution.py:958
  508.5 2.2 multiply_reduce_fusion.2
  513.8 58.5 %attend_bwd.5 = (bf16[512,768]{1,0:T(8,128)(2,1)}, f32[512,768]{1,0:T(8,128)}, f32[512,768]{1,0:T(8,128)}, bf16[512,768]{1,0:T(8,128)(2,1)}, bf16[512,768]{1,0:T...) custom-call(bf16[512,2304]{1,0:T(8,128)(2,1)} %copy-done, bf16[512,2304]{1,0:T(8,128)(2,1)} %copy-done, ...), custom_call_target="tpu_custom_call" | custom-call | flops 8053063680 | bytes 14155776 | tf_op jit(solution)/shard_map/attend_bwd/pallas_call | solution.py:958
  572.3 2.6 pad_maximum_fusion.4
  576.8 1.8 fusion.8
  582.5 1.9 fusion.4
  585.2 2.9 add_convert_fusion
  589.2 3.8 convolution_convert_fusion
  594.2 36.3 %end.1 = (bf16[2,256,768]{2,1,0:T(8,128)(2,1)}, f32[24,768]{1,0:T(8,128)}, f32[24,2304]{1,0:T(8,128)}, f32[24,128]{1,0:T(8,128)}) custom-call(bf16[4,128,768]{2,1,0:T(8,128)(2,1)} %bitcast.126, bf16[2,2,2,96,768]{4,3,2,1,0:T(8,128)(2,1)} %bitcast.113, bf16[2,2,2,96,2304]{4,3,2,1,0:T(8,128)(2,1)} %bitcast.114, ...), custom_call_target="tpu_custom_call" | custom-call | tf_op jit(solution)/shard_map/end/pallas_call | solution.py:958
  637.6 2.5 convert_element_type.226
  (279 shorter events, 71.1 us)
Async XLA Ops:
  173.7 11.8 %collective-permute-start = (bf16[512,1536]{1,0:T(8,128)(2,1)S(1)}, bf16[512,1536]{1,0:T(8,128)(2,1)}, u32[]{:S(2)}, u32[]{:S(2)}) collective-permute-start(bf16[512,1536]{1,0:T(8,128)(2,1)S(1)} %slice.199), channel_id=1, source_target_pairs={{0,4},{4,0},{8,12},{12,8},{16,20},{20,16},{24,28},{28,24},{1,5},{5... | collective-permute-start | bytes 4718600 | tf_op jit(solution)/shard_map/ppermute | solution.py:1128
  185.4 21.0 %copy-start.56 = (bf16[2,2,2,4,24,768]{5,4,3,2,1,0:T(8,128)(2,1)S(1)}, bf16[2,2,2,4,24,768]{5,4,3,2,1,0:T(8,128)(2,1)}, u32[]{:S(2)}) copy-start(bf16[2,2,2,4,24,768]{5,4,3,2,1,0:T(8,128)(2,1)} %get-tuple-element.105) | copy-start | bytes 3538948
  212.5 32.2 %collective-permute-start.1 = (bf16[512,1536]{1,0:T(8,128)(2,1)S(1)}, bf16[512,1536]{1,0:T(8,128)(2,1)}, u32[]{:S(2)}, u32[]{:S(2)}) collective-permute-start(bf16[512,1536]{1,0:T(8,128)(2,1)S(1)} %slice.205), channel_id=1, source_target_pairs={{0,4},{4,0},{8,12},{12,8},{16,20},{20,16},{24,28},{28,24},{1,5},{5... | collective-permute-start | bytes 4718600 | tf_op jit(solution)/shard_map/ppermute | solution.py:1128
  244.7 19.1 %collective-permute-start.2 = (bf16[512,1536]{1,0:T(8,128)(2,1)}, bf16[512,1536]{1,0:T(8,128)(2,1)}, u32[]{:S(2)}, u32[]{:S(2)}) collective-permute-start(bf16[512,1536]{1,0:T(8,128)(2,1)} %fusion.5.refs_1_.refs_2_), channel_id=1, source_target_pairs={{0,4},{4,0},{8,12},{12,8},{16,20},{20,16},{24,28},{28,24},{1,5},{5... | collective-permute-start | bytes 4718600 | tf_op jit(solution)/shard_map/ppermute | solution.py:1128
  260.2 3.7 copy-start.4
  328.4 49.7 %copy-start.3 = (f32[512,768]{1,0:T(8,128)S(1)}, f32[512,768]{1,0:T(8,128)}, u32[]{:S(2)}) copy-start(f32[512,768]{1,0:T(8,128)} %copy-done.2) | copy-start | bytes 4718596
  378.2 3.4 copy-start.5
  378.2 3.4 copy-start.22
  437.5 3.5 collective-permute-start.4
  437.9 3.1 copy-start.15
  437.9 3.1 copy-start.16
  437.9 11.4 %collective-permute-start.3 = (bf16[512,1536]{1,0:T(8,128)(2,1)S(1)}, bf16[512,1536]{1,0:T(8,128)(2,1)S(1)}, u32[]{:S(2)}, u32[]{:S(2)}) collective-permute-start(bf16[512,1536]{1,0:T(8,128)(2,1)S(1)} %pad_maximum_fusion.2), channel_id=1, source_target_pairs={{0,4},{4,0},{8,12},{12,8},{16,20},{20,16},{24,28},{28,24},{1,5},{5... | collective-permute-start | bytes 4718600 | tf_op jit(solution)/shard_map/ppermute | solution.py:1128
  441.4 5.0 copy-start.8
  442.5 3.9 copy-start.54
  446.4 2.9 copy-start.14
  575.0 7.2 %collective-permute-start.5 = (bf16[512,1536]{1,0:T(8,128)(2,1)}, bf16[512,1536]{1,0:T(8,128)(2,1)}, u32[]{:S(2)}, u32[]{:S(2)}) collective-permute-start(bf16[512,1536]{1,0:T(8,128)(2,1)} %pad_maximum_fusion.4), channel_id=1, source_target_pairs={{0,4},{4,0},{8,12},{12,8},{16,20},{20,16},{24,28},{28,24},{1,5},{5... | collective-permute-start | bytes 4718600 | tf_op jit(solution)/shard_map/ppermute | solution.py:1128
  575.4 3.3 copy-start.50
  575.4 3.3 copy-start.49
  575.4 3.3 copy-start.48
  575.4 3.4 copy-start.43
  575.4 3.5 copy-start.25
  630.5 9.5 %copy-start.20 = (bf16[2,256,768]{2,1,0:T(8,128)(2,1)S(1)}, bf16[2,256,768]{2,1,0:T(8,128)(2,1)}, u32[]{:S(2)}) copy-start(bf16[2,256,768]{2,1,0:T(8,128)(2,1)} %get-tuple-element.336) | copy-start | bytes 2359300
  637.6 3.4 copy-start.21
  640.0 3.1 copy-start.32
  640.9 3.0 copy-start.31
  640.9 3.7 copy-start.33
  640.9 4.4 copy-start.39
  640.9 5.0 copy-start.38
  641.8 4.7 copy-start.35
  641.8 5.4 copy-start.37
  641.8 6.0 copy-start.30
  642.5 6.0 copy-start.29
  (40 other events, 80.6 us)

commit v6 on v5

--- a/solution.py
+++ b/solution.py
@@ -1388,8 +1388,8 @@
     dp, z, core = place()
     small = pack_small(enc_bias, dec_bias, enc_gain, dec_gain, enc_up_bias, dec_up_bias)
     weights = [enc_qkv, enc_out, small, enc_up, enc_down, dec_qkv, dec_out, cross_kv, cross_q, cross_out, dec_up, dec_down]
-    _, ((enc_t, seg_other, ret_other), near) = carry(
-        [spread_job([enc_in], [segments, retrieved], 0.3), gather_job(weights, BIG_CHUNK)], 0, "begin"
+    _, ((enc_t, dec_t, seg_other, ret_other), near) = carry(
+        [spread_job([enc_in, dec_in], [segments, retrieved], 0.3), gather_job(weights, BIG_CHUNK)], 0, "begin"
     )
     (
         w_enc_qkv, w_enc_out, _, w_enc_up, w_enc_down, w_dec_qkv,
@@ -1397,7 +1397,7 @@
     ) = map(matrix, near)
     zs = enc_t.shape[0]
     rows = zs * BLOCK
-    enc_t = enc_t.reshape(rows, D)
+    enc_t, dec_t = enc_t.reshape(rows, D), dec_t.reshape(rows, D)
     here = z // 2 == core
     seg = lax.dynamic_index_in_dim(jnp.where(here, segments, seg_other), lax.rem(z, 2), 0, keepdims=False)
     ret = lax.dynamic_index_in_dim(jnp.where(here, retrieved, ret_other), lax.rem(z, 2), 0, keepdims=False)
@@ -1419,10 +1419,9 @@
 
     e_proj = (matmul(enc_t, w_enc_qkv) + jnp.concatenate([eb[0], zero_row, eb[1]], axis=1)).astype(BRAIN)
     e_other = to_sibling(e_proj[:, D:])
-    e_att, e_lse, ((dec_t,),) = attention_forward(
-        e_proj, 0, e_proj, D // PAIR, e_other, enc_mask, False, [spread_job([dec_in])], 1
-    )
-    dec_t = dec_t.reshape(rows, D)
+    e_att, e_lse, _ = attention_forward(
+        e_proj, 0, e_proj, D // PAIR, e_other, enc_mask, False
+    )
     d_proj = (matmul(dec_t, w_dec_qkv) + jnp.concatenate([db[0], zero_row, db[1]], axis=1)).astype(BRAIN)
     d_other = to_sibling(d_proj[:, D:])
     d_att, d_lse, _ = attention_forward(

time: 658 us -> 665 us (1.011)
    unnamed x158 -> x156, local copies, waits for them, and re-layouts: 30.3 us -> 29 us
  transfers between devices with their start and end apart: 6 -> 6, of which waited for: 1 -> 1; matrix products, arithmetic and copies ran while one was open for 6% -> 7% of each run, Pallas kernels for 6% -> 7%
where the time goes in v6:
time: 665 us; the launch traced here: 656 us
  Pallas kernels  524 us (79%)
  matrix products  55.8 us (8%)
  local copies, waits for them, and re-layouts  41.4 us (6%)
  other arithmetic  31.2 us (5%)
    pallas_call x11, Pallas kernels, carry(): pl.pallas_call(body, grid=(grid,), out_shape=list(out_shape) + flat(2), i...  524 us
    unnamed x156, local copies, waits for them, and re-layouts  29 us
    dot_general x7, matrix products, matmul(): return jnp.dot(left_side, right_side, preferred_element_type=FLOAT)  20.8 us
    dot_general x7, matrix products, matmul_left(): lax.dot_general(left_side, right_side, (((0,), (0,)), ((), ())), preferre...  18.1 us
    dot_general x7, matrix products, matmul_right(): lax.dot_general(left_side, right_side, (((1,), (1,)), ((), ())), preferre...  16.9 us
  transfers between devices with their start and end apart: 6, of which 1 were waited for; matrix products, arithmetic and copies ran while one was open for 7% of the time, Pallas kernels for 7%

profile of v6, /device:TPU:0, one launch (start us, length us, event | category | flops | bytes accessed | tf_op | source)
XLA Modules:
  0.0 655.6 jit_solution(12867081797750471940)
XLA Ops:
  5.2 175.0 %begin.1 = (bf16[4,128,768]{2,1,0:T(8,128)(2,1)}, bf16[4,128,768]{2,1,0:T(8,128)(2,1)}, s32[2,1024]{1,0:T(2,128)}, s32[2,8,512]{2,1,0:T(8,128)}, bf16[2,2,2,4,24...) custom-call(bf16[2,256,768]{2,1,0:T(8,128)(2,1)} %refs_0_.1, ...), custom_call_target="tpu_custom_call" | custom-call | tf_op jit(solution)/shard_map/begin/pallas_call | solution.py:958
  183.8 4.4 fusion.1.refs_0_.refs_1_.refs_2_
  190.1 2.0 fusion.refs_0_.refs_1_.refs_2_
  205.4 15.0 %attend_fwd.4 = (bf16[512,768]{1,0:T(8,128)(2,1)}, f32[6,8,512]{2,1,0:T(8,128)}) custom-call(bf16[512,2304]{1,0:T(8,128)(2,1)} %copy-done, bf16[512,2304]{1,0:T(8,128)(2,1)} %copy-done, bf16[512,2304]{1,0:T(8,128)(2,1)} %copy-done, bf16[512,1536]{1,0:T(8,128)(2,1)} %collective-permute-done.1.refs_3_.refs_4_, ...), custom_call_target="tpu_custom_call" | custom-call | flops 3221225472 | bytes 7864320 | tf_op jit(solution)/shard_map/attend_fwd/pallas_call | solution.py:958
  220.4 2.6 fusion.47
  224.7 21.4 %ffn_fwd.1 = (bf16[512,3072]{1,0:T(8,128)(2,1)}, bf16[512,3072]{1,0:T(8,128)(2,1)}, f32[512,768]{1,0:T(8,128)}, bf16[512,768]{1,0:T(8,128)(2,1)}, bf16[4,128,768]{2,1,0:T(8,128)(2,1)}) custom-call(f32[512,768]{1,0:T(8,128)} %multiply_add_fusion.1.refs_0_, bf16[768,3072]{1,0:T(8,128)(2,1)} %bitcast.137, f32[1,3072]{1,0:T(1,128)} %reshape.375.refs_2_, ...), custom_call_target="tpu_custom_call" | custom-call | flops 4831838208 | bytes 15728640 | tf_op jit(solution)/shard_map/ffn_fwd/pallas_call | solution.py:958
  246.1 4.5 fusion.5.refs_1_.refs_2_
  250.5 12.7 %attend_fwd.3 = (bf16[512,768]{1,0:T(8,128)(2,1)}, f32[6,8,512]{2,1,0:T(8,128)}) custom-call(bf16[512,2304]{1,0:T(8,128)(2,1)} %copy-done.1, bf16[512,2304]{1,0:T(8,128)(2,1)} %copy-done.1, bf16[512,2304]{1,0:T(8,128)(2,1)} %copy-done.1, bf16[512,1536]{1,0:T(8,128)(2,1)} %collective-permute-done.refs_3_.refs_4_, ...), custom_call_target="tpu_custom_call" | custom-call | flops 3221225472 | bytes 7864320 | tf_op jit(solution)/shard_map/attend_fwd/pallas_call | solution.py:958
  263.2 2.6 fusion.46
  269.5 15.4 %attend_fwd.5 = (bf16[512,768]{1,0:T(8,128)(2,1)}, f32[6,8,512]{2,1,0:T(8,128)}) custom-call(bf16[512,768]{1,0:T(8,128)(2,1)} %add_convert_fusion.2.refs_0_, bf16[512,1536]{1,0:T(8,128)(2,1)} %fusion.5.refs_1_.refs_2_, bf16[512,1536]{1,0:T(8,128)(2,1)} %fusion.5.refs_1_.refs_2_, bf16[512,1536]{1,0:T(8,128)(2,1)} %collective-permute-done.2.refs_3_.refs_4_, ...), custom_call_target="tpu_custom_call" | custom-call | flops 3221225472 | bytes 7864320 | tf_op jit(solution)/shard_map/attend_fwd/pallas_call | solution.py:958
  284.9 2.9 fusion.48
  289.6 37.3 %ffn_both.1 = (bf16[512,768]{1,0:T(8,128)(2,1)}, f32[512,768]{1,0:T(8,128)}, bf16[768,3072]{1,0:T(8,128)(2,1)}, f32[1,3072]{1,0:T(1,128)}, bf16[3072,768]{1,0:T(...) custom-call(f32[512,768]{1,0:T(8,128)} %multiply_add_fusion.refs_0_,, ...), custom_call_target="tpu_custom_call" | custom-call | flops 14495514624 | bytes 15728640 | tf_op jit(solution)/shard_map/ffn_both/pallas_call | solution.py:958
  327.0 2.2 multiply_reduce_fusion
  332.2 1.8 convolution_convert_fusion.6
  334.1 49.9 %attend_bwd.3 = (bf16[512,768]{1,0:T(8,128)(2,1)}, f32[512,768]{1,0:T(8,128)}, f32[512,768]{1,0:T(8,128)}, bf16[512,768]{1,0:T(8,128)(2,1)}, bf16[512,768]{1,0:T...) custom-call(bf16[512,768]{1,0:T(8,128)(2,1)} %add_convert_fusion.2.refs_0_, ...), custom_call_target="tpu_custom_call" | custom-call | flops 8053063680 | bytes 14155776 | tf_op jit(solution)/shard_map/attend_bwd/pallas_call | solution.py:958
  384.0 3.4 multiply_reduce_fusion.1
  387.4 2.1 convolution_convert_fusion.5
  392.4 49.3 %attend_bwd.4 = (bf16[512,768]{1,0:T(8,128)(2,1)}, f32[512,768]{1,0:T(8,128)}, f32[512,768]{1,0:T(8,128)}, bf16[512,768]{1,0:T(8,128)(2,1)}, bf16[512,768]{1,0:T...) custom-call(bf16[512,2304]{1,0:T(8,128)(2,1)} %copy-done.1, bf16[512,2304]{1,0:T(8,128)(2,1)} %copy-done.1, ...), custom_call_target="tpu_custom_call" | custom-call | flops 8053063680 | bytes 14155776 | tf_op jit(solution)/shard_map/attend_bwd/pallas_call | solution.py:958
  448.3 3.9 convolution_convert_fusion.1
  452.2 2.9 add_convert_fusion.1
  456.3 2.8 convolution_convert_fusion.2
  459.1 2.6 convert_add_fusion.refs_4_
  461.6 52.8 %ffn_bwd.1 = (f32[512,768]{1,0:T(8,128)}, bf16[768,3072]{1,0:T(8,128)(2,1)}, f32[1,3072]{1,0:T(1,128)}, bf16[3072,768]{1,0:T(8,128)(2,1)}, f32[1,768]{1,0:T(1,12...) custom-call(f32[512,768]{1,0:T(8,128)} %multiply_add_fusion.1.refs_0, ...), custom_call_target="tpu_custom_call" | custom-call | flops 9663676416 | bytes 15728640 | tf_op jit(solution)/shard_map/ffn_bwd/pallas_call | solution.py:958
  514.5 2.2 multiply_reduce_fusion.2
  519.7 58.5 %attend_bwd.5 = (bf16[512,768]{1,0:T(8,128)(2,1)}, f32[512,768]{1,0:T(8,128)}, f32[512,768]{1,0:T(8,128)}, bf16[512,768]{1,0:T(8,128)(2,1)}, bf16[512,768]{1,0:T...) custom-call(bf16[512,2304]{1,0:T(8,128)(2,1)} %copy-done, bf16[512,2304]{1,0:T(8,128)(2,1)} %copy-done, ...), custom_call_target="tpu_custom_call" | custom-call | flops 8053063680 | bytes 14155776 | tf_op jit(solution)/shard_map/attend_bwd/pallas_call | solution.py:958
  578.3 2.6 pad_maximum_fusion.4
  582.8 1.8 fusion.8
  588.4 1.9 fusion.4
  591.1 2.9 add_convert_fusion
  595.2 3.8 convolution_convert_fusion
  600.1 36.5 %end.1 = (bf16[2,256,768]{2,1,0:T(8,128)(2,1)}, f32[24,768]{1,0:T(8,128)}, f32[24,2304]{1,0:T(8,128)}, f32[24,128]{1,0:T(8,128)}) custom-call(bf16[4,128,768]{2,1,0:T(8,128)(2,1)} %bitcast.124, bf16[2,2,2,96,768]{4,3,2,1,0:T(8,128)(2,1)} %bitcast.111, bf16[2,2,2,96,2304]{4,3,2,1,0:T(8,128)(2,1)} %bitcast.112, ...), custom_call_target="tpu_custom_call" | custom-call | tf_op jit(solution)/shard_map/end/pallas_call | solution.py:958
  643.6 2.5 convert_element_type.226
  (277 shorter events, 71.5 us)
Async XLA Ops:
  183.7 6.4 copy-start.53
  189.4 15.9 %collective-permute-start.1 = (bf16[512,1536]{1,0:T(8,128)(2,1)}, bf16[512,1536]{1,0:T(8,128)(2,1)}, u32[]{:S(2)}, u32[]{:S(2)}) collective-permute-start(bf16[512,1536]{1,0:T(8,128)(2,1)} %slice.210), channel_id=1, source_target_pairs={{0,4},{4,0},{8,12},{12,8},{16,20},{20,16},{24,28},{28,24},{1,5},{5... | collective-permute-start | bytes 4718600 | tf_op jit(solution)/shard_map/ppermute | solution.py:1128
  193.6 57.0 %collective-permute-start = (bf16[512,1536]{1,0:T(8,128)(2,1)S(1)}, bf16[512,1536]{1,0:T(8,128)(2,1)}, u32[]{:S(2)}, u32[]{:S(2)}) collective-permute-start(bf16[512,1536]{1,0:T(8,128)(2,1)S(1)} %slice.199), channel_id=1, source_target_pairs={{0,4},{4,0},{8,12},{12,8},{16,20},{20,16},{24,28},{28,24},{1,5},{5... | collective-permute-start | bytes 4718600 | tf_op jit(solution)/shard_map/ppermute | solution.py:1128
  250.5 18.9 %collective-permute-start.2 = (bf16[512,1536]{1,0:T(8,128)(2,1)}, bf16[512,1536]{1,0:T(8,128)(2,1)}, u32[]{:S(2)}, u32[]{:S(2)}) collective-permute-start(bf16[512,1536]{1,0:T(8,128)(2,1)} %fusion.5.refs_1_.refs_2_), channel_id=1, source_target_pairs={{0,4},{4,0},{8,12},{12,8},{16,20},{20,16},{24,28},{28,24},{1,5},{5... | collective-permute-start | bytes 4718600 | tf_op jit(solution)/shard_map/ppermute | solution.py:1128
  265.8 3.7 copy-start.4
  334.1 49.9 %copy-start.3 = (f32[512,768]{1,0:T(8,128)S(1)}, f32[512,768]{1,0:T(8,128)}, u32[]{:S(2)}) copy-start(f32[512,768]{1,0:T(8,128)} %copy-done.2) | copy-start | bytes 4718596
  384.0 3.4 copy-start.5
  384.0 3.4 copy-start.22
  443.3 3.5 collective-permute-start.4
  443.7 3.1 copy-start.15
  443.7 3.1 copy-start.16
  443.7 11.4 %collective-permute-start.3 = (bf16[512,1536]{1,0:T(8,128)(2,1)S(1)}, bf16[512,1536]{1,0:T(8,128)(2,1)S(1)}, u32[]{:S(2)}, u32[]{:S(2)}) collective-permute-start(bf16[512,1536]{1,0:T(8,128)(2,1)S(1)} %pad_maximum_fusion.2), channel_id=1, source_target_pairs={{0,4},{4,0},{8,12},{12,8},{16,20},{20,16},{24,28},{28,24},{1,5},{5... | collective-permute-start | bytes 4718600 | tf_op jit(solution)/shard_map/ppermute | solution.py:1128
  447.2 5.0 copy-start.8
  448.3 3.9 copy-start.54
  452.2 2.9 copy-start.14
  580.9 7.2 %collective-permute-start.5 = (bf16[512,1536]{1,0:T(8,128)(2,1)}, bf16[512,1536]{1,0:T(8,128)(2,1)}, u32[]{:S(2)}, u32[]{:S(2)}) collective-permute-start(bf16[512,1536]{1,0:T(8,128)(2,1)} %pad_maximum_fusion.4), channel_id=1, source_target_pairs={{0,4},{4,0},{8,12},{12,8},{16,20},{20,16},{24,28},{28,24},{1,5},{5... | collective-permute-start | bytes 4718600 | tf_op jit(solution)/shard_map/ppermute | solution.py:1128
  581.4 3.3 copy-start.50
  581.4 3.3 copy-start.49
  581.4 3.3 copy-start.48
  581.4 3.4 copy-start.43
  581.4 3.5 copy-start.25
  636.6 9.5 %copy-start.20 = (bf16[2,256,768]{2,1,0:T(8,128)(2,1)S(1)}, bf16[2,256,768]{2,1,0:T(8,128)(2,1)}, u32[]{:S(2)}) copy-start(bf16[2,256,768]{2,1,0:T(8,128)(2,1)} %get-tuple-element.336) | copy-start | bytes 2359300
  643.6 3.4 copy-start.21
  646.1 3.1 copy-start.32
  647.0 3.0 copy-start.31
  647.0 3.7 copy-start.33
  647.0 4.4 copy-start.39
  647.0 5.0 copy-start.38
  647.9 4.7 copy-start.35
  647.9 5.4 copy-start.37
  647.9 6.0 copy-start.30
  648.6 6.0 copy-start.29
  (39 other events, 77.8 us)
